TPU v7x, 32 devices: a whole 2x2x4 slice. The times are simulated.
32 devices in a mesh: dp: 16 (over z, y, x), tensor: 2 (over core).
Axes of the slice: x: 2, y: 2, z: 4, core: 2. Of those that a mesh axis runs over, the one named last changes fastest.
Arguments:
- inputs: bfloat16 [16384, 1024], P(('dp', 'tensor')), may hold values from -6 to 6
- cotangent: bfloat16 [16384, 1024], P(('dp', 'tensor')), may hold values from -6 to 6
- slot_flags: int32 [16], P('dp'), may hold values 0 or 1
- early_norm_gain: float32 [1024], replicated, may hold values from 0.1 to 1.9
- early_norm_shift: float32 [1024], replicated, may hold values from -3 to 3
- early_up: bfloat16 [1024, 4096], P(None, 'tensor'), may hold values from -0.1875 to 0.1875
- early_up_bias: float32 [4096], P('tensor'), may hold values from -3 to 3
- early_down: bfloat16 [4096, 1024], P('tensor'), may hold values from -0.1875 to 0.1875
- early_down_bias: float32 [1024], replicated, may hold values from -3 to 3
- attend_norm_gain: float32 [1024], replicated, may hold values from 0.1 to 1.9
- attend_norm_shift: float32 [1024], replicated, may hold values from -3 to 3
- query_weight: bfloat16 [1024, 1024], P(None, 'tensor'), may hold values from -0.1875 to 0.1875
- query_bias: float32 [1024], P('tensor'), may hold values from -3 to 3
- key_weight: bfloat16 [1024, 1024], P(None, 'tensor'), may hold values from -0.1875 to 0.1875
- value_weight: bfloat16 [1024, 1024], P(None, 'tensor'), may hold values from -0.1875 to 0.1875
- value_bias: float32 [1024], P('tensor'), may hold values from -3 to 3
- distance_table: float32 [73, 64], replicated, may hold values from -6 to 6
- attend_weight: bfloat16 [1024, 1024], P('tensor'), may hold values from -1 to 1
- attend_bias: float32 [1024], replicated, may hold values from -3 to 3
- mixer_norm_gain: float32 [1024], replicated, may hold values from 0.1 to 1.9
- mixer_norm_shift: float32 [1024], replicated, may hold values from -3 to 3
- gated_weight: bfloat16 [2, 1024, 1024], P(None, None, 'tensor'), may hold values from -0.1875 to 0.1875
- depth_kernel: float32 [31, 1024], P(None, 'tensor'), may hold values from -1 to 1
- depth_norm_gain: float32 [1024], P('tensor'), may hold values from 0.1 to 1.9
- depth_norm_shift: float32 [1024], P('tensor'), may hold values from -3 to 3
- mixer_out: bfloat16 [1024, 1024], P('tensor'), may hold values from -0.25 to 0.25
- late_norm_gain: float32 [1024], replicated, may hold values from 0.1 to 1.9
- late_norm_shift: float32 [1024], replicated, may hold values from -3 to 3
- late_up: bfloat16 [1024, 4096], P(None, 'tensor'), may hold values from -0.1875 to 0.1875
- late_up_bias: float32 [4096], P('tensor'), may hold values from -3 to 3
- late_down: bfloat16 [4096, 1024], P('tensor'), may hold values from -0.1875 to 0.1875
- late_down_bias: float32 [1024], replicated, may hold values from -3 to 3
- final_gain: float32 [1024], replicated, may hold values from 0.1 to 1.9
- final_shift: float32 [1024], replicated, may hold values from -3 to 3
Outputs:
- output: bfloat16 [16384, 1024], P(('dp', 'tensor'))
- input_gradient: float32 [16384, 1024], P(('dp', 'tensor'))
- early_norm_gain_gradient: float32 [1024], replicated
- early_norm_shift_gradient: float32 [1024], replicated
- early_up_gradient: float32 [1024, 4096], P('dp', 'tensor')
- early_up_bias_gradient: float32 [4096], P('tensor')
- early_down_gradient: float32 [4096, 1024], P('tensor', 'dp')
- early_down_bias_gradient: float32 [1024], replicated
- attend_norm_gain_gradient: float32 [1024], replicated
- attend_norm_shift_gradient: float32 [1024], replicated
- query_weight_gradient: float32 [1024, 1024], P('dp', 'tensor')
- query_bias_gradient: float32 [1024], P('tensor')
- key_weight_gradient: float32 [1024, 1024], P('dp', 'tensor')
- value_weight_gradient: float32 [1024, 1024], P('dp', 'tensor')
- value_bias_gradient: float32 [1024], P('tensor')
- distance_table_gradient: float32 [73, 64], replicated
- attend_weight_gradient: float32 [1024, 1024], P('tensor', 'dp')
- attend_bias_gradient: float32 [1024], replicated
- mixer_norm_gain_gradient: float32 [1024], replicated
- mixer_norm_shift_gradient: float32 [1024], replicated
- gated_weight_gradient: float32 [2, 1024, 1024], P(None, 'dp', 'tensor')
- depth_kernel_gradient: float32 [31, 1024], P(None, 'tensor')
- depth_norm_gain_gradient: float32 [1024], P('tensor')
- depth_norm_shift_gradient: float32 [1024], P('tensor')
- mixer_out_gradient: float32 [1024, 1024], P('tensor', 'dp')
- late_norm_gain_gradient: float32 [1024], replicated
- late_norm_shift_gradient: float32 [1024], replicated
- late_up_gradient: float32 [1024, 4096], P('dp', 'tensor')
- late_up_bias_gradient: float32 [4096], P('tensor')
- late_down_gradient: float32 [4096, 1024], P('tensor', 'dp')
- late_down_bias_gradient: float32 [1024], replicated
- final_gain_gradient: float32 [1024], replicated
- final_shift_gradient: float32 [1024], replicated
Inputs may be any that keep to these rules, and one draw needn't show every extreme that they name: `slot_flags`: 1 where the slot holds a clip, 0 where it is empty.
All inputs are finite; a program needn't handle non-finite values. No bound on the sum of `slot_flags` on one device may be relied on, other than what follows from the above.
Results may differ from a plain program's by a relative error of at most 0.03.
Values may be sent and summed in bfloat16 or wider, within the bound.
No kernel may reach another device: no remote copies, remote signals or barrier semaphores. Data moves between devices by JAX's collectives and lax.ppermute only.
A program may use at most 256 MiB of HBM per device.

v0:
```python
import jax
import jax.numpy as jnp
from jax import lax
from jax.sharding import PartitionSpec as P

HEAD_DIM = 64
LEFT = 64
RIGHT = 8


epsilon = 1e-05


def matmul(left, right):
    return jnp.dot(left, right, preferred_element_type=jnp.float32)


def contract_rows(left, right):
    return lax.dot_general(
        left, right, (((0,), (0,)), ((), ())), preferred_element_type=jnp.float32
    )


def contract_columns(left, right):
    return lax.dot_general(
        left, right, (((1,), (1,)), ((), ())), preferred_element_type=jnp.float32
    )


def column_total(values):
    return jnp.sum(values.astype(jnp.float32), axis=0)


def swish(values):
    return values * jax.nn.sigmoid(values)


def swish_slope(values):
    sigmoid_value = jax.nn.sigmoid(values)
    return sigmoid_value * (1.0 + values * (1.0 - sigmoid_value))


def norm_forward(values, gain, shift):
    center = values - jnp.mean(values, axis=1, keepdims=True)
    inverse = lax.rsqrt(jnp.mean(center * center, axis=1, keepdims=True) + epsilon)
    normed = center * inverse
    return (normed * gain + shift, normed, inverse)


def norm_backward(upstream, normed, inverse, gain):
    hat_gradient = upstream * gain
    first = jnp.mean(hat_gradient, axis=1, keepdims=True)
    second = jnp.mean(hat_gradient * normed, axis=1, keepdims=True)
    return (
        inverse * (hat_gradient - first - normed * second),
        jnp.sum(upstream * normed, axis=0),
        jnp.sum(upstream, axis=0),
    )


def gather_rows(values):
    return lax.all_gather(values, "tensor", axis=0, tiled=True)


def sum_rows(partial_value):
    return lax.psum_scatter(
        partial_value.astype(jnp.bfloat16), "tensor", scatter_dimension=0, tiled=True
    ).astype(jnp.float32)


def gather_cotangent(values):
    return lax.all_gather(values, "tensor", axis=0, tiled=True)


def sum_cotangent(partial_value):
    return lax.psum_scatter(
        partial_value.astype(jnp.bfloat16), "tensor", scatter_dimension=0, tiled=True
    ).astype(jnp.float32)


def channel_total(values):
    return lax.psum(values, "tensor")


def key_offsets(start, count, length):
    rows = start + lax.broadcasted_iota(jnp.int32, (count, length), 0)
    columns = lax.broadcasted_iota(jnp.int32, (count, length), 1)
    return columns - rows


def skew_band(values, start, length):
    heads, count, width = values.shape
    flat = jnp.pad(values, ((0, 0), (0, 0), (0, count))).reshape(heads, count * (width + count))
    band = flat[:, : count * (width + count - 1)].reshape(heads, count, width + count - 1)
    padded = jnp.pad(band, ((0, 0), (0, 0), (length, length)))
    begin = length - start + LEFT
    return lax.dynamic_slice_in_dim(padded, begin, length, 2)


def relative_term(table_rows, start, length):
    width = table_rows.shape[2]
    offsets = key_offsets(start, table_rows.shape[1], length)[None]
    band = skew_band(table_rows, start, length)
    return jnp.where(
        offsets <= -LEFT,
        table_rows[:, :, :1],
        jnp.where(offsets >= RIGHT, table_rows[:, :, width - 1 :], band),
    )


def relative_sums(values, start, length):
    heads, count = (values.shape[0], values.shape[1])
    width = LEFT + RIGHT + 1
    offsets = key_offsets(start, count, length)[None]
    left_total = jnp.sum(jnp.where(offsets <= -LEFT, values, 0.0), axis=2)
    right_total = jnp.sum(jnp.where(offsets >= RIGHT, values, 0.0), axis=2)
    padded = jnp.pad(values, ((0, 0), (0, 0), (length, length)))
    begin = length + start - LEFT
    window = lax.dynamic_slice_in_dim(padded, begin, count + width - 1, 2).reshape(
        heads, count * (count + width - 1)
    )
    picked = jnp.pad(window, ((0, 0), (0, count))).reshape(heads, count, count + width)[
        :, :, 1 : width - 1
    ]
    return jnp.concatenate([left_total[..., None], picked, right_total[..., None]], axis=2)


def block_scores(query_rows, keys_all, table_rows, start, scale):
    scores = jnp.einsum("qhd,khd->hqk", query_rows, keys_all, preferred_element_type=jnp.float32)
    return (scores + relative_term(table_rows, start, keys_all.shape[0])) * scale


def depthwise(signal, kernel):
    taps = kernel.shape[0]
    length = signal.shape[0]
    padded = jnp.pad(signal, ((taps - 1, 0), (0, 0)))

    def add_tap(index, total):
        tap_row = lax.dynamic_index_in_dim(kernel, index, 0, keepdims=False)
        return total + tap_row * lax.dynamic_slice_in_dim(padded, index, length, 0)

    return lax.fori_loop(0, taps, add_tap, jnp.zeros_like(signal))


def depthwise_back(upstream, signal, kernel):
    taps = kernel.shape[0]
    length = signal.shape[0]
    padded_upstream = jnp.pad(upstream, ((0, taps - 1), (0, 0)))
    padded_signal = jnp.pad(signal, ((taps - 1, 0), (0, 0)))

    def add_tap(index, carry):
        signal_gradient, kernel_gradient = carry
        tap_row = lax.dynamic_index_in_dim(kernel, index, 0, keepdims=False)
        shifted = lax.dynamic_slice_in_dim(padded_upstream, taps - 1 - index, length, 0)
        signal_gradient = signal_gradient + tap_row * shifted
        kernel_row = jnp.sum(
            upstream * lax.dynamic_slice_in_dim(padded_signal, index, length, 0), axis=0
        )
        kernel_gradient = lax.dynamic_update_index_in_dim(kernel_gradient, kernel_row, index, 0)
        return (signal_gradient, kernel_gradient)

    initial = (jnp.zeros_like(signal), jnp.zeros(kernel.shape, jnp.float32))
    return lax.fori_loop(0, taps, add_tap, initial)


def feed_forward(residual, gain, shift, up_weight, up_bias, down_weight, down_bias):
    normed_out, normed, inverse = norm_forward(residual, gain, shift)
    gathered = gather_rows(normed_out.astype(jnp.bfloat16))
    hidden = matmul(gathered, up_weight) + up_bias
    active = swish(hidden).astype(jnp.bfloat16)
    branch = sum_rows(matmul(active, down_weight)) + down_bias
    return (residual + 0.5 * branch, (normed, inverse, gathered, hidden, active))


def feed_back(gradient, saved, gain, up_weight, down_weight):
    normed, inverse, gathered, hidden, active = saved
    branch_low = (0.5 * gradient).astype(jnp.bfloat16)
    full_branch = gather_cotangent(branch_low)
    down_gradient = contract_rows(active, full_branch)
    hidden_low = (contract_columns(full_branch, down_weight) * swish_slope(hidden)).astype(
        jnp.bfloat16
    )
    up_gradient = contract_rows(gathered, hidden_low)
    normed_gradient = sum_cotangent(contract_columns(hidden_low, up_weight))
    residual_gradient, gain_gradient, shift_gradient = norm_backward(
        normed_gradient, normed, inverse, gain
    )
    norms = (gain_gradient, shift_gradient, column_total(branch_low))
    return (
        gradient + residual_gradient,
        norms,
        (up_gradient, down_gradient),
        column_total(hidden_low),
    )


def attention(
    residual,
    gain,
    shift,
    query_weight,
    query_bias,
    key_weight,
    value_weight,
    value_bias,
    distance_table,
    out_weight,
    out_bias,
):
    normed_out, normed, inverse = norm_forward(residual, gain, shift)
    gathered = gather_rows(normed_out.astype(jnp.bfloat16))
    length = gathered.shape[0]
    heads = query_weight.shape[1] // HEAD_DIM
    queries = (
        (matmul(gathered, query_weight) + query_bias)
        .astype(jnp.bfloat16)
        .reshape(length, heads, HEAD_DIM)
    )
    keys_all = matmul(gathered, key_weight).astype(jnp.bfloat16).reshape(length, heads, HEAD_DIM)
    values_all = (
        (matmul(gathered, value_weight) + value_bias)
        .astype(jnp.bfloat16)
        .reshape(length, heads, HEAD_DIM)
    )
    table = distance_table.astype(jnp.bfloat16)
    relative = jnp.einsum("qhd,rd->hqr", queries, table, preferred_element_type=jnp.float32)
    scale = HEAD_DIM ** (-0.5)
    block = min(512, length)
    starts = jnp.arange(length // block, dtype=jnp.int32) * block

    def forward_block(start):
        query_rows = lax.dynamic_slice_in_dim(queries, start, block, 0)
        table_rows = lax.dynamic_slice_in_dim(relative, start, block, 1)
        scores = block_scores(query_rows, keys_all, table_rows, start, scale)
        peak = jnp.max(scores, axis=2, keepdims=True)
        exponent = jnp.exp(scores - peak)
        total = jnp.sum(exponent, axis=2, keepdims=True)
        probability = (exponent / total).astype(jnp.bfloat16)
        mixed_block = jnp.einsum(
            "hqk,khd->qhd", probability, values_all, preferred_element_type=jnp.float32
        )
        return (mixed_block, peak + jnp.log(total))

    outputs, totals = lax.map(forward_block, starts)
    mixed = outputs.reshape(length, heads * HEAD_DIM).astype(jnp.bfloat16)
    logsum = jnp.transpose(totals, (1, 0, 2, 3)).reshape(heads, length, 1)
    branch = sum_rows(matmul(mixed, out_weight)) + out_bias
    return (
        residual + branch,
        (normed, inverse, gathered, queries, keys_all, values_all, relative, logsum, mixed),
    )


def attention_back(
    gradient, saved, gain, query_weight, key_weight, value_weight, distance_table, out_weight
):
    normed, inverse, gathered, queries, keys_all, values_all, relative, logsum, mixed = saved
    branch_low = gradient.astype(jnp.bfloat16)
    full_branch = gather_cotangent(branch_low)
    out_gradient = contract_rows(mixed, full_branch)
    length = queries.shape[0]
    heads = queries.shape[1]
    width = LEFT + RIGHT + 1
    mixed_low = (
        contract_columns(full_branch, out_weight)
        .astype(jnp.bfloat16)
        .reshape(length, heads, HEAD_DIM)
    )
    table = distance_table.astype(jnp.bfloat16)
    scale = HEAD_DIM ** (-0.5)
    block = min(512, length)
    starts = jnp.arange(length // block, dtype=jnp.int32) * block

    def backward_block(carry, start):
        key_sum, value_sum = carry
        query_rows = lax.dynamic_slice_in_dim(queries, start, block, 0)
        upstream_rows = lax.dynamic_slice_in_dim(mixed_low, start, block, 0)
        table_rows = lax.dynamic_slice_in_dim(relative, start, block, 1)
        logsum_rows = lax.dynamic_slice_in_dim(logsum, start, block, 1)
        scores = block_scores(query_rows, keys_all, table_rows, start, scale)
        probability = jnp.exp(scores - logsum_rows)
        weight_slope = jnp.einsum(
            "qhd,khd->hqk", upstream_rows, values_all, preferred_element_type=jnp.float32
        )
        delta = jnp.sum(weight_slope * probability, axis=2, keepdims=True)
        score_low = (probability * (weight_slope - delta)).astype(jnp.bfloat16)
        value_sum = value_sum + jnp.einsum(
            "hqk,qhd->khd",
            probability.astype(jnp.bfloat16),
            upstream_rows,
            preferred_element_type=jnp.float32,
        )
        key_sum = key_sum + scale * jnp.einsum(
            "hqk,qhd->khd", score_low, query_rows, preferred_element_type=jnp.float32
        )
        distance_low = (scale * relative_sums(score_low.astype(jnp.float32), start, length)).astype(
            jnp.bfloat16
        )
        query_block = scale * jnp.einsum(
            "hqk,khd->qhd", score_low, keys_all, preferred_element_type=jnp.float32
        )
        query_block = query_block + jnp.einsum(
            "hqr,rd->qhd", distance_low, table, preferred_element_type=jnp.float32
        )
        return ((key_sum, value_sum), (query_block, distance_low))

    initial = (
        jnp.zeros((length, heads, HEAD_DIM), jnp.float32),
        jnp.zeros((length, heads, HEAD_DIM), jnp.float32),
    )
    (key_sum, value_sum), (query_parts, distance_parts) = lax.scan(backward_block, initial, starts)
    distance_all = jnp.transpose(distance_parts, (1, 0, 2, 3)).reshape(heads, length, width)
    table_gradient = jnp.einsum(
        "hqr,qhd->rd", distance_all, queries, preferred_element_type=jnp.float32
    )
    query_low = query_parts.reshape(length, heads * HEAD_DIM).astype(jnp.bfloat16)
    key_low = key_sum.astype(jnp.bfloat16).reshape(length, heads * HEAD_DIM)
    value_low = value_sum.astype(jnp.bfloat16).reshape(length, heads * HEAD_DIM)
    partial_value = (
        contract_columns(query_low, query_weight)
        + contract_columns(key_low, key_weight)
        + contract_columns(value_low, value_weight)
    )
    normed_gradient = sum_cotangent(partial_value)
    residual_gradient, gain_gradient, shift_gradient = norm_backward(
        normed_gradient, normed, inverse, gain
    )
    norms = (gain_gradient, shift_gradient, column_total(branch_low), table_gradient)
    matrices = (
        contract_rows(gathered, query_low),
        contract_rows(gathered, key_low),
        contract_rows(gathered, value_low),
        out_gradient,
    )
    return (
        gradient + residual_gradient,
        norms,
        matrices,
        (column_total(query_low), column_total(value_low)),
    )


def mixer(residual, gain, shift, gated_weight, depth_kernel, depth_gain, depth_shift, out_weight):
    normed_out, normed, inverse = norm_forward(residual, gain, shift)
    gathered = gather_rows(normed_out.astype(jnp.bfloat16))
    linear = matmul(gathered, gated_weight[0])
    gate_sigmoid = jax.nn.sigmoid(matmul(gathered, gated_weight[1]))
    glu = linear * gate_sigmoid
    mixed = depthwise(glu, depth_kernel)
    width = depth_kernel.shape[1] * lax.axis_size("tensor")
    center = mixed - channel_total(jnp.sum(mixed, axis=1, keepdims=True)) / width
    spread = channel_total(jnp.sum(center * center, axis=1, keepdims=True)) / width
    inner_inverse = lax.rsqrt(spread + epsilon)
    hat = center * inner_inverse
    scaled = hat * depth_gain + depth_shift
    active = swish(scaled).astype(jnp.bfloat16)
    branch = sum_rows(matmul(active, out_weight))
    return (
        residual + branch,
        (normed, inverse, gathered, linear, gate_sigmoid, glu, hat, inner_inverse, scaled, active),
    )


def mixer_back(gradient, saved, gain, gated_weight, depth_kernel, depth_gain, out_weight):
    normed, inverse, gathered, linear, gate_sigmoid, glu, hat, inner_inverse, scaled, active = saved
    branch_low = gradient.astype(jnp.bfloat16)
    full_branch = gather_cotangent(branch_low)
    out_gradient = contract_rows(active, full_branch)
    scaled_gradient = contract_columns(full_branch, out_weight) * swish_slope(scaled)
    hat_gradient = scaled_gradient * depth_gain
    width = depth_kernel.shape[1] * lax.axis_size("tensor")
    first, second = lax.psum(
        (
            jnp.sum(hat_gradient, axis=1, keepdims=True),
            jnp.sum(hat_gradient * hat, axis=1, keepdims=True),
        ),
        "tensor",
    )
    mixed_gradient = inner_inverse * (hat_gradient - first / width - hat * (second / width))
    glu_gradient, kernel_gradient = depthwise_back(mixed_gradient, glu, depth_kernel)
    linear_low = (glu_gradient * gate_sigmoid).astype(jnp.bfloat16)
    gate_low = (glu_gradient * linear * gate_sigmoid * (1.0 - gate_sigmoid)).astype(jnp.bfloat16)
    gated_gradient = jnp.stack(
        [contract_rows(gathered, linear_low), contract_rows(gathered, gate_low)]
    )
    normed_gradient = sum_cotangent(
        contract_columns(linear_low, gated_weight[0]) + contract_columns(gate_low, gated_weight[1])
    )
    residual_gradient, gain_gradient, shift_gradient = norm_backward(
        normed_gradient, normed, inverse, gain
    )
    small = (
        kernel_gradient,
        jnp.sum(scaled_gradient * hat, axis=0),
        jnp.sum(scaled_gradient, axis=0),
    )
    return (
        gradient + residual_gradient,
        (gain_gradient, shift_gradient),
        (gated_gradient, out_gradient),
        small,
    )


def shards(
    inputs,
    cotangent,
    slot_flags,
    early_norm_gain,
    early_norm_shift,
    early_up,
    early_up_bias,
    early_down,
    early_down_bias,
    attend_norm_gain,
    attend_norm_shift,
    query_weight,
    query_bias,
    key_weight,
    value_weight,
    value_bias,
    distance_table,
    attend_weight,
    attend_bias,
    mixer_norm_gain,
    mixer_norm_shift,
    gated_weight,
    depth_kernel,
    depth_norm_gain,
    depth_norm_shift,
    mixer_out,
    late_norm_gain,
    late_norm_shift,
    late_up,
    late_up_bias,
    late_down,
    late_down_bias,
    final_gain,
    final_shift,
):
    flag = slot_flags.astype(jnp.float32)[0]
    residual = inputs.astype(jnp.float32)
    residual, early_saved = feed_forward(
        residual,
        early_norm_gain,
        early_norm_shift,
        early_up,
        early_up_bias,
        early_down,
        early_down_bias,
    )
    residual, attend_saved = attention(
        residual,
        attend_norm_gain,
        attend_norm_shift,
        query_weight,
        query_bias,
        key_weight,
        value_weight,
        value_bias,
        distance_table,
        attend_weight,
        attend_bias,
    )
    residual, mixer_saved = mixer(
        residual,
        mixer_norm_gain,
        mixer_norm_shift,
        gated_weight,
        depth_kernel,
        depth_norm_gain,
        depth_norm_shift,
        mixer_out,
    )
    residual, late_saved = feed_forward(
        residual, late_norm_gain, late_norm_shift, late_up, late_up_bias, late_down, late_down_bias
    )
    final_out, final_hat, final_inverse = norm_forward(residual, final_gain, final_shift)
    output = (flag * final_out).astype(jnp.bfloat16)
    gradient, final_gain_part, final_shift_part = norm_backward(
        flag * cotangent.astype(jnp.float32), final_hat, final_inverse, final_gain
    )
    gradient, late_norms, late_matrices, late_bias_part = feed_back(
        gradient, late_saved, late_norm_gain, late_up, late_down
    )
    gradient, mixer_norms, mixer_matrices, mixer_small = mixer_back(
        gradient,
        mixer_saved,
        mixer_norm_gain,
        gated_weight,
        depth_kernel,
        depth_norm_gain,
        mixer_out,
    )
    gradient, attend_norms, attend_matrices, attend_small = attention_back(
        gradient,
        attend_saved,
        attend_norm_gain,
        query_weight,
        key_weight,
        value_weight,
        distance_table,
        attend_weight,
    )
    gradient, early_norms, early_matrices, early_bias_part = feed_back(
        gradient, early_saved, early_norm_gain, early_up, early_down
    )
    matrices = (
        lax.psum_scatter(early_matrices[0], "dp", scatter_dimension=0, tiled=True),
        lax.psum_scatter(early_matrices[1], "dp", scatter_dimension=1, tiled=True),
        lax.psum_scatter(attend_matrices[0], "dp", scatter_dimension=0, tiled=True),
        lax.psum_scatter(attend_matrices[1], "dp", scatter_dimension=0, tiled=True),
        lax.psum_scatter(attend_matrices[2], "dp", scatter_dimension=0, tiled=True),
        lax.psum_scatter(attend_matrices[3], "dp", scatter_dimension=1, tiled=True),
        lax.psum_scatter(mixer_matrices[0], "dp", scatter_dimension=1, tiled=True),
        lax.psum_scatter(mixer_matrices[1], "dp", scatter_dimension=1, tiled=True),
        lax.psum_scatter(late_matrices[0], "dp", scatter_dimension=0, tiled=True),
        lax.psum_scatter(late_matrices[1], "dp", scatter_dimension=1, tiled=True),
    )
    shared = lax.psum(
        (
            early_norms[0],
            early_norms[1],
            early_norms[2],
            attend_norms[0],
            attend_norms[1],
            attend_norms[2],
            attend_norms[3],
            mixer_norms[0],
            mixer_norms[1],
            late_norms[0],
            late_norms[1],
            late_norms[2],
            final_gain_part,
            final_shift_part,
        ),
        ("dp", "tensor"),
    )
    split = lax.psum(
        (
            early_bias_part,
            attend_small[0],
            attend_small[1],
            mixer_small[0],
            mixer_small[1],
            mixer_small[2],
            late_bias_part,
        ),
        "dp",
    )
    return (
        output,
        gradient,
        shared[0],
        shared[1],
        matrices[0],
        split[0],
        matrices[1],
        shared[2],
        shared[3],
        shared[4],
        matrices[2],
        split[1],
        matrices[3],
        matrices[4],
        split[2],
        shared[6],
        matrices[5],
        shared[5],
        shared[7],
        shared[8],
        matrices[6],
        split[3],
        split[4],
        split[5],
        matrices[7],
        shared[9],
        shared[10],
        matrices[8],
        split[6],
        matrices[9],
        shared[11],
        shared[12],
        shared[13],
    )


def solution(mesh):
    placed = (
        P(("dp", "tensor"), None),
        P(("dp", "tensor"), None),
        P("dp"),
        P(),
        P(),
        P(None, "tensor"),
        P("tensor"),
        P("tensor", None),
        P(),
        P(),
        P(),
        P(None, "tensor"),
        P("tensor"),
        P(None, "tensor"),
        P(None, "tensor"),
        P("tensor"),
        P(),
        P("tensor", None),
        P(),
        P(),
        P(),
        P(None, None, "tensor"),
        P(None, "tensor"),
        P("tensor"),
        P("tensor"),
        P("tensor", None),
        P(),
        P(),
        P(None, "tensor"),
        P("tensor"),
        P("tensor", None),
        P(),
        P(),
        P(),
    )
    return jax.shard_map(
        shards,
        mesh=mesh,
        in_specs=placed,
        out_specs=(
            P(("dp", "tensor"), None),
            P(("dp", "tensor"), None),
            P(),
            P(),
            P("dp", "tensor"),
            P("tensor"),
            P("tensor", "dp"),
            P(),
            P(),
            P(),
            P("dp", "tensor"),
            P("tensor"),
            P("dp", "tensor"),
            P("dp", "tensor"),
            P("tensor"),
            P(),
            P("tensor", "dp"),
            P(),
            P(),
            P(),
            P(None, "dp", "tensor"),
            P(None, "tensor"),
            P("tensor"),
            P("tensor"),
            P("tensor", "dp"),
            P(),
            P(),
            P("dp", "tensor"),
            P("tensor"),
            P("tensor", "dp"),
            P(),
            P(),
            P(),
        ),
        check_vma=False,
    )
```

profile of v0, /device:TPU:0, one launch (start us, length us, event | category | flops | bytes accessed | tf_op | source)
XLA Modules:
  0.0 2906.2 jit_solution(5206496811673814595)
XLA Ops:
  12.6 13.4 all-gather.9.cloned.1.call-done
  26.1 11.3 multiply_convert_fusion.4
  61.2 11.7 all-gather.11.cloned.1.call-done
  85.0 198.8 %while.69 = (s32[]{:T(128)}, bf16[2,512,8,64]{1,3,2,0:T(8,128)(2,1)}, f32[2,8,512,1]{2,1,3,0:T(8,128)}, s32[2]{0:T(128)S(1)}, bf16[1024,8,64]{0,2,1:T(8,128)(2,1...) while((s32[]{:T(128)}, ...), condition=%wide.region_8.9_spmd, body=%wide.region_5.8_spmd.sunk | while | flops 1117254144 | bytes 265294288 | solution.py:244
  101.6 11.5 reshape.465
  140.5 13.3 reshape.468
  153.8 15.1 fusion.215
  200.6 11.5 reshape.465
  239.5 13.3 reshape.468
  252.8 15.1 fusion.215
  290.1 11.0 reduce-scatter.21.cloned.1.call-done
  305.9 11.9 all-gather.13.cloned.1.call-done
  323.9 127.8 %while.70 = (s32[]{:T(128)}, f32[1024,512]{1,0:T(8,128)}, f32[31,512]{1,0:T(8,128)}, f32[1054,512]{1,0:T(8,128)S(1)}, s32[]{:T(128)}, /*index=5*/s32[]{:T(128)}) while((s32[]{:T(128)}, f32[1024,512]{1,0:T(8,128)}, f32[31,512]{1,0:T(8,128)}, f32[1054,512]{1,0:T(8,128)S(1)}, s32[]{:T(128)}, /*index=5*/s32[]{:T(128)}) %tuple.207), condition=%wide.region_13.14_spmd.clone, body=%wide.region_12.13_spmd.clone.sunk | while | flops 1572867 | bytes 6297695 | solution.py:142
  482.8 11.8 all-gather.15.cloned.1.call-done
  494.6 11.3 multiply_convert_fusion.3
  533.2 11.7 all-gather.17.cloned.1.call-done
  563.5 11.0 reduce-scatter.27.cloned.1.call-done
  582.9 11.9 all-gather.19.cloned.1.call-done
  608.6 218.9 %while.71 = (s32[]{:T(128)}, f32[1024,512]{1,0:T(8,128)}, f32[31,512]{1,0:T(8,128)}, f32[31,512]{1,0:T(8,128)}, f32[1054,512]{1,0:T(8,128)}, /*index=5*/f32[1054...) while((s32[]{:T(128)}, f32[1024,512]{1,0:T(8,128)}, ...), condition=%wide.region_35.36_spmd.clone, body=%wide.region_33.35_spmd.clone.sunk | while | flops 2620935 | bytes 10498237 | solution.py:163
  835.5 11.0 reduce-scatter.29.cloned.1.call-done
  852.7 11.9 all-gather.21.cloned.1.call-done
  869.8 437.5 %while.72 = (s32[]{:T(128)}, f32[1024,8,64]{0,2,1:T(8,128)}, f32[1024,8,64]{0,2,1:T(8,128)}, bf16[2,512,8,64]{1,3,2,0:T(8,128)(2,1)}, bf16[2,8,512,73]{2,3,1,0:T...) while((s32[]{:T(128)}, f32[1024,8,64]{0,2,1:T(8,128)}, ...), condition=%wide.region_43.44_spmd.clone, body=%wide.region_39.43_spmd.clone.sunk | while | flops 2801029632 | bytes 574219328 | solution.py:311
  886.7 11.5 reshape.469
  925.6 13.3 reshape.472
  938.9 16.1 fusion.230
  977.0 17.9 fusion.231
  1011.9 13.5 reshape.473
  1051.0 12.8 reshape.476
  1102.3 11.5 reshape.469
  1141.2 13.3 reshape.472
  1154.5 15.9 fusion.230
  1193.0 17.9 fusion.231
  1227.9 13.7 reshape.473
  1267.1 12.8 reshape.476
  1318.1 11.0 reduce-scatter.31.cloned.1.call-done
  1335.6 11.9 all-gather.23.cloned.1.call-done
  1347.6 11.3 convert_reduce_fusion.1
  1463.1 94.6 %reduce-scatter.47.cloned.1.call-done = f32[2,64,512]{2,1,0:T(8,128)} async-done(((f32[2,1024,512]{2,1,0:T(8,128)}), f32[2,64,512]{2,1,0:T(8,128)}) %reduce-scatter.47.cloned.1.call-update) | async-done | bytes 262160 | tf_op jit(solution)/shard_map/reduce_scatter | solution.py:515
  1557.7 83.8 %reduce-scatter.45.cloned.1.call-done = f32[512,64]{0,1:T(8,128)} async-done(((f32[512,1024]{0,1:T(8,128)}), f32[512,64]{0,1:T(8,128)}) %reduce-scatter.45.cloned.1.call-update) | async-done | bytes 131088 | tf_op jit(solution)/shard_map/reduce_scatter | solution.py:514
  1641.6 81.0 %reduce-scatter.43.cloned.1.call-done = f32[64,512]{1,0:T(8,128)} async-done(((f32[1024,512]{1,0:T(8,128)}), f32[64,512]{1,0:T(8,128)}) %reduce-scatter.43.cloned.1.call-update) | async-done | bytes 131088 | tf_op jit(solution)/shard_map/reduce_scatter | solution.py:513
  1722.5 81.2 %reduce-scatter.39.cloned.1.call-done = f32[64,512]{1,0:T(8,128)} async-done(((f32[1024,512]{1,0:T(8,128)}), f32[64,512]{1,0:T(8,128)}) %reduce-scatter.39.cloned.1.call-update) | async-done | bytes 131088 | tf_op jit(solution)/shard_map/reduce_scatter | solution.py:511
  1803.7 80.8 %reduce-scatter.41.cloned.1.call-done = f32[64,512]{1,0:T(8,128)} async-done(((f32[1024,512]{1,0:T(8,128)}), f32[64,512]{1,0:T(8,128)}) %reduce-scatter.41.cloned.1.call-update) | async-done | bytes 131088 | tf_op jit(solution)/shard_map/reduce_scatter | solution.py:512
  1884.5 177.4 %reduce-scatter.51.cloned.1.call-done = f32[64,2048]{1,0:T(8,128)} async-done(((f32[1024,2048]{1,0:T(8,128)}), f32[64,2048]{1,0:T(8,128)}) %reduce-scatter.51.cloned.1.call-update) | async-done | bytes 524304 | tf_op jit(solution)/shard_map/reduce_scatter | solution.py:517
  2061.9 183.0 %reduce-scatter.53.cloned.1.call-done = f32[2048,64]{0,1:T(8,128)} async-done(((f32[2048,1024]{0,1:T(8,128)}), f32[2048,64]{0,1:T(8,128)}) %reduce-scatter.53.cloned.1.call-update) | async-done | bytes 524304 | tf_op jit(solution)/shard_map/reduce_scatter | solution.py:518
  2245.0 118.8 %all-reduce.16.cloned.1.call-done = (f32[2048]{0:T(1024)}, f32[512]{0:T(512)}, f32[512]{0:T(512)}, f32[31,512]{1,0:T(8,128)}, f32[512]{0:T(512)}, /*index=5*/f32[512]{0:T(512)}, f32[2048]{0:T(1024)}) async-done(((f32[2048]{0:T(1024)}, f32[512]{0:T(512)}, f32[512]{0:T(512)}, f32[31,512]{1,0:T(8,128)}, f32[512]{0:T(512)}, /*index=5*/f32[512]{0:T(512)}, f32[2048]{0:T(1024)}), (f32[2048]{0:T(1024)}, ...) | async-done | bytes 88080 | tf_op jit(solution)/shard_map/psum | solution.py:539
  2363.8 143.4 %all-reduce.14.cloned.1.call-done = (f32[1024]{0:T(1024)}, f32[1024]{0:T(1024)}, f32[1024]{0:T(1024)}, f32[1024]{0:T(1024)}, f32[1024]{0:T(1024)}, /*index=5*/f3...) async-done(((f32[1024]{0:T(1024)}, f32[1024]{0:T(1024)}, ...) | async-done | bytes 71952 | tf_op jit(solution)/shard_map/psum | solution.py:520
  2507.1 181.8 %reduce-scatter.35.cloned.1.call-done = f32[64,2048]{1,0:T(8,128)} async-done(((f32[1024,2048]{1,0:T(8,128)}), f32[64,2048]{1,0:T(8,128)}) %reduce-scatter.35.cloned.1.call-update) | async-done | bytes 524304 | tf_op jit(solution)/shard_map/reduce_scatter | solution.py:509
  2688.9 183.2 %reduce-scatter.37.cloned.1.call-done = f32[2048,64]{0,1:T(8,128)} async-done(((f32[2048,1024]{0,1:T(8,128)}), f32[2048,64]{0,1:T(8,128)}) %reduce-scatter.37.cloned.1.call-update) | async-done | bytes 524304 | tf_op jit(solution)/shard_map/reduce_scatter | solution.py:510
  (692 shorter events, 1033.0 us)
Async XLA Ops:
  7.2 456.7 %copy-start = (bf16[512,1024]{1,0:T(8,128)(2,1)S(1)}, bf16[512,1024]{1,0:T(8,128)(2,1)}, u32[]{:S(2)}) copy-start(bf16[512,1024]{1,0:T(8,128)(2,1)} %param.67) | copy-start | bytes 3145732
  7.3 18.8 all-gather.9.cloned.1.call-start
  8.9 17.2 copy-start.104
  12.6 43.6 %reduce-scatter.19.cloned.1.call-start = ((), (), s32[]{:S(2)}) async-start(), calls=%async_computation.19 | async-start | bytes 3145728 | tf_op jit(solution)/shard_map/reduce_scatter | solution.py:66
  45.1 14.1 copy-start.74
  45.1 14.1 copy-start.86
  45.1 27.8 all-gather.11.cloned.1.call-start
  59.2 13.7 copy-start.99
  59.3 13.7 copy-start.106
  60.9 240.2 %reduce-scatter.21.cloned.1.call-start = ((), (), s32[]{:S(2)}) async-start(), calls=%async_computation.21 | async-start | bytes 3145728 | tf_op jit(solution)/shard_map/reduce_scatter | solution.py:66
  61.2 14.7 copy-start.63
  153.8 23.0 copy-start.24
  153.8 23.0 copy-start.40
  252.8 23.0 copy-start.24
  252.8 23.0 copy-start.40
  287.4 13.8 copy-start.66
  287.4 13.8 copy-start.87
  290.1 27.7 all-gather.13.cloned.1.call-start
  305.8 171.8 %reduce-scatter.23.cloned.1.call-start = ((), (), s32[]{:S(2)}) async-start(), calls=%async_computation.23 | async-start | bytes 3145728 | tf_op jit(solution)/shard_map/reduce_scatter | solution.py:66
  466.6 28.0 all-gather.15.cloned.1.call-start
  481.2 13.4 copy-start.103
  482.6 42.1 %reduce-scatter.25.cloned.1.call-start = ((), (), s32[]{:S(2)}) async-start(), calls=%async_computation.25 | async-start | bytes 3145728 | tf_op jit(solution)/shard_map/reduce_scatter | solution.py:66
  513.6 31.4 %all-gather.17.cloned.1.call-start = ((), (), s32[]{:S(2)}) async-start(), calls=%async_computation.26 | async-start | bytes 3145728 | tf_op jit(solution)/shard_map/all_gather | solution.py:72
  532.9 41.7 %reduce-scatter.27.cloned.1.call-start = ((), (), s32[]{:S(2)}) async-start(), calls=%async_computation.27 | async-start | bytes 3145728 | tf_op jit(solution)/shard_map/reduce_scatter | solution.py:76
  563.5 14.7 copy-start.90
  563.5 31.3 %all-gather.19.cloned.1.call-start = ((), (), s32[]{:S(2)}) async-start(), calls=%async_computation.28 | async-start | bytes 3145728 | tf_op jit(solution)/shard_map/all_gather | solution.py:72
  582.8 263.8 %reduce-scatter.29.cloned.1.call-start = ((), (), s32[]{:S(2)}) async-start(), calls=%async_computation.29 | async-start | bytes 3145728 | tf_op jit(solution)/shard_map/reduce_scatter | solution.py:76
  835.5 29.1 %all-gather.21.cloned.1.call-start = ((), (), s32[]{:S(2)}) async-start(), calls=%async_computation.30 | async-start | bytes 3145728 | tf_op jit(solution)/shard_map/all_gather | solution.py:72
  852.6 476.6 %reduce-scatter.31.cloned.1.call-start = ((), (), s32[]{:S(2)}) async-start(), calls=%async_computation.31 | async-start | bytes 3145728 | tf_op jit(solution)/shard_map/reduce_scatter | solution.py:76
  1315.3 13.9 copy-start.67
  1315.3 13.9 copy-start.75
  1315.3 13.8 copy-start.83
  1318.1 29.5 %all-gather.23.cloned.1.call-start = ((), (), s32[]{:S(2)}) async-start(), calls=%async_computation.32 | async-start | bytes 3145728 | tf_op jit(solution)/shard_map/all_gather | solution.py:72
  1332.4 15.1 copy-start.105
  1335.6 95.5 %reduce-scatter.33.cloned.1.call-start = ((), (), s32[]{:S(2)}) async-start(), calls=%async_computation.33 | async-start | bytes 3145728 | tf_op jit(solution)/shard_map/reduce_scatter | solution.py:76
  1366.6 96.5 %reduce-scatter.49.cloned.1.call-start = ((), (), s32[]{:S(2)}) async-start(), calls=%async_computation.41 | async-start | bytes 2228224 | tf_op jit(solution)/shard_map/reduce_scatter | solution.py:516
  1372.0 185.7 %reduce-scatter.47.cloned.1.call-start = ((), (), s32[]{:S(2)}) async-start(), calls=%async_computation.40 | async-start | bytes 4456448 | tf_op jit(solution)/shard_map/reduce_scatter | solution.py:515
  1380.4 261.1 %reduce-scatter.45.cloned.1.call-start = ((), (), s32[]{:S(2)}) async-start(), calls=%async_computation.39 | async-start | bytes 2228224 | tf_op jit(solution)/shard_map/reduce_scatter | solution.py:514
  1385.9 336.6 %reduce-scatter.43.cloned.1.call-start = ((), (), s32[]{:S(2)}) async-start(), calls=%async_computation.38 | async-start | bytes 2228224 | tf_op jit(solution)/shard_map/reduce_scatter | solution.py:513
  1390.2 413.5 %reduce-scatter.39.cloned.1.call-start = ((), (), s32[]{:S(2)}) async-start(), calls=%async_computation.36 | async-start | bytes 2228224 | tf_op jit(solution)/shard_map/reduce_scatter | solution.py:511
  1395.7 488.8 %reduce-scatter.41.cloned.1.call-start = ((), (), s32[]{:S(2)}) async-start(), calls=%async_computation.37 | async-start | bytes 2228224 | tf_op jit(solution)/shard_map/reduce_scatter | solution.py:512
  1401.1 660.8 %reduce-scatter.51.cloned.1.call-start = ((), (), s32[]{:S(2)}) async-start(), calls=%async_computation.42 | async-start | bytes 8912896 | tf_op jit(solution)/shard_map/reduce_scatter | solution.py:517
  1411.8 833.1 %reduce-scatter.53.cloned.1.call-start = ((), (), s32[]{:S(2)}) async-start(), calls=%async_computation.43 | async-start | bytes 8912896 | tf_op jit(solution)/shard_map/reduce_scatter | solution.py:518
  1422.6 941.2 %all-reduce.16.cloned.1.call-start = ((), (), s32[]{:S(2)}) async-start(), calls=%async_computation.45 | async-start | bytes 180224 | tf_op jit(solution)/shard_map/psum | solution.py:539
  1431.0 1076.1 %all-reduce.14.cloned.1.call-start = ((), (), s32[]{:S(2)}) async-start(), calls=%async_computation.44 | async-start | bytes 172032 | tf_op jit(solution)/shard_map/psum | solution.py:520
  1434.0 1254.9 %reduce-scatter.35.cloned.1.call-start = ((), (), s32[]{:S(2)}) async-start(), calls=%async_computation.34 | async-start | bytes 8912896 | tf_op jit(solution)/shard_map/reduce_scatter | solution.py:509
  1444.7 1427.4 %reduce-scatter.37.cloned.1.call-start = ((), (), s32[]{:S(2)}) async-start(), calls=%async_computation.35 | async-start | bytes 8912896 | tf_op jit(solution)/shard_map/reduce_scatter | solution.py:510
  1455.8 1443.3 %copy-start.1 = (bf16[512,1024]{1,0:T(8,128)(2,1)S(1)}, bf16[512,1024]{1,0:T(8,128)(2,1)}, u32[]{:S(2)}) copy-start(bf16[512,1024]{1,0:T(8,128)(2,1)} %param.67) | copy-start | bytes 3145732
  (111 other events, 546.6 us)
Sparse Core Ops, SparseCore 0:
  12.7 13.2 all-gather.8
  45.2 10.9 reduce-scatter.18
  61.1 11.8 all-gather.10
  290.2 10.9 reduce-scatter.20
  305.9 11.8 all-gather.12
  466.7 10.8 reduce-scatter.22
  482.7 11.8 all-gather.14
  513.7 10.8 reduce-scatter.24
  533.0 11.8 all-gather.16
  563.6 10.9 reduce-scatter.26
  582.9 11.8 all-gather.18
  835.6 10.9 reduce-scatter.28
  852.7 11.8 all-gather.20
  1318.2 10.9 reduce-scatter.30
  1335.7 11.8 all-gather.22
  1366.7 10.8 reduce-scatter.32
  1380.4 82.6 reduce-scatter.48
  1465.8 91.8 reduce-scatter.46
  1560.6 80.9 reduce-scatter.44
  1644.3 78.2 reduce-scatter.42
  1725.4 78.2 reduce-scatter.38
  1806.5 77.9 reduce-scatter.40
  1887.4 174.5 reduce-scatter.50
  2064.7 180.2 reduce-scatter.52
  2253.7 110.0 all-reduce.15
  2372.9 134.1 all-reduce.13
  2509.8 179.0 reduce-scatter.34
  2691.8 180.3 reduce-scatter.36
where the time goes:
time: 2930 us; the launch traced here: 2910 us
  waiting for transfers between devices  1580 us (54%)
  local copies, waits for them, and re-layouts  563 us (19%)
  other arithmetic  399 us (14%)
  matrix products  309 us (11%)
    reduce_scatter x1, waiting for transfers between devices, shards(): lax.psum_scatter(early_matrices[1], 'dp', scatter_dimension=1, tiled=True)  183 us
    reduce_scatter x1, waiting for transfers between devices, shards(): lax.psum_scatter(late_matrices[1], 'dp', scatter_dimension=1, tiled=True)  183 us
    reduce_scatter x1, waiting for transfers between devices, shards(): lax.psum_scatter(early_matrices[0], 'dp', scatter_dimension=0, tiled=True)  182 us
    reduce_scatter x1, waiting for transfers between devices, shards(): lax.psum_scatter(late_matrices[0], 'dp', scatter_dimension=0, tiled=True)  177 us
    add x31, other arithmetic, add_tap(): signal_gradient = signal_gradient + tap_row * shifted  155 us
    while x94, local copies, waits for them, and re-layouts  154 us
    psum x1, waiting for transfers between devices, shards(): lax.psum((early_norms[0], early_norms[1], early_norms[2], attend_norms[0]...  143 us
    psum x1, waiting for transfers between devices, shards(): lax.psum((early_bias_part, attend_small[0], attend_small[1], mixer_small[...  119 us
  transfers between devices with their start and end apart: 28, of which 27 were waited for; matrix products, arithmetic and copies ran while one was open for 3% of the time, Pallas kernels for 0%

commit v1 on v0

v1 whole, which is shorter than its diff:
```python
import functools

import jax
import jax.numpy as jnp
from jax import lax
from jax.experimental import pallas as pl
from jax.experimental.pallas import tpu as pltpu
from jax.sharding import PartitionSpec as P

HEAD_DIM = 64
LEFT = 64
RIGHT = 8
REL = LEFT + RIGHT + 1
TILE = 128
HALO = 32
CHUNK = 64
GRANT = 58 << 20
EPS = 1e-05
SHARED = 24
LOW = jnp.bfloat16
F32 = jnp.float32


def dot(left, right, dims=((1,), (0,))):
    return lax.dot_general(left, right, (dims, ((), ())), preferred_element_type=F32)


def dot_t(left, right):
    return dot(left, right, ((1,), (1,)))


def sigmoid(values):
    return 0.5 * jnp.tanh(0.5 * values) + 0.5


def shape(dims, kind):
    return jax.ShapeDtypeStruct(dims, kind)


def whole(dims):
    return pl.BlockSpec(dims, lambda i, *_: (0,) * len(dims))


def first_half(i, count):
    return jnp.minimum(i, count - 1)


def second_half(i, count):
    return jnp.maximum(i - count, 0)


def launch(body, name, grid, operands, specs, outs, out_specs, scratch=(), scalars=(), flops=0):
    moved = sum(item.size * item.dtype.itemsize for item in (*operands, *outs))
    return pl.pallas_call(
        body,
        grid_spec=pltpu.PrefetchScalarGridSpec(
            num_scalar_prefetch=len(scalars),
            grid=grid,
            in_specs=specs,
            out_specs=out_specs,
            scratch_shapes=list(scratch),
        ),
        out_shape=outs,
        compiler_params=pltpu.CompilerParams(
            dimension_semantics=("arbitrary",) * len(grid), vmem_limit_bytes=GRANT
        ),
        cost_estimate=pl.CostEstimate(flops=flops, transcendentals=0, bytes_accessed=moved),
        name=name,
    )(*scalars, *operands)


def normed_rows(values):
    center = values - jnp.mean(values, axis=1, keepdims=True)
    inverse = lax.rsqrt(jnp.mean(center * center, axis=1, keepdims=True) + EPS)
    return center * inverse, inverse


def row_loop(rows, body, initial=0):
    def step(i, carry):
        return body(pl.ds(pl.multiple_of(i * CHUNK, CHUNK), CHUNK), carry)

    return lax.fori_loop(0, rows // CHUNK, step, initial)


def norm_into(source, gain, shift, target):
    def rows(at, carry):
        hat, _ = normed_rows(source[at, :].astype(F32))
        target[at, :] = (hat * gain[...] + shift[...]).astype(LOW)
        return carry

    row_loop(source.shape[0], rows)


def fold(values):
    return jnp.sum(values.reshape(values.shape[0] // 8, 8, values.shape[1]), axis=0)


def norm_back(upstream, values, gain):
    hat, inverse = normed_rows(values)
    scaled = upstream * gain
    first = jnp.mean(scaled, axis=1, keepdims=True)
    second = jnp.mean(scaled * hat, axis=1, keepdims=True)
    return inverse * (scaled - first - hat * second), hat


def feed_kernel(x, gain, shift, up0, up1, bias0, bias1, down0, down1, bias, n, s0, s1, a0, a1, out):
    i = pl.program_id(0)
    count = pl.num_programs(0) // 2

    @pl.when(i == 0)
    def _():
        norm_into(x, gain, shift, n)

    def part(up, up_bias, down, slope, active, start):
        hidden = dot(n[...], up[...]) + up_bias[...]
        gate = sigmoid(hidden)
        swished = hidden * gate
        slope[...] = (gate + swished * (1.0 - gate)).astype(LOW)
        low = swished.astype(LOW)
        active[...] = low
        product = dot(low, down[...])
        if start:
            out[...] = product
        else:
            out[...] += product

    pl.when(i == 0)(lambda: part(up0, bias0, down0, s0, a0, True))
    pl.when((i > 0) & (i < count))(lambda: part(up0, bias0, down0, s0, a0, False))
    pl.when(i >= count)(lambda: part(up1, bias1, down1, s1, a1, False))

    @pl.when(i == 2 * count - 1)
    def _():
        def rows(at, carry):
            out[at, :] = x[at, :].astype(F32) + 0.5 * (out[at, :] + bias[...])
            return carry

        row_loop(x.shape[0], rows)


def feed_forward(x, gain, shift, up, up_bias, down, bias):
    rows, width = x.shape
    hidden = up[0].shape[1]
    tile = min(512, hidden)
    count = hidden // tile
    own = functools.partial(first_half, count=count)
    oth = functools.partial(second_half, count=count)
    column = lambda height, pick: pl.BlockSpec((height, tile), lambda i: (0, pick(i)))
    row = lambda pick: pl.BlockSpec((tile, width), lambda i: (pick(i), 0))
    return launch(
        feed_kernel,
        "feed_forward",
        (2 * count,),
        (x, gain, shift, *up, *up_bias, *down, bias),
        [
            whole((rows, width)),
            whole((1, width)),
            whole((1, width)),
            column(width, own),
            column(width, oth),
            column(1, own),
            column(1, oth),
            row(own),
            row(oth),
            whole((1, width)),
        ],
        [shape((rows, width), LOW)] + [shape((rows, hidden), LOW)] * 4 + [shape((rows, width), F32)],
        [
            whole((rows, width)),
            column(rows, own),
            column(rows, oth),
            column(rows, own),
            column(rows, oth),
            whole((rows, width)),
        ],
        flops=8 * rows * width * hidden,
    )


def feed_half_kernel(first, x, *refs):
    i = pl.program_id(0)
    if first:
        gain, shift, up, up_bias, down, n, slope, active, out = refs
        pl.when(i == 0)(lambda: norm_into(x, gain, shift, n))
    else:
        n, prior, bias, up, up_bias, down, slope, active, out = refs
    hidden = dot(n[...], up[...]) + up_bias[...]
    gate = sigmoid(hidden)
    swished = hidden * gate
    slope[...] = (gate + swished * (1.0 - gate)).astype(LOW)
    low = swished.astype(LOW)
    active[...] = low
    product = dot(low, down[...])

    @pl.when(i == 0)
    def _():
        out[...] = product if first else prior[...] + product

    @pl.when(i > 0)
    def _():
        out[...] += product

    if not first:
        @pl.when(i == pl.num_programs(0) - 1)
        def _():
            def rows(at, carry):
                out[at, :] = x[at, :].astype(F32) + 0.5 * (out[at, :] + bias[...])
                return carry

            row_loop(x.shape[0], rows)


def feed_half(first, x, extra, up, up_bias, down):
    rows, width = x.shape
    hidden = up.shape[1]
    tile = min(512, hidden)
    column = lambda height: pl.BlockSpec((height, tile), lambda i: (0, i))
    outs = [shape((rows, width), LOW)] * first
    outs += [shape((rows, hidden), LOW)] * 2 + [shape((rows, width), F32)]
    return launch(
        functools.partial(feed_half_kernel, first),
        "feed_half",
        (hidden // tile,),
        (x, *extra, up, up_bias, down),
        [whole(item.shape) for item in (x, *extra)]
        + [column(width), column(1), pl.BlockSpec((tile, width), lambda i: (i, 0))],
        outs,
        [whole((rows, width))] * first + [column(rows), column(rows), whole((rows, width))],
        flops=4 * rows * width * hidden,
    )


def feed_back_kernel(scale, g, d, x, gain, up0, up1, down0, down1, s0, s1, k0, k1, t0, t1, out, *rest):
    i = pl.program_id(0)
    count = pl.num_programs(0) // 2
    low, sums, total = rest if scale else (None, *rest)

    def part(up, down, slope, key, tally, start):
        back = dot_t(d[...], down[...]) * slope[...].astype(F32)
        key_low = back.astype(LOW)
        key[...] = key_low
        tally[...] = dot(jnp.ones((8, key_low.shape[0]), LOW), key_low)
        product = dot_t(key_low, up[...])
        if start:
            total[...] = product
        else:
            total[...] += product

    pl.when(i == 0)(lambda: part(up0, down0, s0, k0, t0, True))
    pl.when((i > 0) & (i < count))(lambda: part(up0, down0, s0, k0, t0, False))
    pl.when(i >= count)(lambda: part(up1, down1, s1, k1, t1, False))

    @pl.when(i == 2 * count - 1)
    def _():
        def rows(at, carry):
            upstream = total[at, :]
            change, hat = norm_back(upstream, x[at, :].astype(F32), gain[...])
            gradient = g[at, :] + change
            out[at, :] = gradient
            if scale:
                low[at, :] = (scale * gradient).astype(LOW)
            return (
                carry[0] + fold(upstream * hat),
                carry[1] + fold(upstream),
                carry[2] + fold(d[at, :].astype(F32)),
            )

        zero = jnp.zeros((8, x.shape[1]), F32)
        first, second, third = row_loop(x.shape[0], rows, (zero, zero, zero))
        sums[0:8, :] = first
        sums[8:16, :] = second
        sums[16:24, :] = third


def feed_back(scale, g, d, x, gain, up, down, slope):
    rows, width = x.shape
    hidden = up[0].shape[1]
    tile = min(512, hidden)
    count = hidden // tile
    own = functools.partial(first_half, count=count)
    oth = functools.partial(second_half, count=count)
    column = lambda height, pick: pl.BlockSpec((height, tile), lambda i: (0, pick(i)))
    row = lambda pick: pl.BlockSpec((tile, width), lambda i: (pick(i), 0))
    outs = [shape((rows, hidden), LOW)] * 2 + [shape((8, hidden), F32)] * 2
    outs += [shape((rows, width), F32)] + [shape((rows, width), LOW)] * bool(scale)
    outs += [shape((24, width), F32)]
    return launch(
        functools.partial(feed_back_kernel, scale),
        "feed_back",
        (2 * count,),
        (g, d, x, gain, *up, *down, *slope),
        [
            whole((rows, width)),
            whole((rows, width)),
            whole((rows, width)),
            whole((1, width)),
            column(width, own),
            column(width, oth),
            row(own),
            row(oth),
            column(rows, own),
            column(rows, oth),
        ],
        outs,
        [column(rows, own), column(rows, oth), column(8, own), column(8, oth)]
        + [whole((rows, width))] * (1 + bool(scale))
        + [whole((24, width))],
        scratch=[pltpu.VMEM((rows, width), F32)],
        flops=8 * rows * width * hidden,
    )


def feed_key_kernel(d, down0, down1, s0, s1, k0, k1, t0, t1):
    i = pl.program_id(0)
    count = pl.num_programs(0) // 2

    def part(down, slope, key, tally):
        low = (dot_t(d[...], down[...]) * slope[...].astype(F32)).astype(LOW)
        key[...] = low
        tally[...] = dot(jnp.ones((8, low.shape[0]), LOW), low)

    pl.when(i < count)(lambda: part(down0, s0, k0, t0))
    pl.when(i >= count)(lambda: part(down1, s1, k1, t1))


def feed_key(d, down, slope):
    rows, width = d.shape
    hidden = slope[0].shape[1]
    tile = min(512, hidden)
    count = hidden // tile
    own = functools.partial(first_half, count=count)
    oth = functools.partial(second_half, count=count)
    column = lambda height, pick: pl.BlockSpec((height, tile), lambda i: (0, pick(i)))
    row = lambda pick: pl.BlockSpec((tile, width), lambda i: (pick(i), 0))
    return launch(
        feed_key_kernel,
        "feed_key",
        (2 * count,),
        (d, *down, *slope),
        [whole((rows, width)), row(own), row(oth), column(rows, own), column(rows, oth)],
        [shape((rows, hidden), LOW)] * 2 + [shape((8, hidden), F32)] * 2,
        [column(rows, own), column(rows, oth), column(8, own), column(8, oth)],
        flops=4 * rows * width * hidden,
    )


def feed_end_kernel(g, d, x, gain, up0, up1, k0, k1, out, sums, total):
    i = pl.program_id(0)
    count = pl.num_programs(0) // 2

    def part(up, key, start):
        product = dot_t(key[...], up[...])
        if start:
            total[...] = product
        else:
            total[...] += product

    pl.when(i == 0)(lambda: part(up0, k0, True))
    pl.when((i > 0) & (i < count))(lambda: part(up0, k0, False))
    pl.when(i >= count)(lambda: part(up1, k1, False))

    @pl.when(i == 2 * count - 1)
    def _():
        def rows(at, carry):
            upstream = total[at, :]
            change, hat = norm_back(upstream, x[at, :].astype(F32), gain[...])
            out[at, :] = g[at, :] + change
            return (
                carry[0] + fold(upstream * hat),
                carry[1] + fold(upstream),
                carry[2] + fold(d[at, :].astype(F32)),
            )

        zero = jnp.zeros((8, x.shape[1]), F32)
        first, second, third = row_loop(x.shape[0], rows, (zero, zero, zero))
        sums[0:8, :] = first
        sums[8:16, :] = second
        sums[16:24, :] = third


def feed_end(g, d, x, gain, up, key):
    rows, width = x.shape
    hidden = key[0].shape[1]
    tile = min(512, hidden)
    count = hidden // tile
    own = functools.partial(first_half, count=count)
    oth = functools.partial(second_half, count=count)
    column = lambda height, pick: pl.BlockSpec((height, tile), lambda i: (0, pick(i)))
    wide = whole((rows, width))
    return launch(
        feed_end_kernel,
        "feed_end",
        (2 * count,),
        (g, d, x, gain, *up, *key),
        [wide, wide, wide, whole((1, width))]
        + [column(width, own), column(width, oth), column(rows, own), column(rows, oth)],
        [shape((rows, width), F32), shape((24, width), F32)],
        [wide, whole((24, width))],
        scratch=[pltpu.VMEM((rows, width), F32)],
        flops=4 * rows * width * hidden,
    )


def final_kernel(flag, x, cotangent, gain, shift, out, gradient, low, sums):
    live = flag[0].astype(F32)

    @pl.when(pl.program_id(0) == 0)
    def _():
        sums[...] = jnp.zeros_like(sums)

    hat, inverse = normed_rows(x[...])
    out[...] = (live * (hat * gain[...] + shift[...])).astype(LOW)
    upstream = live * cotangent[...].astype(F32)
    scaled = upstream * gain[...]
    first = jnp.mean(scaled, axis=1, keepdims=True)
    second = jnp.mean(scaled * hat, axis=1, keepdims=True)
    change = inverse * (scaled - first - hat * second)
    gradient[...] = change
    low[...] = (0.5 * change).astype(LOW)
    sums[0:8, :] += fold(upstream * hat)
    sums[8:16, :] += fold(upstream)


def final_norm(flag, x, cotangent, gain, shift):
    rows, width = x.shape
    step = min(128, rows)
    block = pl.BlockSpec((step, width), lambda i, *_: (i, 0))
    return launch(
        final_kernel,
        "final_norm",
        (rows // step,),
        (x, cotangent, gain, shift),
        [block, block, whole((1, width)), whole((1, width))],
        [shape((rows, width), LOW), shape((rows, width), F32), shape((rows, width), LOW), shape((16, width), F32)],
        [block, block, block, whole((16, width))],
        scalars=(flag,),
    )


def project_kernel(x, gain, shift, kw0, kw1, vw0, vw1, vb, n, kv):
    i = pl.program_id(0)
    step = kw0.shape[1]
    width = x.shape[1]
    half = width // 2

    @pl.when(i == 0)
    def _():
        norm_into(x, gain, shift, n)

    for side, (kw, vw) in enumerate(((kw0, vw0), (kw1, vw1))):
        at = pl.ds(pl.multiple_of(side * half + i * step, step), step)
        to = pl.ds(pl.multiple_of(width + side * half + i * step, step), step)
        kv[:, at] = dot(n[...], kw[...]).astype(LOW)
        kv[:, to] = (dot(n[...], vw[...]) + vb[:, at]).astype(LOW)


def project(x, gain, shift, kw, vw, vb):
    rows, width = x.shape
    half = width // 2
    step = 256
    weight = pl.BlockSpec((width, step), lambda i: (0, i))
    thin = whole((1, width))
    return launch(
        project_kernel,
        "project",
        (half // step,),
        (x, gain, shift, *kw, *vw, vb),
        [whole((rows, width)), thin, thin] + [weight] * 4 + [thin],
        [shape((rows, width), LOW), shape((rows, 2 * width), LOW)],
        [whole((rows, width)), whole((rows, 2 * width))],
        flops=4 * rows * width * width,
    )


def query_kernel(n, qw0, qw1, qb, q):
    i = pl.program_id(0)
    step = qw0.shape[1]
    half = q.shape[1] // 2
    for side, qw in enumerate((qw0, qw1)):
        at = pl.ds(pl.multiple_of(side * half + i * step, step), step)
        q[:, at] = ((dot(n[...], qw[...]) + qb[:, at]).astype(LOW).astype(F32) * HEAD_DIM**-0.5).astype(LOW)


def query(n, qw, qb):
    rows, width = n.shape
    half = width // 2
    step = 256
    weight = pl.BlockSpec((width, step), lambda i: (0, i))
    wide = whole((rows, width))
    return launch(
        query_kernel,
        "query",
        (half // step,),
        (n, *qw, qb),
        [wide, weight, weight, whole((1, width))],
        [shape((rows, width), LOW)],
        [wide],
        flops=2 * rows * width * width,
    )[0]


def in_head(head, dims):
    return (lax.broadcasted_iota(jnp.int32, dims, 1) // HEAD_DIM) == head


def band_of(block):
    rows = block.shape[0]
    left = jnp.broadcast_to(block[:, 0:1], (rows, TILE))
    right = jnp.broadcast_to(block[:, TILE - 1 : TILE], (rows, TILE))
    lane = lax.broadcasted_iota(jnp.int32, (rows, TILE), 1)
    mixed = jnp.where(lane < TILE // 2, right, left)
    spread = jnp.concatenate([block, right, mixed, left], axis=1)
    band = pltpu.roll(spread, LEFT, 1, stride=1, stride_axis=0)
    return left, right, [band[:, t * TILE : (t + 1) * TILE] for t in range(3)]


def attend_kernel(core, q, k0, v0, k1, v1, table, o, lse, prob, scores):
    rows = q.shape[0]
    blocks = rows // TILE
    second = core[0] == 1
    mixed = []
    peaks = []
    for head in range(2):
        inside = in_head(head, q.shape)
        query = jnp.where(inside, q[...], jnp.zeros_like(q))
        scores[:, :rows] = dot_t(query, k0[...])
        scores[:, rows:] = dot_t(query, k1[...])
        relative = dot_t(query, table[...])
        totals = []
        for b in range(blocks):
            at = slice(b * TILE, (b + 1) * TILE)
            left, right, band = band_of(relative[at, :])
            far = jnp.where(second, left, right)
            tiles = []
            for t in range(blocks):
                gap = t - b
                term = left if gap <= -2 else right if gap >= 2 else band[gap + 1]
                tiles.append(scores[at, t * TILE : (t + 1) * TILE] + term)
            for t in range(blocks):
                term = far
                if b == blocks - 1 and t == 0:
                    term = jnp.where(second, left, band[2])
                if b == 0 and t == blocks - 1:
                    term = jnp.where(second, band[0], right)
                tiles.append(scores[at, rows + t * TILE : rows + (t + 1) * TILE] + term)
            peak = functools.reduce(jnp.maximum, tiles)
            peak = jnp.max(peak, axis=1, keepdims=True)
            total = jnp.zeros((TILE, TILE), F32)
            for t, tile in enumerate(tiles):
                value = jnp.exp(tile - peak)
                total = total + value
                prob[at, t * TILE : (t + 1) * TILE] = value.astype(LOW)
            total = jnp.sum(total, axis=1, keepdims=True)
            totals.append((peak, total))
        product = dot(prob[:, :rows], v0[...]) + dot(prob[:, rows:], v1[...])
        mixed.append(
            jnp.concatenate(
                [
                    product[b * TILE : (b + 1) * TILE] * (1.0 / totals[b][1])
                    for b in range(blocks)
                ],
                axis=0,
            )
        )
        peaks.append(jnp.concatenate([peak + jnp.log(total) for peak, total in totals], axis=0))
    o[0] = jnp.where(in_head(0, q.shape), mixed[0], mixed[1]).astype(LOW)
    lane = lax.broadcasted_iota(jnp.int32, (rows, TILE), 1)
    columns = jnp.where(lane == 0, peaks[0], jnp.where(lane == 1, peaks[1], 0.0))
    lse[...] = jnp.transpose(columns)[0:8, :]


def pair_specs(rows, pairs, start):
    near = pl.BlockSpec((rows, TILE), lambda i, *_: (0, start + i))
    near_value = pl.BlockSpec((rows, TILE), lambda i, *_: (0, pairs + start + i))
    far = pl.BlockSpec((rows, TILE), lambda i, *_: (0, (start + i + pairs // 2) % pairs))
    far_value = pl.BlockSpec((rows, TILE), lambda i, *_: (0, pairs + (start + i + pairs // 2) % pairs))
    return [near, near_value, far, far_value]


def attend(core, q, kv, kvr, table):
    rows, width = q.shape
    pairs = width // TILE
    specs = pair_specs(rows, pairs, 0)
    count = pairs // 2
    joined = pl.BlockSpec((1, rows, TILE), lambda i, *_: (i // count, 0, i % count))
    return launch(
        attend_kernel,
        "attend",
        (pairs,),
        (q, kv, kv, kvr, kvr, table),
        [specs[0], *specs, whole((TILE, TILE))],
        [shape((2, rows, width // 2), LOW), shape((8 * pairs, rows), F32)],
        [joined, pl.BlockSpec((8, rows), lambda i, *_: (i, 0))],
        scratch=[pltpu.VMEM((rows, 2 * rows), LOW), pltpu.VMEM((rows, 2 * rows), F32)],
        scalars=(core,),
        flops=8 * rows * rows * width,
    )


def attend_back_kernel(
    core, q, do, o, k0, v0, k1, v1, table, lse, kq, dk0, dv0, dkv1, dtable, prob, slope, scores, ds_back, de
):
    rows = q.shape[0]
    blocks = rows // TILE
    second = core[0] == 1

    @pl.when(pl.program_id(0) == 0)
    def _():
        dtable[...] = jnp.zeros_like(dtable)

    lane = lax.broadcasted_iota(jnp.int32, (TILE, TILE), 1)
    sub = lax.broadcasted_iota(jnp.int32, (TILE, TILE), 0)
    flip = jnp.where(lane + sub == TILE - 1, 1.0, 0.0).astype(LOW)
    keys_t = [jnp.transpose(ref[...].astype(F32)).astype(LOW) for ref in (k0, k1)]
    table_t = jnp.transpose(table[...].astype(F32)).astype(LOW)
    product = do[...].astype(F32) * o[0].astype(F32)
    pieces = []
    gq = []
    for head in range(2):
        inside = in_head(head, q.shape)
        zero = jnp.zeros_like(q)
        query = jnp.where(inside, q[...], zero)
        upstream = jnp.where(inside, do[...], zero)
        ones = jnp.where(in_head(head, (8, TILE)), 1.0, 0.0).astype(F32)
        delta = lax.dot_general(
            ones, product, (((1,), (1,)), ((), ())), precision=lax.Precision.HIGHEST, preferred_element_type=F32
        )[0:1, :]
        level = lse[head : head + 1, :]
        relative = dot_t(query, table[...])
        ends = dot_t(jnp.concatenate([table[0:8, :], table[TILE - 8 :, :]], axis=0), query)
        left_end = ends[0:1, :] - level
        right_end = ends[15:16, :] - level
        far_end = jnp.where(second, left_end, right_end)
        scores[:rows, :] = dot_t(k0[...], query)
        scores[rows:, :] = dot_t(k1[...], query)
        ds_back[:rows, :] = dot_t(v0[...], upstream)
        ds_back[rows:, :] = dot_t(v1[...], upstream)
        for b in range(blocks):
            at = slice(b * TILE, (b + 1) * TILE)
            _, _, band = band_of(relative[at, :])
            turned = [jnp.transpose(item) - level[:, at] for item in band]
            kept = {}
            for t in range(2 * blocks):
                down = slice(t * TILE, (t + 1) * TILE)
                gap = t - b
                if t < blocks:
                    if gap <= -2:
                        term = left_end[:, at]
                    elif gap >= 2:
                        term = right_end[:, at]
                    else:
                        term = turned[gap + 1]
                else:
                    term = far_end[:, at]
                    if b == blocks - 1 and t == blocks:
                        term = jnp.where(second, jnp.broadcast_to(left_end[:, at], (TILE, TILE)), turned[2])
                    if b == 0 and t == 2 * blocks - 1:
                        term = jnp.where(second, turned[0], jnp.broadcast_to(right_end[:, at], (TILE, TILE)))
                value = jnp.exp(scores[down, at] + term)
                prob[down, at] = value.astype(LOW)
                change = (value * (ds_back[down, at] - delta[:, at])).astype(LOW)
                slope[down, at] = change
                if t < blocks and abs(gap) <= 1:
                    kept[gap + 1] = change
                if b == blocks - 1 and t == blocks:
                    kept[2] = jnp.where(second, jnp.zeros_like(change), change)
                if b == 0 and t == 2 * blocks - 1:
                    kept[0] = jnp.where(second, change, jnp.zeros_like(change))
            stretched = jnp.concatenate([dot_t(flip, kept[g]) for g in range(3)] + [jnp.zeros((TILE, TILE), F32)], axis=1)
            back = pltpu.roll(stretched, 3 * TILE + 1 - LEFT, 1, stride=1, stride_axis=0)
            tiles = [back[:, t * TILE : (t + 1) * TILE] for t in range(4)]
            right_sum = tiles[1] + jnp.where(lane < TILE // 2, tiles[2], 0.0)
            left_sum = tiles[3] + jnp.where(lane < TILE // 2, 0.0, tiles[2])
            right_sum = jnp.sum(right_sum, axis=1, keepdims=True)
            left_sum = jnp.sum(left_sum, axis=1, keepdims=True)
            full = tiles[0] + jnp.where(lane == 0, left_sum, 0.0) + jnp.where(lane == TILE - 1, right_sum, 0.0)
            de[:, at] = dot(jnp.transpose(full).astype(LOW), flip)
        here = slice(head * HEAD_DIM, (head + 1) * HEAD_DIM)
        sums = [0.0, 0.0]
        gradient = 0.0
        for side in range(2):
            column = lax.broadcasted_iota(jnp.int32, (16, rows), 1) // TILE
            row = lax.broadcasted_iota(jnp.int32, (16, rows), 0)
            marks = jnp.where(column == row, 1.0, 0.0).astype(LOW)
            mixed = dot(
                jnp.concatenate([keys_t[side][here, :], marks], axis=0),
                slope[side * rows : (side + 1) * rows, :],
            )
            gradient = gradient + mixed[:HEAD_DIM]
            sums[side] = mixed[HEAD_DIM : HEAD_DIM + 8]
        position = lax.broadcasted_iota(jnp.int32, (8, rows), 1) // TILE
        tile_row = lax.broadcasted_iota(jnp.int32, (8, rows), 0)
        gap = tile_row - position
        left_add = jnp.where((gap <= -2) & (tile_row < blocks), sums[0], 0.0)
        right_add = jnp.where((gap >= 2) & (tile_row < blocks), sums[0], 0.0)
        others = jnp.where(tile_row < blocks, sums[1], 0.0)
        left_other = jnp.where((position == 0) & (tile_row == blocks - 1), 0.0, others)
        right_other = jnp.where((position == blocks - 1) & (tile_row == 0), 0.0, others)
        left_add = left_add + jnp.where(second, left_other, 0.0)
        right_add = right_add + jnp.where(second, 0.0, right_other)
        left_add = jnp.sum(left_add, axis=0, keepdims=True)
        right_add = jnp.sum(right_add, axis=0, keepdims=True)
        where = lax.broadcasted_iota(jnp.int32, (TILE, rows), 0)
        de_low = (
            de[...] + jnp.where(where == 0, left_add, 0.0) + jnp.where(where == TILE - 1, right_add, 0.0)
        ).astype(LOW)
        gradient = gradient + dot(table_t[here, :], de_low)
        gq.append(gradient)
        pieces.append(
            (
                dot(slope[:rows, :], q[...]),
                dot(prob[:rows, :], do[...]),
                dot(slope[rows:, :], q[...]),
                dot(prob[rows:, :], do[...]),
                dot(de_low, q[...]),
            )
        )
    turned = jnp.transpose(jnp.concatenate(gq, axis=0))
    kq[...] = (turned * HEAD_DIM**-0.5).astype(LOW)
    chosen = in_head(0, q.shape)
    dk0[...] = jnp.where(chosen, pieces[0][0], pieces[1][0])
    dv0[...] = jnp.where(chosen, pieces[0][1], pieces[1][1])
    dkv1[0] = jnp.where(chosen, pieces[0][2], pieces[1][2]).astype(LOW)
    dkv1[1] = jnp.where(chosen, pieces[0][3], pieces[1][3]).astype(LOW)
    dtable[...] += jnp.where(in_head(0, (TILE, TILE)), pieces[0][4], pieces[1][4])


def attend_back(core, start, q, do, o, kv, kvr, table, lse):
    rows, width = q.shape
    pairs = width // TILE
    half = width // 2
    specs = pair_specs(rows, pairs, start)
    near = pl.BlockSpec((rows, TILE), lambda i, *_: (0, i))
    square = whole((TILE, TILE))
    return launch(
        attend_back_kernel,
        "attend_back",
        (pairs // 2,),
        (q, do, o, kv, kv, kvr, kvr, table, lse),
        [
            specs[0],
            near,
            pl.BlockSpec((1, rows, TILE), lambda i, *_: (start // (pairs // 2), 0, i)),
            *specs,
            square,
            pl.BlockSpec((8, rows), lambda i, *_: (start + i, 0)),
        ],
        [
            shape((rows, half), LOW),
            shape((rows, half), F32),
            shape((rows, half), F32),
            shape((2, rows, half), LOW),
            shape((TILE, TILE), F32),
        ],
        [near, near, near, pl.BlockSpec((2, rows, TILE), lambda i, *_: (0, 0, i)), square],
        scratch=[
            pltpu.VMEM((2 * rows, rows), LOW),
            pltpu.VMEM((2 * rows, rows), LOW),
            pltpu.VMEM((2 * rows, rows), F32),
            pltpu.VMEM((2 * rows, rows), F32),
            pltpu.VMEM((TILE, rows), F32),
        ],
        scalars=(core,),
        flops=10 * rows * rows * width,
    )


def mixer_in_kernel(o0, o1, x, out0, out1, bias, gain, shift, lin0, gate0, lin1, gate1, x2, n, u, sig, edge):
    i = pl.program_id(0)
    count = pl.num_programs(0) // 2

    @pl.when(i == 0)
    def _():
        x2[...] = x[...] + (dot(o0[0], out0[...]) + dot(o1[0], out1[...]) + bias[...])
        norm_into(x2, gain, shift, n)

    def part(lin, gate):
        value = sigmoid(dot(n[...], gate[0]))
        sig[...] = value
        product = dot(n[...], lin[0]) * value
        u[...] = product
        edge[...] = product[product.shape[0] - HALO :]

    pl.when(i < count)(lambda: part(lin0, gate0))
    pl.when(i >= count)(lambda: part(lin1, gate1))


def mixer_in(o, x, out, bias, gain, shift, gated):
    rows, width = x.shape
    half = width // 2
    tile = 256
    count = half // tile
    wide, thin = whole((rows, width)), whole((1, width))
    pick = lambda index, side: pl.BlockSpec(
        (1, width, tile), lambda i: (index, 0, side(i, count))
    )
    column = pl.BlockSpec((rows, tile), lambda i: (0, i))
    return launch(
        mixer_in_kernel,
        "mixer_in",
        (2 * count,),
        (o, o, x, *out, bias, gain, shift, gated[0], gated[0], gated[1], gated[1]),
        [
            pl.BlockSpec((1, rows, half), lambda i: (0, 0, 0)),
            pl.BlockSpec((1, rows, half), lambda i: (1, 0, 0)),
            wide,
            whole((half, width)),
            whole((half, width)),
            thin,
            thin,
            thin,
            pick(0, first_half),
            pick(1, first_half),
            pick(0, second_half),
            pick(1, second_half),
        ],
        [
            shape((rows, width), F32),
            shape((rows, width), LOW),
            shape((rows, width), F32),
            shape((rows, width), F32),
            shape((HALO, width), F32),
        ],
        [
            wide,
            wide,
            column,
            column,
            pl.BlockSpec((HALO, tile), lambda i: (0, (i + count) % (2 * count))),
        ],
        flops=6 * rows * width * width,
    )


def mixer_out_kernel(u, edge, kernel, gain, shift, out0, out1, x2, z, w0, w1, x3, held):
    i = pl.program_id(0)
    rows = u.shape[0]
    taps = kernel.shape[0] - 1
    held[:HALO, :] = edge[...]
    held[HALO:, :] = u[...]
    at = pl.ds(pl.multiple_of(i * TILE, TILE), TILE)
    for start in range(0, rows, CHUNK):
        total = jnp.zeros((CHUNK, TILE), F32)
        for k in range(taps):
            begin = start + k + HALO + 1 - taps
            total = total + kernel[k : k + 1, :] * held[begin : begin + CHUNK, :]
        z[start : start + CHUNK, at] = total

    @pl.when(i == pl.num_programs(0) - 1)
    def _():
        half = out0.shape[0]

        def step(rows_at, carry):
            hat, _ = normed_rows(z[rows_at, :])
            y = hat * gain[...] + shift[...]
            w = (y * sigmoid(y)).astype(LOW)
            w0[rows_at, :] = w[:, :half]
            w1[rows_at, :] = w[:, half:]
            return carry

        row_loop(rows, step)
        x3[...] = x2[...] + (dot(w0[...], out0[...]) + dot(w1[...], out1[...]))


def mixer_out(u, edge, kernel, gain, shift, out, x2):
    rows, width = u.shape
    half = width // 2
    wide, thin = whole((rows, width)), whole((1, width))
    column = lambda height: pl.BlockSpec((height, TILE), lambda i: (0, i))
    return launch(
        mixer_out_kernel,
        "mixer_out",
        (width // TILE,),
        (u, edge, kernel, gain, shift, *out, x2),
        [column(rows), column(HALO), column(kernel.shape[0]), thin, thin]
        + [whole((half, width))] * 2
        + [wide],
        [shape((rows, width), F32)] + [shape((rows, half), LOW)] * 2 + [shape((rows, width), F32)],
        [wide] + [whole((rows, half))] * 2 + [wide],
        scratch=[pltpu.VMEM((rows + HALO, TILE), F32)],
        flops=2 * rows * width * width,
    )


def mixer_mid_kernel(d, out0, out1, z, gain, shift, bz, sums, head):
    half = out0.shape[0]
    rows = d.shape[0]
    bz[:, :half] = dot_t(d[...], out0[...])
    bz[:, half:] = dot_t(d[...], out1[...])

    def step(at, carry):
        hat, inverse = normed_rows(z[at, :])
        y = hat * gain[...] + shift[...]
        gate = sigmoid(y)
        upstream = bz[at, :] * (gate + y * gate * (1.0 - gate))
        scaled = upstream * gain[...]
        first = jnp.mean(scaled, axis=1, keepdims=True)
        second = jnp.mean(scaled * hat, axis=1, keepdims=True)
        bz[at, :] = inverse * (scaled - first - hat * second)
        return carry[0] + fold(upstream * hat), carry[1] + fold(upstream)

    zero = jnp.zeros((8, d.shape[1]), F32)
    first, second = row_loop(rows, step, (zero, zero))
    sums[0:8, :] = first
    sums[8:16, :] = second
    head[:, half:] = bz[:HALO, :half]
    head[:, :half] = bz[:HALO, half:]


def mixer_mid(d, out, z, gain, shift):
    rows, width = d.shape
    half = width // 2
    wide, thin = whole((rows, width)), whole((1, width))
    return launch(
        mixer_mid_kernel,
        "mixer_mid",
        (1,),
        (d, *out, z, gain, shift),
        [wide, whole((half, width)), whole((half, width)), wide, thin, thin],
        [shape((rows, width), F32), shape((16, width), F32), shape((HALO, width), F32)],
        [wide, whole((16, width)), whole((HALO, width))],
        flops=2 * rows * width * width,
    )


def mixer_back_kernel(
    bz, tail, u, edge, kernel, sig, lin0, gate0, lin1, gate1, x2, gain, g, out0, out1,
    own, oth, dkernel, gradient, low, do0, do1, sums, held, later, total, taps_sum, keys,
):
    i = pl.program_id(0)
    count = pl.num_programs(0) // 2
    rows = u.shape[0]
    taps = kernel.shape[0] - 1
    held[:HALO, :] = edge[...]
    held[HALO:, :] = u[...]
    later[:rows, :] = bz[...]
    later[rows:, :] = tail[...]
    taps_sum[...] = jnp.zeros_like(taps_sum)
    for start in range(0, rows, CHUNK):
        here = slice(start, start + CHUNK)
        upstream = later[here, :]
        change = jnp.zeros((CHUNK, TILE), F32)
        for k in range(taps):
            ahead = start + taps - 1 - k
            change = change + kernel[k : k + 1, :] * later[ahead : ahead + CHUNK, :]
            begin = start + k + HALO + 1 - taps
            taps_sum[8 * k : 8 * k + 8, :] += fold(upstream * held[begin : begin + CHUNK, :])
        gate = sig[here, :]
        linear = change * gate
        keys[here, :TILE] = linear.astype(LOW)
        keys[here, TILE:] = (change * held[start + HALO : start + HALO + CHUNK, :] * (1.0 - gate)).astype(LOW)
    dkernel[...] = jnp.sum(taps_sum[...].reshape(kernel.shape[0], 8, TILE), axis=1)

    def part(lin, gate, target, start):
        target[0] = keys[:, :TILE]
        target[1] = keys[:, TILE:]
        product = dot_t(keys[...], jnp.concatenate([lin[0], gate[0]], axis=1))
        if start:
            total[...] = product
        else:
            total[...] += product

    pl.when(i == 0)(lambda: part(lin0, gate0, own, True))
    pl.when((i > 0) & (i < count))(lambda: part(lin0, gate0, own, False))
    pl.when(i >= count)(lambda: part(lin1, gate1, oth, False))

    @pl.when(i == pl.num_programs(0) - 1)
    def _():
        def step(at, carry):
            upstream = total[at, :]
            change, hat = norm_back(upstream, x2[at, :], gain[...])
            value = g[at, :] + change
            gradient[at, :] = value
            rounded = value.astype(LOW)
            low[at, :] = rounded
            return (
                carry[0] + fold(upstream * hat),
                carry[1] + fold(upstream),
                carry[2] + fold(rounded.astype(F32)),
            )

        zero = jnp.zeros((8, x2.shape[1]), F32)
        first, second, third = row_loop(rows, step, (zero, zero, zero))
        sums[0:8, :] = first
        sums[8:16, :] = second
        sums[16:24, :] = third
        do0[...] = dot_t(low[...], out0[...]).astype(LOW)
        do1[...] = dot_t(low[...], out1[...]).astype(LOW)


def mixer_back(bz, tail, u, edge, kernel, sig, gated, x2, gain, g, out):
    rows, width = u.shape
    half = width // 2
    count = half // TILE
    wide, thin = whole((rows, width)), whole((1, width))
    column = lambda height: pl.BlockSpec((height, TILE), lambda i: (0, i))
    pick = lambda index, side: pl.BlockSpec(
        (1, width, TILE), lambda i: (index, 0, side(i, count))
    )
    return launch(
        mixer_back_kernel,
        "mixer_back",
        (2 * count,),
        (bz, tail, u, edge, kernel, sig, gated[0], gated[0], gated[1], gated[1], x2, gain, g, *out),
        [
            column(rows),
            column(HALO),
            column(rows),
            column(HALO),
            column(kernel.shape[0]),
            column(rows),
            pick(0, first_half),
            pick(1, first_half),
            pick(0, second_half),
            pick(1, second_half),
            wide,
            thin,
            wide,
            whole((half, width)),
            whole((half, width)),
        ],
        [
            shape((2, rows, half), LOW),
            shape((2, rows, half), LOW),
            shape(kernel.shape, F32),
            shape((rows, width), F32),
            shape((rows, width), LOW),
            shape((rows, half), LOW),
            shape((rows, half), LOW),
            shape((24, width), F32),
        ],
        [
            pl.BlockSpec((2, rows, TILE), lambda i: (0, 0, first_half(i, count))),
            pl.BlockSpec((2, rows, TILE), lambda i: (0, 0, second_half(i, count))),
            column(kernel.shape[0]),
            wide,
            wide,
            whole((rows, half)),
            whole((rows, half)),
            whole((24, width)),
        ],
        scratch=[
            pltpu.VMEM((rows + HALO, TILE), F32),
            pltpu.VMEM((rows + HALO, TILE), F32),
            pltpu.VMEM((rows, width), F32),
            pltpu.VMEM((8 * kernel.shape[0], TILE), F32),
            pltpu.VMEM((rows, 2 * TILE), LOW),
        ],
        flops=6 * rows * width * width,
    )


def project_back_kernel(
    kq0, dk0, dv0, far0, kq1, dk1, dv1, far1, qw0, kw0, vw0, qw1, kw1, vw1, x, gain, g,
    own, oth, gradient, low, sums, total,
):
    i = pl.program_id(0)
    count = pl.num_programs(0) // 2
    rows = x.shape[0]
    step = kq0.shape[1]
    at = pl.ds(pl.multiple_of(i * step, TILE), step)

    def part(kq, dk, dv, far, qw, kw, vw, target, start):
        kk = (dk[...] + far[0].astype(F32)).astype(LOW)
        kv = (dv[...] + far[1].astype(F32)).astype(LOW)
        target[0] = kk
        target[1] = kv
        product = dot_t(kq[...], qw[...]) + dot_t(kk, kw[...]) + dot_t(kv, vw[...])
        if start:
            total[...] = product
        else:
            total[...] += product
        ones = jnp.ones((8, rows), LOW)
        sums[16:24, at] = dot(ones, kq[...]) * 0.125
        sums[24:32, at] = dot(ones, kv) * 0.125

    first = (kq0, dk0, dv0, far0, qw0, kw0, vw0, own)
    pl.when(i == 0)(lambda: part(*first, True))
    pl.when((i > 0) & (i < count))(lambda: part(*first, False))
    pl.when(i >= count)(lambda: part(kq1, dk1, dv1, far1, qw1, kw1, vw1, oth, False))

    @pl.when(i == pl.num_programs(0) - 1)
    def _():
        def step(rows_at, carry):
            upstream = total[rows_at, :]
            change, hat = norm_back(upstream, x[rows_at, :], gain[...])
            value = g[rows_at, :] + change
            gradient[rows_at, :] = value
            low[rows_at, :] = (0.5 * value).astype(LOW)
            return carry[0] + fold(upstream * hat), carry[1] + fold(upstream)

        zero = jnp.zeros((8, x.shape[1]), F32)
        first, second = row_loop(rows, step, (zero, zero))
        sums[0:8, :] = first
        sums[8:16, :] = second


def project_back(own, oth, qw, kw, vw, x, gain, g):
    rows, width = x.shape
    half = width // 2
    tile = 256
    count = half // tile
    wide, thin = whole((rows, width)), whole((1, width))

    def flat(side):
        return pl.BlockSpec((rows, tile), lambda i: (0, side(i, count)))

    def stacked(side):
        return pl.BlockSpec((2, rows, tile), lambda i: (0, 0, side(i, count)))

    weight = lambda side: pl.BlockSpec((width, tile), lambda i: (0, side(i, count)))
    return launch(
        project_back_kernel,
        "project_back",
        (2 * count,),
        (*own, *oth, qw[0], kw[0], vw[0], qw[1], kw[1], vw[1], x, gain, g),
        [flat(first_half)] * 3
        + [stacked(first_half)]
        + [flat(second_half)] * 3
        + [stacked(second_half)]
        + [weight(first_half)] * 3
        + [weight(second_half)] * 3
        + [wide, thin, wide],
        [
            shape((2, rows, half), LOW),
            shape((2, rows, half), LOW),
            shape((rows, width), F32),
            shape((rows, width), LOW),
            shape((32, width), F32),
        ],
        [stacked(first_half), stacked(second_half), wide, wide, whole((32, width))],
        scratch=[pltpu.VMEM((rows, width), F32)],
        flops=6 * rows * width * width,
    )


def bit_order(devices, color):
    first = ((0, 1, 2), (1, 0, 2), (0, 1, 2), (1, 2, 0), (2, 0, 1))[color]
    return [*first, *range(3, devices.bit_length() - 1)]


def weight_kernel(devices, plan, sides, pairs, me, *refs):
    used = sorted({color for _, _, color in plan})
    places = sorted({(side, color) for side, _, color in plan})
    lefts, refs = refs[: 2 * sides], refs[2 * sides :]
    inputs, refs = refs[: 2 * pairs], refs[2 * pairs :]
    outs, turned = refs[: 2 * len(used)], refs[2 * len(used) :]
    rows, width = lefts[0].shape
    block = width // devices
    half = width // 2
    i = pl.program_id(0)

    def arrange(side):
        colors = [color for item, color in places if item == side]
        for part, source in enumerate(lefts[2 * side : 2 * side + 2]):
            for lane in range(0, width, TILE):
                piece = jnp.transpose(source[:, lane : lane + TILE].astype(F32)).astype(LOW)
                for inner in range(0, TILE, block):
                    relative = ((lane + inner) // block) ^ me[0]
                    for color in colors:
                        place = 0
                        for level, bit in enumerate(bit_order(devices, color)):
                            flag = 1 - ((relative >> bit) & 1)
                            place = place + flag * (devices >> (level + 1))
                        start = pl.multiple_of(place * block, block)
                        turned[places.index((side, color))][
                            pl.ds(start, block), part * rows : (part + 1) * rows
                        ] = piece[inner : inner + block, :]

    for step, (side, source, color) in enumerate(plan):
        fresh = side not in [item[0] for item in plan[:step]]

        def work(side=side, source=source, color=color, fresh=fresh):
            if fresh:
                arrange(side)
            q0, q1 = (ref if len(ref.shape) == 2 else ref.at[0] for ref in inputs[2 * source : 2 * source + 2])
            left = turned[places.index((side, color))]
            slot = used.index(color)
            product = dot(left[:, :rows], q0[...]) + dot(left[:, rows:], q1[...])
            outs[2 * slot][...] = product[:half].astype(LOW)
            outs[2 * slot + 1][...] = product[half:].astype(LOW)

        pl.when(i == step)(work)


def weight_gradient(devices, me, lefts, jobs, tile):
    rows, width = lefts[0][0].shape
    specs, operands, plan = [whole((rows, width))] * (2 * len(lefts)), [item for pair in lefts for item in pair], []
    for source, (side, pair, colors) in enumerate(jobs):
        first, last = len(plan), len(colors) - 1
        if pair[0].ndim == 2:
            spec = pl.BlockSpec((rows, tile), lambda i, *_, f=first, t=last: (0, jnp.clip(i - f, 0, t)))
        else:
            per = pair[0].shape[2] // tile

            def pick(i, *_, f=first, t=last, per=per):
                place = jnp.clip(i - f, 0, t)
                return place // per, 0, place % per

            spec = pl.BlockSpec((1, rows, tile), pick)
        specs += [spec, spec]
        operands += list(pair)
        plan += [(side, source, color) for color in colors]
    used = sorted({color for _, _, color in plan})
    outs, out_specs = [], []
    for color in used:
        steps = [step for step, item in enumerate(plan) if item[2] == color]

        def column(i, *_, steps=steps):
            place = 0
            for step in steps[1:]:
                place = place + jnp.where(i >= step, 1, 0)
            return 0, place

        outs += [shape((width // 2, tile * len(steps)), LOW)] * 2
        out_specs += [pl.BlockSpec((width // 2, tile), column)] * 2
    places = {(side, color) for side, _, color in plan}
    return launch(
        functools.partial(weight_kernel, devices, plan, len(lefts), len(jobs)),
        "weight_gradient",
        (len(plan),),
        operands,
        specs,
        outs,
        out_specs,
        scratch=[pltpu.VMEM((width, 2 * rows), LOW)] * len(places),
        scalars=(me,),
        flops=4 * rows * width * tile * len(plan),
    )


def gather_kernel(early, late, query_bias, value_bias, gain, shift, kernel, out):
    width = query_bias.shape[1]
    out[0:1, :] = early[...]
    out[1:2, :] = late[...]
    for slot, item in enumerate((query_bias, value_bias, gain, shift)):
        out[2 + slot : 3 + slot, :width] = item[...]
    out[8 : 8 + kernel.shape[0], :width] = kernel[...]


def gather(early, late, items, kernel):
    operands = (early, late, *items, kernel)
    rows = 8 + (kernel.shape[0] + 7) // 8 * 8
    return launch(
        gather_kernel,
        "gather",
        (1,),
        operands,
        [whole(item.shape) for item in operands],
        [shape((rows, early.shape[1]), F32)],
        [whole((rows, early.shape[1]))],
    )[0]


def swap(values):
    return lax.ppermute(values, "tensor", [(0, 1), (1, 0)])


def cross(values, devices, mask):
    return lax.ppermute(values, "dp", [(i, i ^ mask) for i in range(devices)])


def whole_slice(devices, block):
    return devices & (devices - 1) or devices < 8 or block % 16 or TILE % block


class Reduction:
    def __init__(self, devices, me, lefts, jobs, tile=512):
        self.devices = devices
        self.tile = tile
        self.colors = sorted({color for _, _, colors in jobs for color in colors})
        self.order = {color: [] for color in self.colors}
        for job, (_, pair, colors) in enumerate(jobs):
            for place, color in enumerate(colors):
                self.order[color].append((job, place))
        self.level = 0
        self.rows = lefts[0][0].shape[1]
        self.state = []
        self.result = None
        if whole_slice(devices, lefts[0][0].shape[1] // devices):
            pieces = []
            for side, pair, colors in jobs:
                both = jnp.concatenate([item if item.ndim == 2 else item[: -(-tile * len(colors) // item.shape[2])] for item in pair], axis=-2)
                if both.ndim == 3:
                    both = jnp.concatenate(list(both), axis=1)[:, : tile * len(colors)]
                left = jnp.concatenate(lefts[side], axis=0)
                pieces.append(dot(left, both, ((0,), (0,))).astype(LOW))
            total = lax.psum_scatter(jnp.concatenate(pieces, axis=1), "dp", scatter_dimension=0, tiled=True)
            cuts = [0]
            for piece in pieces:
                cuts.append(cuts[-1] + piece.shape[1])
            self.result = [total[:, a:b].astype(F32) for a, b in zip(cuts, cuts[1:])]
            return
        parts = weight_gradient(devices, me, lefts, jobs, tile)
        self.state = list(parts)

    def send(self):
        if self.result is not None:
            return
        for slot in range(len(self.state) // 2):
            bit = bit_order(self.devices, self.colors[slot])[self.level]
            self.state[2 * slot] = cross(self.state[2 * slot], self.devices, 1 << bit)

    def add(self):
        if self.result is not None:
            return
        self.level += 1
        arrived, kept = self.state[::2], self.state[1::2]
        half = kept[0].shape[0] // 2
        if half * 2 * self.devices == self.rows:
            self.state = [arrived[0].astype(F32) + kept[0].astype(F32)]
            return
        away = [one[:half] + two[:half] for one, two in zip(arrived, kept)]
        stay = [one[half:] + two[half:] for one, two in zip(arrived, kept)]
        bits = {bit_order(self.devices, color)[self.level] for color in self.colors}
        if len(bits) == 1 and len(away) > 1:
            away, stay = [jnp.concatenate(away, axis=1)], [jnp.concatenate(stay, axis=1)]
        self.state = [item for pair in zip(away, stay) for item in pair]

    def parts(self):
        if self.result is not None:
            return self.result
        tile = self.tile
        found = {}
        keys = [key for color in self.colors for key in self.order[color]]
        for column, key in enumerate(keys):
            found[key] = self.state[0][:, column * tile : (column + 1) * tile]
        jobs = sorted({job for job, _ in found})
        return [
            jnp.concatenate([found[key] for key in sorted(found) if key[0] == job], axis=1) for job in jobs
        ]


def hold(main, *reductions):
    flat = list(main)
    for item in reductions:
        flat += item.state
    flat = lax.optimization_barrier(tuple(flat))
    place = len(main)
    for item in reductions:
        count = len(item.state)
        item.state = list(flat[place : place + count])
        place += count
    return flat[: len(main)]


def pack_kernel(late, final, mixer, attended, depth, early, dkernel, dtable0, dtable1, t10, t11, t40, t41, own, oth, table):
    width = late.shape[1]
    half = width // 2
    own[...] = jnp.zeros_like(own)
    oth[...] = jnp.zeros_like(oth)
    rolled = dtable0[...] + dtable1[...]
    table[0:REL, :] = rolled[0:REL]
    table[REL - 1 : REL, :] = jnp.sum(rolled[REL - 1 :], axis=0, keepdims=True)
    table[REL:, :] = jnp.zeros((table.shape[0] - REL, TILE), F32)

    def folded(source, group):
        return jnp.sum(source[8 * group : 8 * group + 8, :], axis=0, keepdims=True)

    shared = [folded(late, g) for g in range(3)] + [folded(final, g) for g in range(2)]
    shared += [folded(mixer, g) for g in range(3)] + [folded(attended, g) for g in range(2)]
    shared += [folded(early, g) for g in range(3)]
    mixed = [folded(attended, g) for g in (2, 3)] + [folded(depth, g) for g in range(2)]
    for target, start, tallies in ((own, 0, (t10, t40)), (oth, half, (t11, t41))):
        for place, item in enumerate(shared):
            target[place : place + 1, :] = item
        for g in range(8):
            target[SHARED - 11 : SHARED - 1, g * TILE : (g + 1) * TILE] = table[10 * g : 10 * g + 10, :]
        for place, item in enumerate(mixed):
            target[SHARED + place : SHARED + place + 1, :half] = item[:, start : start + half]
        target[SHARED + 4 : SHARED + 18, :half] = dkernel[0:14, start : start + half]
        target[SHARED : SHARED + 17, half:] = dkernel[14:31, start : start + half]
        place = SHARED + 18
        for item in tallies:
            for begin in range(0, item.shape[1], width):
                target[place : place + 1, :] = item[0:1, begin : begin + width]
                place += 1


def pack(operands):
    width = operands[0].shape[1]
    rows = SHARED + 24
    return launch(
        pack_kernel,
        "pack",
        (1,),
        operands,
        [whole(item.shape) for item in operands],
        [shape((rows, width), F32)] * 2,
        [whole((rows, width))] * 2,
        scratch=[pltpu.VMEM((80, TILE), F32)],
    )


def shards(
    devices,
    inputs,
    cotangent,
    slot_flags,
    early_norm_gain,
    early_norm_shift,
    early_up,
    early_up_bias,
    early_down,
    early_down_bias,
    attend_norm_gain,
    attend_norm_shift,
    query_weight,
    query_bias,
    key_weight,
    value_weight,
    value_bias,
    distance_table,
    attend_weight,
    attend_bias,
    mixer_norm_gain,
    mixer_norm_shift,
    gated_weight,
    depth_kernel,
    depth_norm_gain,
    depth_norm_shift,
    mixer_weight,
    late_norm_gain,
    late_norm_shift,
    late_up,
    late_up_bias,
    late_down,
    late_down_bias,
    final_gain,
    final_shift,
):
    row = lambda vector: vector[None, :]
    both = lambda weight: (weight, swap(weight))
    side = lax.axis_index("tensor").astype(jnp.int32)
    core = side[None]
    me = lax.axis_index("dp").astype(jnp.int32)[None]
    half = depth_kernel.shape[1]
    hidden = early_up.shape[1]
    taps = depth_kernel.shape[0]

    vectors = (query_bias, value_bias, depth_norm_gain, depth_norm_shift)
    small = gather(row(early_up_bias), row(late_up_bias), [row(item) for item in vectors], depth_kernel)
    other = swap(small)
    early_bias = (row(early_up_bias), other[0:1])
    late_bias = (row(late_up_bias), other[1:2])
    query_bias_all, value_bias_all, depth_gain_all, depth_shift_all = [
        jnp.concatenate([row(item), other[2 + slot : 3 + slot, :half]], axis=1)
        for slot, item in enumerate(vectors)
    ]
    kernel_all = jnp.concatenate([small[8 : 9 + taps, :half], other[8 : 9 + taps, :half]], axis=1)
    early_up_all, early_down_all = both(early_up), both(early_down)
    key_all, value_all, query_all = both(key_weight), both(value_weight), both(query_weight)
    table = distance_table.astype(LOW)
    table = jnp.concatenate([table, jnp.broadcast_to(table[REL - 1 :], (TILE - REL, HEAD_DIM))], axis=0)
    table = jnp.concatenate([table, table], axis=1)

    n1, s10, a10, x1 = feed_half(
        True, inputs, (row(early_norm_gain), row(early_norm_shift)), early_up_all[0], early_bias[0], early_down_all[0]
    )
    s11, a11, x1 = feed_half(
        False, inputs, (n1, x1, row(early_down_bias)), early_up_all[1], early_bias[1], early_down_all[1]
    )
    n2, kv = project(x1, row(attend_norm_gain), row(attend_norm_shift), key_all, value_all, value_bias_all)
    kvr = swap(kv)
    q = query(n2, query_all, query_bias_all)
    attend_all, gated_all = both(attend_weight), both(gated_weight)
    q, attend_other, gated_other = hold((q, attend_all[1], gated_all[1]))
    attend_all, gated_all = (attend_weight, attend_other), (gated_weight, gated_other)
    o, lse = attend(core, q, kv, kvr, table)
    o, late_up, late_down, mixer_weight = hold((o, late_up, late_down, mixer_weight))
    mixer_all = both(mixer_weight)
    late_up_all, late_down_all = both(late_up), both(late_down)
    n1p, a1p, n2p = swap(n1), swap(a11), swap(n2)
    x2, n3, u, sig, edge = mixer_in(
        o, x1, attend_all, row(attend_bias), row(mixer_norm_gain), row(mixer_norm_shift), gated_all
    )
    edge = lax.ppermute(edge, "tensor", [(0, 1)])
    op, n3p = swap(o[1:]), swap(n3)
    z, w0, w1, x3 = mixer_out(u, edge, kernel_all, depth_gain_all, depth_shift_all, mixer_all, x2)
    wp = swap(w1)
    x3, n1p, a1p, n2p = hold((x3, n1p, a1p, n2p))
    n4, s40, s41, a40, a41, x4 = feed_forward(
        x3, row(late_norm_gain), row(late_norm_shift), late_up_all, late_bias, late_down_all, row(late_down_bias)
    )
    n4p, a4p = swap(n4), swap(a41)
    x4, op, n3p, wp = hold((x4, op, n3p, wp))
    output, g4, d4, final_sums = final_norm(slot_flags, x4, cotangent, row(final_gain), row(final_shift))
    d4p = swap(d4)

    reduction = functools.partial(Reduction, devices, me)
    k40, k41, t40, t41, g3, d3, late_sums = feed_back(
        1.0, g4, d4, x3, row(late_norm_gain), late_up_all, late_down_all, (s40, s41)
    )
    d3, d4p, n4p, a4p = hold((d3, d4p, n4p, a4p))
    k4p, d3p = swap(k41), swap(d3)
    one = reduction([(d4, d4p)], [(0, (a40, a4p), (0, 0, 1, 1))])
    (d3,) = hold((d3,), one)
    one.send()
    bz, depth_sums, head = mixer_mid(d3, mixer_all, z, depth_gain_all, depth_shift_all)
    tail = lax.ppermute(head, "tensor", [(1, 0)])
    k4p, d3p, bz = hold((k4p, d3p, bz))
    two = reduction([(n4, n4p)], [(0, (k40, k4p), (0, 0, 1, 1))])
    (bz,) = hold((bz,), two)
    two.send()
    ka0, ka1, dkernel, g2, d2, do0, do1, mixer_sums = mixer_back(
        bz, tail, u, edge, kernel_all, sig, gated_all, x2, row(mixer_norm_gain), g3, attend_all
    )
    kap, d2p = swap(ka1), swap(d2)
    one.add()
    do0, kap, d2p = hold((do0, kap, d2p), one)
    one.send()
    kq0, dk0, dv0, dkv0, dtable0 = attend_back(core, 0, q, do0, o, kv, kvr, table, lse)
    far1 = swap(dkv0)
    one.add()
    two.add()
    three = reduction(
        [(d3, d3p), (n3, n3p), (d2, d2p)],
        [(0, (w0, wp), (0,)), (1, (ka0, kap), (0, 1)), (2, (o, op), (1,))],
    )
    do1, kq0, far1 = hold((do1, kq0, far1), one, two, three)
    one.send()
    two.send()
    three.send()
    kq1, dk1, dv1, dkv1, dtable1 = attend_back(core, q.shape[1] // TILE // 2, q, do1, o, kv, kvr, table, lse)
    far0, kqp = swap(dkv1), swap(kq1)
    one.add()
    two.add()
    three.add()
    dk0, kq1 = hold((dk0, kq1), one, two, three)
    one.send()
    two.send()
    three.send()
    kk0, kk1, g1, d1, attend_sums = project_back(
        (kq0, dk0, dv0, far0), (kq1, dk1, dv1, far1), query_all, key_all, value_all, x1, row(attend_norm_gain), g2
    )
    d1p, kkp = swap(d1), swap(kk1)
    one.add()
    two.add()
    three.add()
    d1p, kkp = hold((d1p, kkp), one, two, three)
    two.send()
    three.send()
    four = reduction(
        [(d1, d1p), (n2, n2p)],
        [
            (0, (a10, a1p), (2, 2, 2, 3, 3, 3, 4, 4)),
            (1, (kq0, kqp), (2, 2)),
            (1, (kk0, kkp), (3, 3, 4, 4)),
        ],
        256,
    )
    (d1,) = hold((d1,), four)
    four.send()
    k10, k11, t10, t11 = feed_key(d1, early_down_all, (s10, s11))
    k1p = swap(k11)
    two.add()
    three.add()
    (k10,) = hold((k10,), two, three)
    three.send()
    gradient, early_sums = feed_end(g1, d1, inputs, row(early_norm_gain), early_up_all, (k10, k11))
    three.add()
    (early_sums,) = hold((early_sums,), four)
    four.add()
    early_sums, k1p = hold((early_sums, k1p), four, three)
    four.send()
    small_own, small_oth = pack(
        (
            late_sums, final_sums, mixer_sums, attend_sums, depth_sums, early_sums, dkernel,
            dtable0, dtable1, t10, t11, t40, t41,
        )
    )
    first = small_own
    masks = [1 << bit for bit in (3, 0, 1, 2, *range(4, devices.bit_length() - 1))]
    if devices & (devices - 1) or devices < 16:
        masks = []
    n1, small_oth = hold((n1, small_oth))
    moved = swap(small_oth)
    five = reduction([(n1, n1p)], [(0, (k10, k1p), (2, 2, 2, 3, 3, 3, 4, 4))], 256)
    first, moved = hold((first, moved), five)
    five.send()
    for step in range(4):
        first = first + moved
        moved = cross(first, devices, masks[step]) if masks else jnp.zeros_like(first)
        if step < 3:
            four.add()
        if step < 2:
            four.send()
        five.add()
        (first,) = hold((first,), four, five)
        if step < 3:
            five.send()
    first = first + moved
    for mask in masks[4:]:
        first = first + cross(first, devices, mask)
    if not masks:
        first = lax.psum(first, "dp")
    (late_down_sum,) = one.parts()
    (late_up_sum,) = two.parts()
    mixer_sum, gated_sum, attend_sum = three.parts()
    early_down_sum, query_sum, project_sum = four.parts()
    (early_up_sum,) = five.parts()

    table_out = jnp.concatenate(
        [first[SHARED - 11 : SHARED - 1, g * TILE : (g + 1) * TILE] for g in range(8)], axis=0
    )[:REL]
    table_out = table_out[:, :HEAD_DIM] + table_out[:, HEAD_DIM:]
    left, right = first[SHARED : SHARED + 18, :half], first[SHARED : SHARED + 17, half:]
    pile_sum = jnp.concatenate([left, right], axis=0)
    early_rows = first[10:13]
    count = hidden // (2 * half)
    early_up_bias_sum = first[SHARED + 18 : SHARED + 18 + count].reshape(-1)
    late_up_bias_sum = first[SHARED + 18 + count : SHARED + 18 + 2 * count].reshape(-1)
    return (
        output,
        gradient,
        early_rows[0],
        early_rows[1],
        early_up_sum,
        early_up_bias_sum,
        early_down_sum.T,
        early_rows[2],
        first[8],
        first[9],
        query_sum,
        pile_sum[0],
        project_sum[:, :half],
        project_sum[:, half:],
        pile_sum[1],
        table_out,
        attend_sum.T,
        first[7],
        first[5],
        first[6],
        jnp.stack([gated_sum[:, :half], gated_sum[:, half:]]),
        pile_sum[4:],
        pile_sum[2],
        pile_sum[3],
        mixer_sum.T,
        first[0],
        first[1],
        late_up_sum,
        late_up_bias_sum,
        late_down_sum.T,
        first[2],
        first[3],
        first[4],
    )


def solution(mesh):
    placed = (
        P(("dp", "tensor"), None),
        P(("dp", "tensor"), None),
        P("dp"),
        P(),
        P(),
        P(None, "tensor"),
        P("tensor"),
        P("tensor", None),
        P(),
        P(),
        P(),
        P(None, "tensor"),
        P("tensor"),
        P(None, "tensor"),
        P(None, "tensor"),
        P("tensor"),
        P(),
        P("tensor", None),
        P(),
        P(),
        P(),
        P(None, None, "tensor"),
        P(None, "tensor"),
        P("tensor"),
        P("tensor"),
        P("tensor", None),
        P(),
        P(),
        P(None, "tensor"),
        P("tensor"),
        P("tensor", None),
        P(),
        P(),
        P(),
    )
    return jax.shard_map(
        functools.partial(shards, mesh.shape["dp"]),
        mesh=mesh,
        in_specs=placed,
        out_specs=(
            P(("dp", "tensor"), None),
            P(("dp", "tensor"), None),
            P(),
            P(),
            P("dp", "tensor"),
            P("tensor"),
            P("tensor", "dp"),
            P(),
            P(),
            P(),
            P("dp", "tensor"),
            P("tensor"),
            P("dp", "tensor"),
            P("dp", "tensor"),
            P("tensor"),
            P(),
            P("tensor", "dp"),
            P(),
            P(),
            P(),
            P(None, "dp", "tensor"),
            P(None, "tensor"),
            P("tensor"),
            P("tensor"),
            P("tensor", "dp"),
            P(),
            P(),
            P("dp", "tensor"),
            P("tensor"),
            P("tensor", "dp"),
            P(),
            P(),
            P(),
        ),
        check_vma=False,
    )
```

time: 2930 us -> 533 us (0.18)
  waiting for transfers between devices: 1580 us -> 66.2 us
  local copies, waits for them, and re-layouts: 563 us -> 17.8 us
  other arithmetic: 399 us -> 20.9 us
  Pallas kernels: 0 us -> 357 us
  matrix products: 309 us -> 0 us
  starting transfers between devices: 2.36 us -> 57.7 us
    reduce_scatter x18 -> x0, waiting for transfers between devices: 1230 us -> none  [the longest x1 183 us: shards(): lax.psum_scatter(early_matrices[1], 'dp', scatter_dimension=1, tiled=True)]
    pallas_call x0 -> x24, Pallas kernels: none -> 357 us  [launch(): pl.pallas_call(body, grid_spec=pltpu.PrefetchScalarGridSpec(num_scalar_pr...]
    dot_general x51 -> x0, matrix products: 309 us -> none  [the longest x11 68.4 us: contract_rows(): lax.dot_general(left, right, (((0,), (0,)), ((), ())), preferred_element_...]
    psum x2 -> x0, waiting for transfers between devices: 262 us -> none  [the longest x1 143 us: shards(): lax.psum((early_norms[0], early_norms[1], early_norms[2], attend_norms[0]...]
    add x67 -> x44, other arithmetic: 267 us -> 13.7 us  [the longest x33 10.8 us: add(): stay = [one[half:] + two[half:] for one, two in zip(arrived, kept)]]
    while x95 -> x0, local copies, waits for them, and re-layouts: 157 us -> none
    reshape x14 -> x0, local copies, waits for them, and re-layouts: 143 us -> none  [the longest x4 53.1 us: skew_band(): flat[:, :count * (width + count - 1)]]
    all_gather x8 -> x0, waiting for transfers between devices: 96.3 us -> none  [the longest x4 48.8 us: gather_rows(): return lax.all_gather(values, 'tensor', axis=0, tiled=True)]
  transfers between devices with their start and end apart: 28 -> 76, of which waited for: 27 -> 18; matrix products, arithmetic and copies ran while one was open for 3% -> 4% of each run, Pallas kernels for 0% -> 62%
where the time goes in v1:
time: 533 us; the launch traced here: 523 us
  Pallas kernels  357 us (67%)
  waiting for transfers between devices  66.2 us (12%)
  starting transfers between devices  57.7 us (11%)
  other arithmetic  20.9 us (4%)
  local copies, waits for them, and re-layouts  17.8 us (3%)
    pallas_call x24, Pallas kernels, launch(): pl.pallas_call(body, grid_spec=pltpu.PrefetchScalarGridSpec(num_scalar_pr...  357 us
    ppermute x42, waiting for transfers between devices, cross(): return lax.ppermute(values, 'dp', [(i, i ^ mask) for i in range(devices)])  56.4 us
    ppermute x42, starting transfers between devices, cross(): return lax.ppermute(values, 'dp', [(i, i ^ mask) for i in range(devices)])  44.8 us
    unnamed x91, local copies, waits for them, and re-layouts  12 us
    add x33, other arithmetic, add(): stay = [one[half:] + two[half:] for one, two in zip(arrived, kept)]  10.8 us
  transfers between devices with their start and end apart: 76, of which 18 were waited for; matrix products, arithmetic and copies ran while one was open for 4% of the time, Pallas kernels for 62%

profile of v1, /device:TPU:0, one launch (start us, length us, event | category | flops | bytes accessed | tf_op | source)
XLA Modules:
  0.0 522.5 jit_solution(5017834930889192927)
XLA Ops:
  1.3 1.7 gather.1
  3.9 12.8 %feed_half.2 = (bf16[512,1024]{1,0:T(8,128)(2,1)}, bf16[512,2048]{1,0:T(8,128)(2,1)}, bf16[512,2048]{1,0:T(8,128)(2,1)}, f32[512,1024]{1,0:T(8,128)}) custom-call(bf16[512,1024]{1,0:T(8,128)(2,1)} %x.5, f32[1,1024]{1,0:T(1,128)} %bitcast.82, f32[1,1024]{1,0:T(1,128)} %bitcast.103, bf16[1024,2048]{1,0:T(8,128)(2,1)} %up0.3, f32[1,2048]{1,0:T(1,128)} %bitcast.73, ...), custom_call_target="tpu_custom_call" | custom-call | flops 4294967296 | bytes 16793600 | tf_op jit(solution)/shard_map/feed_half/pallas_call | solution.py:54
  18.2 2.1 copy-done.2
  20.2 12.0 %feed_half.3 = (bf16[512,2048]{1,0:T(8,128)(2,1)}, bf16[512,2048]{1,0:T(8,128)(2,1)}, f32[512,1024]{1,0:T(8,128)}) custom-call(bf16[512,1024]{1,0:T(8,128)(2,1)} %x.5, bf16[512,1024]{1,0:T(8,128)(2,1)} %get-tuple-element.438.refs_0_, f32[512,1024]{1,0:T(8,128)} %get-tuple-element.264.refs_1_, f32[1,1024]{1,0:T(1,128)} %bitcast.104, ...), custom_call_target="tpu_custom_call" | custom-call | flops 4294967296 | bytes 18886656 | tf_op jit(solution)/shard_map/feed_half/pallas_call | solution.py:54
  33.3 8.4 %project.1 = (bf16[512,1024]{1,0:T(8,128)(2,1)}, bf16[512,2048]{1,0:T(8,128)(2,1)}) custom-call(f32[512,1024]{1,0:T(8,128)} %get-tuple-element.265.x, f32[1,1024]{1,0:T(1,128)} %bitcast.80, f32[1,1024]{1,0:T(1,128)} %bitcast.105, bf16[1024,512]{1,0:T(8,128)(2,1)} %kw0.3, bf16[1024,512]{1,0:T(8,128)(2,1)} %copy-done.9, bf16[1024,512]{1,0:T(8,128)(2,1)} %vw0.3, ...), custom_call_target="tpu_custom_call" | custom-call | flops 2147483648 | bytes 9449472 | tf_op jit(solution)/shard_map/project/pallas_call | solution.py:54
  44.0 3.7 collective-permute-done.5.qw1
  47.7 4.1 query.1.q
  53.1 35.2 %attend.1 = (bf16[2,512,512]{2,1,0:T(8,128)(2,1)}, f32[64,512]{1,0:T(8,128)}) custom-call(s32[1]{0:T(128)} %bitcast.core, bf16[512,1024]{1,0:T(8,128)(2,1)} %query.1.q, bf16[512,2048]{1,0:T(8,128)(2,1)} %get-tuple-element.268.k0.v0, bf16[512,2048]{1,0:T(8,128)(2,1)} %get-tuple-element.268.k0.v0, bf16[512,2048]{1,0:T(8,128)(2,1)} %copy-done, ...), custom_call_target="tpu_custom_call" | custom-call | flops 2147483648 | bytes 10649600 | tf_op jit(solution)/shard_map/attend/pallas_call | solution.py:54
  89.4 12.3 %mixer_in.1 = (f32[512,1024]{1,0:T(8,128)}, bf16[512,1024]{1,0:T(8,128)(2,1)}, f32[512,1024]{1,0:T(8,128)}, f32[512,1024]{1,0:T(8,128)}, f32[32,1024]{1,0:T(8,128)}) custom-call(bf16[2,512,512]{2,1,0:T(8,128)(2,1)} %get-tuple-element.270.o0.o1.o.refs_10_, bf16[2,512,512]{2,1,0:T(8,128)(2,1)} %get-tuple-element.270.o0.o1.o.refs_10_, ...), custom_call_target="tpu_custom_call" | custom-call | flops 3221225472 | bytes 22163456 | tf_op jit(solution)/shard_map/mixer_in/pallas_call | solution.py:54
  101.7 2.5 collective-permute-start.9
  104.2 2.2 collective-permute-done.9.edge
  110.1 13.9 %mixer_out.1 = (f32[512,1024]{1,0:T(8,128)}, bf16[512,512]{1,0:T(8,128)(2,1)}, bf16[512,512]{1,0:T(8,128)(2,1)}, f32[512,1024]{1,0:T(8,128)}) custom-call(f32[512,1024]{1,0:T(8,128)} %get-tuple-element.273.u, f32[32,1024]{1,0:T(8,128)} %copy-done.21, f32[32,1024]{1,0:T(8,128)} %pad_maximum_fusion.11.kernel, f32[1,1024]{1,0:T(1,128)} %get-tuple-element.635.gain, ...), custom_call_target="tpu_custom_call" | custom-call | flops 1073741824 | bytes 11804672 | tf_op jit(solution)/shard_map/mixer_out/pallas_call | solution.py:54
  124.9 20.9 %feed_forward.1 = (bf16[512,1024]{1,0:T(8,128)(2,1)}, bf16[512,2048]{1,0:T(8,128)(2,1)}, bf16[512,2048]{1,0:T(8,128)(2,1)}, bf16[512,2048]{1,0:T(8,128)(2,1)}, b...) custom-call(f32[512,1024]{1,0:T(8,128)} %get-tuple-element.279.x, f32[1,1024]{1,0:T(1,128)} %bitcast.108, ...), custom_call_target="tpu_custom_call" | custom-call | flops 8589934592 | bytes 30437376 | tf_op jit(solution)/shard_map/feed_forward/pallas_call | solution.py:54
  146.8 5.8 %final_norm.1 = (bf16[512,1024]{1,0:T(8,128)(2,1)}, f32[512,1024]{1,0:T(8,128)}, bf16[512,1024]{1,0:T(8,128)(2,1)}, f32[16,1024]{1,0:T(8,128)}) custom-call(s32[1]{0:T(128)S(6)} %copy.75.flag, f32[512,1024]{1,0:T(8,128)} %get-tuple-element.285.x, bf16[512,1024]{1,0:T(8,128)(2,1)} %cotangent.1, f32[1,1024]{1,0:T(1,128)} %bitcast.78, f32[1,1024]{1,0:T(1,128)} %bitcast.79), custom_call_target="tpu_custom_call" | custom-call | bytes 7413760 | tf_op jit(solution)/shard_map/final_norm/pallas_call | solution.py:54
  153.1 22.0 %feed_back.1 = (bf16[512,2048]{1,0:T(8,128)(2,1)}, bf16[512,2048]{1,0:T(8,128)(2,1)}, f32[8,2048]{1,0:T(8,128)}, f32[8,2048]{1,0:T(8,128)}, f32[512,1024]{1,0:T(...) custom-call(f32[512,1024]{1,0:T(8,128)} %get-tuple-element.287.g, bf16[512,1024]{1,0:T(8,128)(2,1)} %get-tuple-element.288.d.refs_0_, ...), custom_call_target="tpu_custom_call" | custom-call | flops 8589934592 | bytes 33787904 | tf_op jit(solution)/shard_map/feed_back/pallas_call | solution.py:54
  177.8 9.5 %weight_gradient.5 = (bf16[512,1024]{1,0:T(8,128)(2,1)}, bf16[512,1024]{1,0:T(8,128)(2,1)}, bf16[512,1024]{1,0:T(8,128)(2,1)}, bf16[512,1024]{1,0:T(8,128)(2,1)}) custom-call(s32[1]{0:T(128)} %bitcast.21.me, bf16[512,1024]{1,0:T(8,128)(2,1)} %get-tuple-element.288.d.refs_0_, bf16[512,1024]{1,0:T(8,128)(2,1)} %collective-permute-done.20.refs_1_, ...), custom_call_target="tpu_custom_call" | custom-call | flops 4294967296 | bytes 10485760 | tf_op jit(solution)/shard_map/weight_gradient/pallas_call | solution.py:54
  187.3 2.6 collective-permute-start.28
  191.5 8.8 %mixer_mid.1 = (f32[512,1024]{1,0:T(8,128)}, f32[16,1024]{1,0:T(8,128)}, f32[32,1024]{1,0:T(8,128)}) custom-call(bf16[512,1024]{1,0:T(8,128)(2,1)} %get-tuple-element.303.d.refs_0_, bf16[512,1024]{1,0:T(8,128)(2,1)} %out0.4, bf16[512,1024]{1,0:T(8,128)(2,1)} %copy-done.5, f32[512,1024]{1,0:T(8,128)} %get-tuple-element.304.z, ...), custom_call_target="tpu_custom_call" | custom-call | flops 1073741824 | bytes 7544832 | tf_op jit(solution)/shard_map/mixer_mid/pallas_call | solution.py:54
  201.6 9.7 %weight_gradient.6 = (bf16[512,1024]{1,0:T(8,128)(2,1)}, bf16[512,1024]{1,0:T(8,128)(2,1)}, bf16[512,1024]{1,0:T(8,128)(2,1)}, bf16[512,1024]{1,0:T(8,128)(2,1)}) custom-call(s32[1]{0:T(128)} %bitcast.21.me, bf16[512,1024]{1,0:T(8,128)(2,1)} %get-tuple-element.293.refs_0_, bf16[512,1024]{1,0:T(8,128)(2,1)} %copy-done.36, ...), custom_call_target="tpu_custom_call" | custom-call | flops 4294967296 | bytes 10485760 | tf_op jit(solution)/shard_map/weight_gradient/pallas_call | solution.py:54
  212.0 24.6 %mixer_back.1 = (bf16[2,512,512]{2,1,0:T(8,128)(2,1)}, bf16[2,512,512]{2,1,0:T(8,128)(2,1)}, f32[32,1024]{1,0:T(8,128)}, f32[512,1024]{1,0:T(8,128)}, bf16[512,1...) custom-call(f32[512,1024]{1,0:T(8,128)} %get-tuple-element.314.bz, ...), custom_call_target="tpu_custom_call" | custom-call | flops 3221225472 | bytes 27889664 | tf_op jit(solution)/shard_map/mixer_back/pallas_call | solution.py:54
  244.8 34.3 %attend_back.2 = (bf16[512,512]{1,0:T(8,128)(2,1)}, f32[512,512]{1,0:T(8,128)}, f32[512,512]{1,0:T(8,128)}, bf16[2,512,512]{2,1,0:T(8,128)(2,1)}, f32[128,128]{1,0:T(8,128)}) custom-call(s32[1]{0:T(128)} %bitcast.core, bf16[512,1024]{1,0:T(8,128)(2,1)} %query.1.q, bf16[512,512]{1,0:T(8,128)(2,1)} %get-tuple-element.326.do, ...), custom_call_target="tpu_custom_call" | custom-call | flops 2684354560 | bytes 14909440 | tf_op jit(solution)/shard_map/attend_back/pallas_call | solution.py:54
  279.2 12.4 %weight_gradient.7 = (bf16[512,1024]{1,0:T(8,128)(2,1)}, bf16[512,1024]{1,0:T(8,128)(2,1)}, bf16[512,1024]{1,0:T(8,128)(2,1)}, bf16[512,1024]{1,0:T(8,128)(2,1)}) custom-call(s32[1]{0:T(128)} %bitcast.21.me, bf16[512,1024]{1,0:T(8,128)(2,1)} %get-tuple-element.303.d.refs_0_, bf16[512,1024]{1,0:T(8,128)(2,1)} %copy-done.34, ...), custom_call_target="tpu_custom_call" | custom-call | flops 4294967296 | bytes 15204352 | tf_op jit(solution)/shard_map/weight_gradient/pallas_call | solution.py:54
  291.7 2.2 slice_add_fusion.8
  300.9 1.6 collective-permute-start.34
  302.5 34.1 %attend_back.3 = (bf16[512,512]{1,0:T(8,128)(2,1)}, f32[512,512]{1,0:T(8,128)}, f32[512,512]{1,0:T(8,128)}, bf16[2,512,512]{2,1,0:T(8,128)(2,1)}, f32[128,128]{1,0:T(8,128)}) custom-call(s32[1]{0:T(128)} %bitcast.core, bf16[512,1024]{1,0:T(8,128)(2,1)} %query.1.q, bf16[512,512]{1,0:T(8,128)(2,1)} %get-tuple-element.352.do, ...), custom_call_target="tpu_custom_call" | custom-call | flops 2684354560 | bytes 14909440 | tf_op jit(solution)/shard_map/attend_back/pallas_call | solution.py:54
  343.2 2.6 collective-permute-start.42
  345.9 14.2 %project_back.1 = (bf16[2,512,512]{2,1,0:T(8,128)(2,1)}, bf16[2,512,512]{2,1,0:T(8,128)(2,1)}, f32[512,1024]{1,0:T(8,128)}, bf16[512,1024]{1,0:T(8,128)(2,1)}, f32[32,1024]{1,0:T(8,128)}) custom-call(bf16[512,512]{1,0:T(8,128)(2,1)} %get-tuple-element.350.kq0.refs_6_, f32[512,512]{1,0:T(8,128)} %get-tuple-element.364.dk0, ...), custom_call_target="tpu_custom_call" | custom-call | flops 3221225472 | bytes 23203840 | tf_op jit(solution)/shard_map/project_back/pallas_call | solution.py:54
  364.5 4.4 collective-permute-start.48
  369.0 19.4 %weight_gradient.8 = (bf16[512,1280]{1,0:T(8,128)(2,1)}, bf16[512,1280]{1,0:T(8,128)(2,1)}, bf16[512,1280]{1,0:T(8,128)(2,1)}, bf16[512,1280]{1,0:T(8,128)(2,1)}...) custom-call(s32[1]{0:T(128)} %bitcast.21.me, bf16[512,1024]{1,0:T(8,128)(2,1)} %get-tuple-element.395.refs_0_.d, ...), custom_call_target="tpu_custom_call" | custom-call | flops 7516192768 | bytes 18874368 | tf_op jit(solution)/shard_map/weight_gradient/pallas_call | solution.py:54
  392.4 12.3 %feed_key.1 = (bf16[512,2048]{1,0:T(8,128)(2,1)}, bf16[512,2048]{1,0:T(8,128)(2,1)}, f32[8,2048]{1,0:T(8,128)}, f32[8,2048]{1,0:T(8,128)}) custom-call(bf16[512,1024]{1,0:T(8,128)(2,1)} %get-tuple-element.395.refs_0_.d, bf16[2048,1024]{1,0:T(8,128)(2,1)} %down0.3, bf16[2048,1024]{1,0:T(8,128)(2,1)} %collective-permute-done.2.refs_5_.down1, ...), custom_call_target="tpu_custom_call" | custom-call | flops 4294967296 | bytes 17956864 | tf_op jit(solution)/shard_map/feed_key/pallas_call | solution.py:54
  405.6 2.1 collective-permute-start.53
  407.7 15.6 %feed_end.1 = (f32[512,1024]{1,0:T(8,128)}, f32[24,1024]{1,0:T(8,128)}) custom-call(f32[512,1024]{1,0:T(8,128)} %get-tuple-element.372.g, bf16[512,1024]{1,0:T(8,128)(2,1)} %get-tuple-element.395.refs_0_.d, bf16[512,1024]{1,0:T(8,128)(2,1)} %x.5, f32[1,1024]{1,0:T(1,128)} %bitcast.83, bf16[1024,2048]{1,0:T(8,128)(2,1)} %up0.3, bf16[1024,2048]{1,0:T(8,128)(2,1)} %copy-done.2, ...), custom_call_target="tpu_custom_call" | custom-call | flops 4294967296 | bytes 18976768 | tf_op jit(solution)/shard_map/feed_end/pallas_call | solution.py:54
  426.9 2.0 collective-permute-start.57
  428.9 2.2 pack.1
  431.7 10.9 %weight_gradient.9 = (bf16[512,768]{1,0:T(8,128)(2,1)}, bf16[512,768]{1,0:T(8,128)(2,1)}, bf16[512,768]{1,0:T(8,128)(2,1)}, bf16[512,768]{1,0:T(8,128)(2,1)}, bf...) custom-call(s32[1]{0:T(128)} %bitcast.21.me, bf16[512,1024]{1,0:T(8,128)(2,1)} %get-tuple-element.438.refs_0_, ...), custom_call_target="tpu_custom_call" | custom-call | flops 4294967296 | bytes 10485760 | tf_op jit(solution)/shard_map/weight_gradient/pallas_call | solution.py:54
  442.8 1.6 collective-permute-start.62
  447.0 1.8 collective-permute-done.55
  449.4 11.7 %collective-permute-done.63 = bf16[512,512]{1,0:T(8,128)(2,1)S(1)} collective-permute-done((bf16[512,512]{1,0:T(8,128)(2,1)}, bf16[512,512]{1,0:T(8,128)(2,1)S(1)}, u32[]{:S(2)}, u32[]{:S(2)}) %collective-permute-start.63) | collective-permute-done | bytes 524320 | tf_op jit(solution)/shard_map/ppermute | solution.py:1259
  462.7 3.0 collective-permute-done.62
  465.9 4.9 collective-permute-done.60
  471.0 3.3 collective-permute-done.56
  478.2 4.7 collective-permute-done.68
  482.9 8.4 %collective-permute-done.67 = bf16[256,768]{1,0:T(8,128)(2,1)S(1)} collective-permute-done((bf16[256,768]{1,0:T(8,128)(2,1)S(1)}, bf16[256,768]{1,0:T(8,128)(2,1)S(1)}, u32[]{:S(2)}, u32[]{:S(2)}) %collective-permute-start.67) | collective-permute-done | bytes 393248 | tf_op jit(solution)/shard_map/ppermute | solution.py:1259
  491.4 6.1 %collective-permute-done.65 = bf16[64,3584]{1,0:T(8,128)(2,1)S(1)} collective-permute-done((bf16[64,3584]{1,0:T(8,128)(2,1)S(1)}, bf16[64,3584]{1,0:T(8,128)(2,1)S(1)}, u32[]{:S(2)}, u32[]{:S(2)}) %collective-permute-start.65) | collective-permute-done | bytes 458784 | tf_op jit(solution)/shard_map/ppermute | solution.py:1259
  498.1 1.6 collective-permute-start.72
  500.3 2.8 collective-permute-done.72
  503.1 1.7 collective-permute-done.70
  507.6 7.4 %collective-permute-done.74 = bf16[64,2048]{1,0:T(8,128)(2,1)S(1)} collective-permute-done((bf16[64,2048]{1,0:T(8,128)(2,1)S(1)}, bf16[64,2048]{1,0:T(8,128)(2,1)S(1)}, u32[]{:S(2)}, u32[]{:S(2)}) %collective-permute-start.74) | collective-permute-done | bytes 262176 | tf_op jit(solution)/shard_map/ppermute | solution.py:1259
  (297 shorter events, 75.7 us)
Async XLA Ops:
  3.4 28.9 %collective-permute-start.3 = (bf16[1024,512]{1,0:T(8,128)(2,1)}, bf16[1024,512]{1,0:T(8,128)(2,1)S(1)}, u32[]{:S(2)}, u32[]{:S(2)}) collective-permute-start(bf16[1024,512]{1,0:T(8,128)(2,1)} %kw0.3), channel_id=1, source_target_pairs={{0,1},{1,0},{2,3},{3,2},{4,5},{5,4},{6,7},{7,6},{8,9},{9,8},{10,11... | collective-permute-start | bytes 3145736 | tf_op jit(solution)/shard_map/ppermute | solution.py:1255
  3.5 28.8 %collective-permute-start.4 = (bf16[1024,512]{1,0:T(8,128)(2,1)}, bf16[1024,512]{1,0:T(8,128)(2,1)}, u32[]{:S(2)}, u32[]{:S(2)}) collective-permute-start(bf16[1024,512]{1,0:T(8,128)(2,1)} %vw0.3), channel_id=1, source_target_pairs={{0,1},{1,0},{2,3},{3,2},{4,5},{5,4},{6,7},{7,6},{8,9},{9,8},{10,11... | collective-permute-start | bytes 3145736 | tf_op jit(solution)/shard_map/ppermute | solution.py:1255
  16.8 35.0 %collective-permute-start.7 = (bf16[2,1024,512]{2,1,0:T(8,128)(2,1)}, bf16[2,1024,512]{2,1,0:T(8,128)(2,1)}, u32[]{:S(2)}, u32[]{:S(2)}) collective-permute-start(bf16[2,1024,512]{2,1,0:T(8,128)(2,1)} %gate0.3), channel_id=1, source_target_pairs={{0,1},{1,0},{2,3},{3,2},{4,5},{5,4},{6,7},{7,6},{8,9},{9,8},{10,11... | collective-permute-start | bytes 6291464 | tf_op jit(solution)/shard_map/ppermute | solution.py:1255
  88.3 36.5 %collective-permute-start.14 = (bf16[1024,2048]{1,0:T(8,128)(2,1)}, bf16[1024,2048]{1,0:T(8,128)(2,1)}, u32[]{:S(2)}, u32[]{:S(2)}) collective-permute-start(bf16[1024,2048]{1,0:T(8,128)(2,1)} %up0.2), channel_id=1, source_target_pairs={{0,1},{1,0},{2,3},{3,2},{4,5},{5,4},{6,7},{7,6},{8,9},{9,8},{10,11... | collective-permute-start | bytes 12582920 | tf_op jit(solution)/shard_map/ppermute | solution.py:1255
  88.7 36.2 %collective-permute-start.15 = (bf16[2048,1024]{1,0:T(8,128)(2,1)}, bf16[2048,1024]{1,0:T(8,128)(2,1)}, u32[]{:S(2)}, u32[]{:S(2)}) collective-permute-start(bf16[2048,1024]{1,0:T(8,128)(2,1)} %down0.2), channel_id=1, source_target_pairs={{0,1},{1,0},{2,3},{3,2},{4,5},{5,4},{6,7},{7,6},{8,9},{9,8},{10,11... | collective-permute-start | bytes 12582920 | tf_op jit(solution)/shard_map/ppermute | solution.py:1255
  88.8 17.9 %collective-permute-start.10 = (bf16[512,1024]{1,0:T(8,128)(2,1)S(1)}, bf16[512,1024]{1,0:T(8,128)(2,1)S(1)}, u32[]{:S(2)}, u32[]{:S(2)}) collective-permute-start(bf16[512,1024]{1,0:T(8,128)(2,1)S(1)} %copy-done.3), channel_id=1, source_target_pairs={{0,1},{1,0},{2,3},{3,2},{4,5},{5,4},{6,7},{7,6},{8,9},{9,8},{10,11... | collective-permute-start | bytes 3145736 | tf_op jit(solution)/shard_map/ppermute | solution.py:1255
  89.2 35.3 %collective-permute-start.12 = (bf16[512,2048]{1,0:T(8,128)(2,1)}, bf16[512,2048]{1,0:T(8,128)(2,1)}, u32[]{:S(2)}, u32[]{:S(2)}) collective-permute-start(bf16[512,2048]{1,0:T(8,128)(2,1)} %get-tuple-element.278), channel_id=1, source_target_pairs={{0,1},{1,0},{2,3},{3,2},{4,5},{5,4},{6,7},{7,6},{8,9},{9,8},{10,11... | collective-permute-start | bytes 6291464 | tf_op jit(solution)/shard_map/ppermute | solution.py:1255
  124.0 22.7 %collective-permute-start.17 = (bf16[512,1024]{1,0:T(8,128)(2,1)}, bf16[512,1024]{1,0:T(8,128)(2,1)S(1)}, u32[]{:S(2)}, u32[]{:S(2)}) collective-permute-start(bf16[512,1024]{1,0:T(8,128)(2,1)} %get-tuple-element.283.refs_2_), channel_id=1, source_target_pairs={{0,1},{1,0},{2,3},{3,2},{4,5},{5,4},{6,7},{7,6},{8,9},{9,8},{10,11... | collective-permute-start | bytes 3145736 | tf_op jit(solution)/shard_map/ppermute | solution.py:1255
  124.3 22.4 %collective-permute-start.16 = (bf16[1,512,512]{2,1,0:T(8,128)(2,1)S(1)}, bf16[1,512,512]{2,1,0:T(8,128)(2,1)S(1)}, u32[]{:S(2)}, u32[]{:S(2)}) collective-permute-start(bf16[1,512,512]{2,1,0:T(8,128)(2,1)S(1)} %slice.605), channel_id=1, source_target_pairs={{0,1},{1,0},{2,3},{3,2},{4,5},{5,4},{6,7},{7,6},{8,9},{9,8},{10,11... | collective-permute-start | bytes 1572872 | tf_op jit(solution)/shard_map/ppermute | solution.py:1255
  124.6 22.2 %collective-permute-start.18 = (bf16[512,512]{1,0:T(8,128)(2,1)}, bf16[512,512]{1,0:T(8,128)(2,1)S(1)}, u32[]{:S(2)}, u32[]{:S(2)}) collective-permute-start(bf16[512,512]{1,0:T(8,128)(2,1)} %get-tuple-element.284), channel_id=1, source_target_pairs={{0,1},{1,0},{2,3},{3,2},{4,5},{5,4},{6,7},{7,6},{8,9},{9,8},{10,11... | collective-permute-start | bytes 1572872 | tf_op jit(solution)/shard_map/ppermute | solution.py:1255
  145.7 29.7 %collective-permute-start.22 = (bf16[512,2048]{1,0:T(8,128)(2,1)}, bf16[512,2048]{1,0:T(8,128)(2,1)S(1)}, u32[]{:S(2)}, u32[]{:S(2)}) collective-permute-start(bf16[512,2048]{1,0:T(8,128)(2,1)} %get-tuple-element.294), channel_id=1, source_target_pairs={{0,1},{1,0},{2,3},{3,2},{4,5},{5,4},{6,7},{7,6},{8,9},{9,8},{10,11... | collective-permute-start | bytes 6291464 | tf_op jit(solution)/shard_map/ppermute | solution.py:1255
  152.6 22.8 %collective-permute-start.20 = (bf16[512,1024]{1,0:T(8,128)(2,1)}, bf16[512,1024]{1,0:T(8,128)(2,1)}, u32[]{:S(2)}, u32[]{:S(2)}) collective-permute-start(bf16[512,1024]{1,0:T(8,128)(2,1)} %get-tuple-element.288.d.refs_0_), channel_id=1, source_target_pairs={{0,1},{1,0},{2,3},{3,2},{4,5},{5,4},{6,7},{7,6},{8,9},{9,8},{10,11... | collective-permute-start | bytes 3145736 | tf_op jit(solution)/shard_map/ppermute | solution.py:1255
  152.8 22.6 %collective-permute-start.21 = (bf16[512,1024]{1,0:T(8,128)(2,1)S(1)}, bf16[512,1024]{1,0:T(8,128)(2,1)S(1)}, u32[]{:S(2)}, u32[]{:S(2)}) collective-permute-start(bf16[512,1024]{1,0:T(8,128)(2,1)S(1)} %copy-done.35), channel_id=1, source_target_pairs={{0,1},{1,0},{2,3},{3,2},{4,5},{5,4},{6,7},{7,6},{8,9},{9,8},{10,11... | collective-permute-start | bytes 3145736 | tf_op jit(solution)/shard_map/ppermute | solution.py:1255
  175.1 26.5 %collective-permute-start.19 = (bf16[512,2048]{1,0:T(8,128)(2,1)}, bf16[512,2048]{1,0:T(8,128)(2,1)}, u32[]{:S(2)}, u32[]{:S(2)}) collective-permute-start(bf16[512,2048]{1,0:T(8,128)(2,1)} %get-tuple-element.291), channel_id=1, source_target_pairs={{0,1},{1,0},{2,3},{3,2},{4,5},{5,4},{6,7},{7,6},{8,9},{9,8},{10,11... | collective-permute-start | bytes 6291464 | tf_op jit(solution)/shard_map/ppermute | solution.py:1255
  176.4 25.2 %collective-permute-start.23 = (bf16[512,1024]{1,0:T(8,128)(2,1)}, bf16[512,1024]{1,0:T(8,128)(2,1)S(1)}, u32[]{:S(2)}, u32[]{:S(2)}) collective-permute-start(bf16[512,1024]{1,0:T(8,128)(2,1)} %get-tuple-element.303.d.refs_0_), channel_id=1, source_target_pairs={{0,1},{1,0},{2,3},{3,2},{4,5},{5,4},{6,7},{7,6},{8,9},{9,8},{10,11... | collective-permute-start | bytes 3145736 | tf_op jit(solution)/shard_map/ppermute | solution.py:1255
  187.3 51.1 %collective-permute-start.28 = (bf16[512,1024]{1,0:T(8,128)(2,1)}, bf16[512,1024]{1,0:T(8,128)(2,1)S(1)}, u32[]{:S(2)}, u32[]{:S(2)}) collective-permute-start(bf16[512,1024]{1,0:T(8,128)(2,1)} %get-tuple-element.324), channel_id=1, source_target_pairs={{0,4},{2,6},{4,0},{6,2},{8,12},{10,14},{12,8},{14,10},{16,20},{18,... | collective-permute-start | bytes 3145736 | tf_op jit(solution)/shard_map/ppermute | solution.py:1259
  190.0 49.5 %collective-permute-start.27 = (bf16[512,1024]{1,0:T(8,128)(2,1)}, bf16[512,1024]{1,0:T(8,128)(2,1)S(1)}, u32[]{:S(2)}, u32[]{:S(2)}) collective-permute-start(bf16[512,1024]{1,0:T(8,128)(2,1)} %get-tuple-element.322), channel_id=1, source_target_pairs={{0,2},{2,0},{4,6},{6,4},{8,10},{10,8},{12,14},{14,12},{16,18},{18,... | collective-permute-start | bytes 3145736 | tf_op jit(solution)/shard_map/ppermute | solution.py:1259
  237.9 53.8 %collective-permute-start.33 = (bf16[512,1024]{1,0:T(8,128)(2,1)}, bf16[512,1024]{1,0:T(8,128)(2,1)}, u32[]{:S(2)}, u32[]{:S(2)}) collective-permute-start(bf16[512,1024]{1,0:T(8,128)(2,1)} %get-tuple-element.336), channel_id=1, source_target_pairs={{0,4},{2,6},{4,0},{6,2},{8,12},{10,14},{12,8},{14,10},{16,20},{18,... | collective-permute-start | bytes 3145736 | tf_op jit(solution)/shard_map/ppermute | solution.py:1259
  238.4 55.4 %collective-permute-start.32 = (bf16[512,1024]{1,0:T(8,128)(2,1)}, bf16[512,1024]{1,0:T(8,128)(2,1)S(1)}, u32[]{:S(2)}, u32[]{:S(2)}) collective-permute-start(bf16[512,1024]{1,0:T(8,128)(2,1)} %get-tuple-element.334), channel_id=1, source_target_pairs={{0,2},{2,0},{4,6},{6,4},{8,10},{10,8},{12,14},{14,12},{16,18},{18,... | collective-permute-start | bytes 3145736 | tf_op jit(solution)/shard_map/ppermute | solution.py:1259
  241.8 53.0 %collective-permute-start.30 = (bf16[256,1024]{1,0:T(8,128)(2,1)}, bf16[256,1024]{1,0:T(8,128)(2,1)}, u32[]{:S(2)}, u32[]{:S(2)}) collective-permute-start(bf16[256,1024]{1,0:T(8,128)(2,1)} %get-tuple-element.330), channel_id=1, source_target_pairs={{0,4},{2,6},{4,0},{6,2},{8,12},{10,14},{12,8},{14,10},{16,20},{18,... | collective-permute-start | bytes 1572872 | tf_op jit(solution)/shard_map/ppermute | solution.py:1259
  243.4 52.5 %collective-permute-start.31 = (bf16[256,1024]{1,0:T(8,128)(2,1)}, bf16[256,1024]{1,0:T(8,128)(2,1)S(1)}, u32[]{:S(2)}, u32[]{:S(2)}) collective-permute-start(bf16[256,1024]{1,0:T(8,128)(2,1)} %get-tuple-element.332), channel_id=1, source_target_pairs={{0,2},{2,0},{4,6},{6,4},{8,10},{10,8},{12,14},{14,12},{16,18},{18,... | collective-permute-start | bytes 1572872 | tf_op jit(solution)/shard_map/ppermute | solution.py:1259
  279.1 17.7 %collective-permute-start.29 = (bf16[2,512,512]{2,1,0:T(8,128)(2,1)}, bf16[2,512,512]{2,1,0:T(8,128)(2,1)S(1)}, u32[]{:S(2)}, u32[]{:S(2)}) collective-permute-start(bf16[2,512,512]{2,1,0:T(8,128)(2,1)} %get-tuple-element.329), channel_id=1, source_target_pairs={{0,1},{1,0},{2,3},{3,2},{4,5},{5,4},{6,7},{7,6},{8,9},{9,8},{10,11... | collective-permute-start | bytes 3145736 | tf_op jit(solution)/shard_map/ppermute | solution.py:1255
  296.8 39.8 %collective-permute-start.35 = (bf16[256,1024]{1,0:T(8,128)(2,1)}, bf16[256,1024]{1,0:T(8,128)(2,1)}, u32[]{:S(2)}, u32[]{:S(2)}) collective-permute-start(bf16[256,1024]{1,0:T(8,128)(2,1)} %get-tuple-element.356), channel_id=1, source_target_pairs={{0,4},{2,6},{4,0},{6,2},{8,12},{10,14},{12,8},{14,10},{16,20},{18,... | collective-permute-start | bytes 1572872 | tf_op jit(solution)/shard_map/ppermute | solution.py:1259
  297.3 40.4 %collective-permute-start.36 = (bf16[256,1024]{1,0:T(8,128)(2,1)}, bf16[256,1024]{1,0:T(8,128)(2,1)}, u32[]{:S(2)}, u32[]{:S(2)}) collective-permute-start(bf16[256,1024]{1,0:T(8,128)(2,1)} %get-tuple-element.358), channel_id=1, source_target_pairs={{0,2},{2,0},{4,6},{6,4},{8,10},{10,8},{12,14},{14,12},{16,18},{18,... | collective-permute-start | bytes 1572872 | tf_op jit(solution)/shard_map/ppermute | solution.py:1259
  297.9 42.5 %collective-permute-start.38 = (bf16[512,1024]{1,0:T(8,128)(2,1)}, bf16[512,1024]{1,0:T(8,128)(2,1)S(1)}, u32[]{:S(2)}, u32[]{:S(2)}) collective-permute-start(bf16[512,1024]{1,0:T(8,128)(2,1)} %get-tuple-element.362), channel_id=1, source_target_pairs={{0,4},{2,6},{4,0},{6,2},{8,12},{10,14},{12,8},{14,10},{16,20},{18,... | collective-permute-start | bytes 3145736 | tf_op jit(solution)/shard_map/ppermute | solution.py:1259
  299.4 41.6 %collective-permute-start.37 = (bf16[512,1024]{1,0:T(8,128)(2,1)}, bf16[512,1024]{1,0:T(8,128)(2,1)S(1)}, u32[]{:S(2)}, u32[]{:S(2)}) collective-permute-start(bf16[512,1024]{1,0:T(8,128)(2,1)} %get-tuple-element.360), channel_id=1, source_target_pairs={{0,2},{2,0},{4,6},{6,4},{8,10},{10,8},{12,14},{14,12},{16,18},{18,... | collective-permute-start | bytes 3145736 | tf_op jit(solution)/shard_map/ppermute | solution.py:1259
  300.9 39.4 %collective-permute-start.34 = (bf16[128,2048]{1,0:T(8,128)(2,1)}, bf16[128,2048]{1,0:T(8,128)(2,1)S(1)}, u32[]{:S(2)}, u32[]{:S(2)}) collective-permute-start(bf16[128,2048]{1,0:T(8,128)(2,1)} %pad_maximum_fusion), channel_id=1, source_target_pairs={{0,8},{2,10},{4,12},{6,14},{8,0},{10,2},{12,4},{14,6},{16,24},{18,... | collective-permute-start | bytes 1572872 | tf_op jit(solution)/shard_map/ppermute | solution.py:1259
  337.8 31.2 %collective-permute-start.46 = (bf16[512,512]{1,0:T(8,128)(2,1)}, bf16[512,512]{1,0:T(8,128)(2,1)}, u32[]{:S(2)}, u32[]{:S(2)}) collective-permute-start(bf16[512,512]{1,0:T(8,128)(2,1)} %get-tuple-element.367.kq1), channel_id=1, source_target_pairs={{0,1},{1,0},{2,3},{3,2},{4,5},{5,4},{6,7},{7,6},{8,9},{9,8},{10,11... | collective-permute-start | bytes 1572872 | tf_op jit(solution)/shard_map/ppermute | solution.py:1255
  341.7 19.3 %collective-permute-start.44 = (bf16[256,1024]{1,0:T(8,128)(2,1)S(1)}, bf16[256,1024]{1,0:T(8,128)(2,1)S(1)}, u32[]{:S(2)}, u32[]{:S(2)}) collective-permute-start(bf16[256,1024]{1,0:T(8,128)(2,1)S(1)} %get-tuple-element.379), channel_id=1, source_target_pairs={{0,4},{2,6},{4,0},{6,2},{8,12},{10,14},{12,8},{14,10},{16,20},{18,... | collective-permute-start | bytes 1572872 | tf_op jit(solution)/shard_map/ppermute | solution.py:1259
  342.3 19.3 %collective-permute-start.45 = (bf16[256,1024]{1,0:T(8,128)(2,1)S(1)}, bf16[256,1024]{1,0:T(8,128)(2,1)S(1)}, u32[]{:S(2)}, u32[]{:S(2)}) collective-permute-start(bf16[256,1024]{1,0:T(8,128)(2,1)S(1)} %get-tuple-element.381), channel_id=1, source_target_pairs={{0,2},{2,0},{4,6},{6,4},{8,10},{10,8},{12,14},{14,12},{16,18},{18,... | collective-permute-start | bytes 1572872 | tf_op jit(solution)/shard_map/ppermute | solution.py:1259
  342.9 19.1 %collective-permute-start.43 = (bf16[128,2048]{1,0:T(8,128)(2,1)}, bf16[128,2048]{1,0:T(8,128)(2,1)S(1)}, u32[]{:S(2)}, u32[]{:S(2)}) collective-permute-start(bf16[128,2048]{1,0:T(8,128)(2,1)} %pad_maximum_fusion.2), channel_id=1, source_target_pairs={{0,8},{2,10},{4,12},{6,14},{8,0},{10,2},{12,4},{14,6},{16,24},{18,... | collective-permute-start | bytes 1572872 | tf_op jit(solution)/shard_map/ppermute | solution.py:1259
  364.5 41.1 %collective-permute-start.48 = (bf16[128,2048]{1,0:T(8,128)(2,1)S(1)}, bf16[128,2048]{1,0:T(8,128)(2,1)S(1)}, u32[]{:S(2)}, u32[]{:S(2)}) collective-permute-start(bf16[128,2048]{1,0:T(8,128)(2,1)S(1)} %pad_maximum_fusion.4), channel_id=1, source_target_pairs={{0,8},{2,10},{4,12},{6,14},{8,0},{10,2},{12,4},{14,6},{16,24},{18,... | collective-permute-start | bytes 1572872 | tf_op jit(solution)/shard_map/ppermute | solution.py:1259
  368.9 35.7 %collective-permute-start.47 = (bf16[64,2048]{1,0:T(8,128)(2,1)S(1)}, bf16[64,2048]{1,0:T(8,128)(2,1)S(1)}, u32[]{:S(2)}, u32[]{:S(2)}) collective-permute-start(bf16[64,2048]{1,0:T(8,128)(2,1)S(1)} %get-tuple-element.399), channel_id=1, source_target_pairs={{0,16},{2,18},{4,20},{6,22},{8,24},{10,26},{12,28},{14,30},{16,0},... | collective-permute-start | bytes 786440 | tf_op jit(solution)/shard_map/ppermute | solution.py:1259
  388.3 35.1 %collective-permute-start.49 = (bf16[512,1280]{1,0:T(8,128)(2,1)}, bf16[512,1280]{1,0:T(8,128)(2,1)S(1)}, u32[]{:S(2)}, u32[]{:S(2)}) collective-permute-start(bf16[512,1280]{1,0:T(8,128)(2,1)} %get-tuple-element.412), channel_id=1, source_target_pairs={{0,2},{2,0},{4,6},{6,4},{8,10},{10,8},{12,14},{14,12},{16,18},{18,... | collective-permute-start | bytes 3932168 | tf_op jit(solution)/shard_map/ppermute | solution.py:1259
  389.9 33.5 %collective-permute-start.50 = (bf16[512,1280]{1,0:T(8,128)(2,1)}, bf16[512,1280]{1,0:T(8,128)(2,1)S(1)}, u32[]{:S(2)}, u32[]{:S(2)}) collective-permute-start(bf16[512,1280]{1,0:T(8,128)(2,1)} %get-tuple-element.414), channel_id=1, source_target_pairs={{0,4},{2,6},{4,0},{6,2},{8,12},{10,14},{12,8},{14,10},{16,20},{18,... | collective-permute-start | bytes 3932168 | tf_op jit(solution)/shard_map/ppermute | solution.py:1259
  391.4 32.0 %collective-permute-start.51 = (bf16[512,1024]{1,0:T(8,128)(2,1)}, bf16[512,1024]{1,0:T(8,128)(2,1)S(1)}, u32[]{:S(2)}, u32[]{:S(2)}) collective-permute-start(bf16[512,1024]{1,0:T(8,128)(2,1)} %get-tuple-element.416), channel_id=1, source_target_pairs={{0,8},{2,10},{4,12},{6,14},{8,0},{10,2},{12,4},{14,6},{16,24},{18,... | collective-permute-start | bytes 3145736 | tf_op jit(solution)/shard_map/ppermute | solution.py:1259
  404.7 21.7 %collective-permute-start.52 = (bf16[512,2048]{1,0:T(8,128)(2,1)}, bf16[512,2048]{1,0:T(8,128)(2,1)}, u32[]{:S(2)}, u32[]{:S(2)}) collective-permute-start(bf16[512,2048]{1,0:T(8,128)(2,1)} %get-tuple-element.404.k1), channel_id=1, source_target_pairs={{0,1},{1,0},{2,3},{3,2},{4,5},{5,4},{6,7},{7,6},{8,9},{9,8},{10,11... | collective-permute-start | bytes 6291464 | tf_op jit(solution)/shard_map/ppermute | solution.py:1255
  405.6 17.7 %collective-permute-start.53 = (bf16[64,2048]{1,0:T(8,128)(2,1)S(1)}, bf16[64,2048]{1,0:T(8,128)(2,1)S(1)}, u32[]{:S(2)}, u32[]{:S(2)}) collective-permute-start(bf16[64,2048]{1,0:T(8,128)(2,1)S(1)} %get-tuple-element.425), channel_id=1, source_target_pairs={{0,16},{2,18},{4,20},{6,22},{8,24},{10,26},{12,28},{14,30},{16,0},... | collective-permute-start | bytes 786440 | tf_op jit(solution)/shard_map/ppermute | solution.py:1259
  426.3 18.0 %collective-permute-start.59 = (bf16[256,1024]{1,0:T(8,128)(2,1)}, bf16[256,1024]{1,0:T(8,128)(2,1)S(1)}, u32[]{:S(2)}, u32[]{:S(2)}) collective-permute-start(bf16[256,1024]{1,0:T(8,128)(2,1)} %get-tuple-element.453), channel_id=1, source_target_pairs={{0,2},{2,0},{4,6},{6,4},{8,10},{10,8},{12,14},{14,12},{16,18},{18,... | collective-permute-start | bytes 1572872 | tf_op jit(solution)/shard_map/ppermute | solution.py:1259
  426.9 19.1 %collective-permute-start.57 = (bf16[256,1280]{1,0:T(8,128)(2,1)S(1)}, bf16[256,1280]{1,0:T(8,128)(2,1)S(1)}, u32[]{:S(2)}, u32[]{:S(2)}) collective-permute-start(bf16[256,1280]{1,0:T(8,128)(2,1)S(1)} %get-tuple-element.451), channel_id=1, source_target_pairs={{0,8},{2,10},{4,12},{6,14},{8,0},{10,2},{12,4},{14,6},{16,24},{18,... | collective-permute-start | bytes 1966088 | tf_op jit(solution)/shard_map/ppermute | solution.py:1259
  431.2 17.7 %collective-permute-start.55 = (bf16[256,1280]{1,0:T(8,128)(2,1)S(1)}, bf16[256,1280]{1,0:T(8,128)(2,1)S(1)}, u32[]{:S(2)}, u32[]{:S(2)}) collective-permute-start(bf16[256,1280]{1,0:T(8,128)(2,1)S(1)} %get-tuple-element.449), channel_id=1, source_target_pairs={{0,4},{2,6},{4,0},{6,2},{8,12},{10,14},{12,8},{14,10},{16,20},{18,... | collective-permute-start | bytes 1966088 | tf_op jit(solution)/shard_map/ppermute | solution.py:1259
  442.7 18.5 %collective-permute-start.63 = (bf16[512,512]{1,0:T(8,128)(2,1)}, bf16[512,512]{1,0:T(8,128)(2,1)S(1)}, u32[]{:S(2)}, u32[]{:S(2)}) collective-permute-start(bf16[512,512]{1,0:T(8,128)(2,1)} %get-tuple-element.459), channel_id=1, source_target_pairs={{0,8},{2,10},{4,12},{6,14},{8,0},{10,2},{12,4},{14,6},{16,24},{18,... | collective-permute-start | bytes 1572872 | tf_op jit(solution)/shard_map/ppermute | solution.py:1259
  442.8 22.9 %collective-permute-start.62 = (bf16[512,768]{1,0:T(8,128)(2,1)}, bf16[512,768]{1,0:T(8,128)(2,1)S(1)}, u32[]{:S(2)}, u32[]{:S(2)}) collective-permute-start(bf16[512,768]{1,0:T(8,128)(2,1)} %get-tuple-element.457), channel_id=1, source_target_pairs={{0,4},{2,6},{4,0},{6,2},{8,12},{10,14},{12,8},{14,10},{16,20},{18,... | collective-permute-start | bytes 2359304 | tf_op jit(solution)/shard_map/ppermute | solution.py:1259
  444.4 21.4 %collective-permute-start.61 = (bf16[512,768]{1,0:T(8,128)(2,1)}, bf16[512,768]{1,0:T(8,128)(2,1)S(1)}, u32[]{:S(2)}, u32[]{:S(2)}) collective-permute-start(bf16[512,768]{1,0:T(8,128)(2,1)} %get-tuple-element.455), channel_id=1, source_target_pairs={{0,2},{2,0},{4,6},{6,4},{8,10},{10,8},{12,14},{14,12},{16,18},{18,... | collective-permute-start | bytes 2359304 | tf_op jit(solution)/shard_map/ppermute | solution.py:1259
  446.0 31.5 %collective-permute-start.64 = (f32[48,1024]{1,0:T(8,128)S(1)}, f32[48,1024]{1,0:T(8,128)S(1)}, u32[]{:S(2)}, u32[]{:S(2)}) collective-permute-start(f32[48,1024]{1,0:T(8,128)S(1)} %add.270), channel_id=1, source_target_pairs={{0,16},{2,18},{4,20},{6,22},{8,24},{10,26},{12,28},{14,30},{16,0},... | collective-permute-start | bytes 589832 | tf_op jit(solution)/shard_map/ppermute | solution.py:1259
  448.8 21.9 %collective-permute-start.60 = (bf16[128,1024]{1,0:T(8,128)(2,1)S(1)}, bf16[128,1024]{1,0:T(8,128)(2,1)S(1)}, u32[]{:S(2)}, u32[]{:S(2)}) collective-permute-start(bf16[128,1024]{1,0:T(8,128)(2,1)S(1)} %get-tuple-element.555), channel_id=1, source_target_pairs={{0,4},{2,6},{4,0},{6,2},{8,12},{10,14},{12,8},{14,10},{16,20},{18,... | collective-permute-start | bytes 786440 | tf_op jit(solution)/shard_map/ppermute | solution.py:1259
  476.8 20.8 %collective-permute-start.65 = (bf16[64,3584]{1,0:T(8,128)(2,1)S(1)}, bf16[64,3584]{1,0:T(8,128)(2,1)S(1)}, u32[]{:S(2)}, u32[]{:S(2)}) collective-permute-start(bf16[64,3584]{1,0:T(8,128)(2,1)S(1)} %pad_maximum_fusion.6), channel_id=1, source_target_pairs={{0,16},{2,18},{4,20},{6,22},{8,24},{10,26},{12,28},{14,30},{16,0},... | collective-permute-start | bytes 1376264 | tf_op jit(solution)/shard_map/ppermute | solution.py:1259
  477.6 22.2 %collective-permute-start.69 = (f32[48,1024]{1,0:T(8,128)S(1)}, f32[48,1024]{1,0:T(8,128)S(1)}, u32[]{:S(2)}, u32[]{:S(2)}) collective-permute-start(f32[48,1024]{1,0:T(8,128)S(1)} %add.283), channel_id=1, source_target_pairs={{0,2},{2,0},{4,6},{6,4},{8,10},{10,8},{12,14},{14,12},{16,18},{18,... | collective-permute-start | bytes 589832 | tf_op jit(solution)/shard_map/ppermute | solution.py:1259
  (71 other events, 743.3 us)

commit v2 on v1

--- a/solution.py
+++ b/solution.py
@@ -1460,13 +1460,16 @@
         False, inputs, (n1, x1, row(early_down_bias)), early_up_all[1], early_bias[1], early_down_all[1]
     )
     n2, kv = project(x1, row(attend_norm_gain), row(attend_norm_shift), key_all, value_all, value_bias_all)
+    kv, query_other = hold((kv, query_all[1]))
+    query_all = (query_weight, query_other)
     kvr = swap(kv)
     q = query(n2, query_all, query_bias_all)
     attend_all, gated_all = both(attend_weight), both(gated_weight)
-    q, attend_other, gated_other = hold((q, attend_all[1], gated_all[1]))
+    o, lse = attend(core, q, kv, kvr, table)
+    o, late_up, late_down, mixer_weight, attend_other, gated_other = hold(
+        (o, late_up, late_down, mixer_weight, attend_all[1], gated_all[1])
+    )
     attend_all, gated_all = (attend_weight, attend_other), (gated_weight, gated_other)
-    o, lse = attend(core, q, kv, kvr, table)
-    o, late_up, late_down, mixer_weight = hold((o, late_up, late_down, mixer_weight))
     mixer_all = both(mixer_weight)
     late_up_all, late_down_all = both(late_up), both(late_down)
     n1p, a1p, n2p = swap(n1), swap(a11), swap(n2)
@@ -1490,54 +1493,45 @@
     k40, k41, t40, t41, g3, d3, late_sums = feed_back(
         1.0, g4, d4, x3, row(late_norm_gain), late_up_all, late_down_all, (s40, s41)
     )
-    d3, d4p, n4p, a4p = hold((d3, d4p, n4p, a4p))
     k4p, d3p = swap(k41), swap(d3)
-    one = reduction([(d4, d4p)], [(0, (a40, a4p), (0, 0, 1, 1))])
-    (d3,) = hold((d3,), one)
-    one.send()
     bz, depth_sums, head = mixer_mid(d3, mixer_all, z, depth_gain_all, depth_shift_all)
     tail = lax.ppermute(head, "tensor", [(1, 0)])
-    k4p, d3p, bz = hold((k4p, d3p, bz))
-    two = reduction([(n4, n4p)], [(0, (k40, k4p), (0, 0, 1, 1))])
-    (bz,) = hold((bz,), two)
-    two.send()
+    bz, d4p, n4p, a4p, k4p, d3p = hold((bz, d4p, n4p, a4p, k4p, d3p))
+    one = reduction(
+        [(d4, d4p), (n4, n4p)], [(0, (a40, a4p), (2, 2, 2, 3)), (1, (k40, k4p), (3, 3, 4, 4))]
+    )
+    bz, tail = hold((bz, tail), one)
+    one.send()
     ka0, ka1, dkernel, g2, d2, do0, do1, mixer_sums = mixer_back(
         bz, tail, u, edge, kernel_all, sig, gated_all, x2, row(mixer_norm_gain), g3, attend_all
     )
     kap, d2p = swap(ka1), swap(d2)
-    one.add()
-    do0, kap, d2p = hold((do0, kap, d2p), one)
-    one.send()
     kq0, dk0, dv0, dkv0, dtable0 = attend_back(core, 0, q, do0, o, kv, kvr, table, lse)
+    kq0, kap, d2p = hold((kq0, kap, d2p), one)
     far1 = swap(dkv0)
-    one.add()
-    two.add()
     three = reduction(
         [(d3, d3p), (n3, n3p), (d2, d2p)],
         [(0, (w0, wp), (0,)), (1, (ka0, kap), (0, 1)), (2, (o, op), (1,))],
     )
-    do1, kq0, far1 = hold((do1, kq0, far1), one, two, three)
+    one.add()
+    do1, kq0, far1 = hold((do1, kq0, far1), one, three)
     one.send()
-    two.send()
     three.send()
     kq1, dk1, dv1, dkv1, dtable1 = attend_back(core, q.shape[1] // TILE // 2, q, do1, o, kv, kvr, table, lse)
+    kq1, dkv1 = hold((kq1, dkv1), one)
     far0, kqp = swap(dkv1), swap(kq1)
     one.add()
-    two.add()
-    three.add()
-    dk0, kq1 = hold((dk0, kq1), one, two, three)
+    dk0, far0 = hold((dk0, far0), one)
     one.send()
-    two.send()
-    three.send()
     kk0, kk1, g1, d1, attend_sums = project_back(
         (kq0, dk0, dv0, far0), (kq1, dk1, dv1, far1), query_all, key_all, value_all, x1, row(attend_norm_gain), g2
     )
     d1p, kkp = swap(d1), swap(kk1)
+    (g1,) = hold((g1,), one, three)
     one.add()
-    two.add()
     three.add()
-    d1p, kkp = hold((d1p, kkp), one, two, three)
-    two.send()
+    d1p, kkp = hold((d1p, kkp), one, three)
+    one.send()
     three.send()
     four = reduction(
         [(d1, d1p), (n2, n2p)],
@@ -1548,20 +1542,24 @@
         ],
         256,
     )
-    (d1,) = hold((d1,), four)
+    (d1,) = hold((d1,), four, one, three)
     four.send()
+    one.add()
+    three.add()
+    three.send()
     k10, k11, t10, t11 = feed_key(d1, early_down_all, (s10, s11))
     k1p = swap(k11)
-    two.add()
+    gradient, early_sums = feed_end(g1, d1, inputs, row(early_norm_gain), early_up_all, (k10, k11))
+    (early_sums,) = hold((early_sums,), four, three)
+    four.add()
     three.add()
-    (k10,) = hold((k10,), two, three)
+    n1, k1p = hold((n1, k1p), four, three)
+    four.send()
     three.send()
-    gradient, early_sums = feed_end(g1, d1, inputs, row(early_norm_gain), early_up_all, (k10, k11))
+    five = reduction([(n1, n1p)], [(0, (k10, k1p), (2, 2, 2, 3, 3, 3, 4, 4))], 256)
     three.add()
-    (early_sums,) = hold((early_sums,), four)
-    four.add()
-    early_sums, k1p = hold((early_sums, k1p), four, three)
-    four.send()
+    (early_sums,) = hold((early_sums,), five, three)
+    five.send()
     small_own, small_oth = pack(
         (
             late_sums, final_sums, mixer_sums, attend_sums, depth_sums, early_sums, dkernel,
@@ -1572,13 +1570,21 @@
     masks = [1 << bit for bit in (3, 0, 1, 2, *range(4, devices.bit_length() - 1))]
     if devices & (devices - 1) or devices < 16:
         masks = []
-    n1, small_oth = hold((n1, small_oth))
     moved = swap(small_oth)
-    five = reduction([(n1, n1p)], [(0, (k10, k1p), (2, 2, 2, 3, 3, 3, 4, 4))], 256)
-    first, moved = hold((first, moved), five)
-    five.send()
     for step in range(4):
         first = first + moved
+        if step == 2:
+            late_down_sum, late_up_sum = one.parts()
+            mixer_sum, gated_sum, attend_sum = three.parts()
+            gated_sum = jnp.stack([gated_sum[:, :half], gated_sum[:, half:]])
+            done = (late_down_sum.T, late_up_sum, mixer_sum.T, gated_sum, attend_sum.T)
+            first, *done = hold((first, *done))
+            late_down_sum, late_up_sum, mixer_sum, gated_sum, attend_sum = done
+        if step == 3:
+            early_down_sum, query_sum, project_sum = four.parts()
+            done = (early_down_sum.T, query_sum, project_sum[:, :half], project_sum[:, half:])
+            first, *done = hold((first, *done))
+            early_down_sum, query_sum, key_sum, value_sum = done
         moved = cross(first, devices, masks[step]) if masks else jnp.zeros_like(first)
         if step < 3:
             four.add()
@@ -1593,10 +1599,6 @@
         first = first + cross(first, devices, mask)
     if not masks:
         first = lax.psum(first, "dp")
-    (late_down_sum,) = one.parts()
-    (late_up_sum,) = two.parts()
-    mixer_sum, gated_sum, attend_sum = three.parts()
-    early_down_sum, query_sum, project_sum = four.parts()
     (early_up_sum,) = five.parts()
 
     table_out = jnp.concatenate(
@@ -1616,30 +1618,30 @@
         early_rows[1],
         early_up_sum,
         early_up_bias_sum,
-        early_down_sum.T,
+        early_down_sum,
         early_rows[2],
         first[8],
         first[9],
         query_sum,
         pile_sum[0],
-        project_sum[:, :half],
-        project_sum[:, half:],
+        key_sum,
+        value_sum,
         pile_sum[1],
         table_out,
-        attend_sum.T,
+        attend_sum,
         first[7],
         first[5],
         first[6],
-        jnp.stack([gated_sum[:, :half], gated_sum[:, half:]]),
+        gated_sum,
         pile_sum[4:],
         pile_sum[2],
         pile_sum[3],
-        mixer_sum.T,
+        mixer_sum,
         first[0],
         first[1],
         late_up_sum,
         late_up_bias_sum,
-        late_down_sum.T,
+        late_down_sum,
         first[2],
         first[3],
         first[4],

time: 533 us -> 522 us (0.979)
  waiting for transfers between devices: 66.2 us -> 56.7 us
    ppermute x42 -> x40, waiting for transfers between devices: 56.4 us -> 51.1 us  [cross(): return lax.ppermute(values, 'dp', [(i, i ^ mask) for i in range(devices)])]
    ppermute x42 -> x40, starting transfers between devices: 44.8 us -> 47.7 us  [cross(): return lax.ppermute(values, 'dp', [(i, i ^ mask) for i in range(devices)])]
    pallas_call x24 -> x23, Pallas kernels: 357 us -> 355 us  [launch(): pl.pallas_call(body, grid_spec=pltpu.PrefetchScalarGridSpec(num_scalar_pr...]
    add x33 -> x32, other arithmetic: 10.8 us -> 12.1 us  [add(): stay = [one[half:] + two[half:] for one, two in zip(arrived, kept)]]
    unnamed x91 -> x83, local copies, waits for them, and re-layouts: 12 us -> 11.2 us
  transfers between devices with their start and end apart: 76 -> 74, of which waited for: 18 -> 18; matrix products, arithmetic and copies ran while one was open for 4% -> 5% of each run, Pallas kernels for 62% -> 64%
where the time goes in v2:
time: 522 us; the launch traced here: 512 us
  Pallas kernels  355 us (68%)
  starting transfers between devices  59.2 us (11%)
  waiting for transfers between devices  56.7 us (11%)
  other arithmetic  20.8 us (4%)
  local copies, waits for them, and re-layouts  17.2 us (3%)
    pallas_call x23, Pallas kernels, launch(): pl.pallas_call(body, grid_spec=pltpu.PrefetchScalarGridSpec(num_scalar_pr...  355 us
    ppermute x40, waiting for transfers between devices, cross(): return lax.ppermute(values, 'dp', [(i, i ^ mask) for i in range(devices)])  51.1 us
    ppermute x40, starting transfers between devices, cross(): return lax.ppermute(values, 'dp', [(i, i ^ mask) for i in range(devices)])  47.7 us
    add x32, other arithmetic, add(): stay = [one[half:] + two[half:] for one, two in zip(arrived, kept)]  12.1 us
    unnamed x83, local copies, waits for them, and re-layouts  11.2 us
  transfers between devices with their start and end apart: 74, of which 18 were waited for; matrix products, arithmetic and copies ran while one was open for 5% of the time, Pallas kernels for 64%

profile of v2, /device:TPU:0, one launch (start us, length us, event | category | flops | bytes accessed | tf_op | source)
XLA Modules:
  0.0 511.8 jit_solution(3688361764582605957)
XLA Ops:
  1.3 1.7 gather.1
  3.9 12.9 %feed_half.2 = (bf16[512,1024]{1,0:T(8,128)(2,1)}, bf16[512,2048]{1,0:T(8,128)(2,1)}, bf16[512,2048]{1,0:T(8,128)(2,1)}, f32[512,1024]{1,0:T(8,128)}) custom-call(bf16[512,1024]{1,0:T(8,128)(2,1)} %x.5, f32[1,1024]{1,0:T(1,128)} %bitcast.82, f32[1,1024]{1,0:T(1,128)} %bitcast.103, bf16[1024,2048]{1,0:T(8,128)(2,1)} %up0.3, f32[1,2048]{1,0:T(1,128)} %bitcast.73, ...), custom_call_target="tpu_custom_call" | custom-call | flops 4294967296 | bytes 16793600 | tf_op jit(solution)/shard_map/feed_half/pallas_call | solution.py:54
  18.3 2.0 copy-done.2
  20.3 12.0 %feed_half.3 = (bf16[512,2048]{1,0:T(8,128)(2,1)}, bf16[512,2048]{1,0:T(8,128)(2,1)}, f32[512,1024]{1,0:T(8,128)}) custom-call(bf16[512,1024]{1,0:T(8,128)(2,1)} %x.5, bf16[512,1024]{1,0:T(8,128)(2,1)} %get-tuple-element.476.refs_0_, f32[512,1024]{1,0:T(8,128)} %get-tuple-element.293.refs_1_, f32[1,1024]{1,0:T(1,128)} %bitcast.104, ...), custom_call_target="tpu_custom_call" | custom-call | flops 4294967296 | bytes 18886656 | tf_op jit(solution)/shard_map/feed_half/pallas_call | solution.py:54
  32.4 8.4 %project.1 = (bf16[512,1024]{1,0:T(8,128)(2,1)}, bf16[512,2048]{1,0:T(8,128)(2,1)}) custom-call(f32[512,1024]{1,0:T(8,128)} %get-tuple-element.294.x, f32[1,1024]{1,0:T(1,128)} %bitcast.80, f32[1,1024]{1,0:T(1,128)} %bitcast.105, bf16[1024,512]{1,0:T(8,128)(2,1)} %kw0.3, bf16[1024,512]{1,0:T(8,128)(2,1)} %collective-permute-done.3.kw1, ...), custom_call_target="tpu_custom_call" | custom-call | flops 2147483648 | bytes 9449472 | tf_op jit(solution)/shard_map/project/pallas_call | solution.py:54
  43.2 4.0 query.1.q
  48.6 35.3 %attend.1 = (bf16[2,512,512]{2,1,0:T(8,128)(2,1)}, f32[64,512]{1,0:T(8,128)}) custom-call(s32[1]{0:T(128)} %bitcast.core, bf16[512,1024]{1,0:T(8,128)(2,1)} %query.1.q, bf16[512,2048]{1,0:T(8,128)(2,1)} %get-tuple-element.298.k0.v0, bf16[512,2048]{1,0:T(8,128)(2,1)} %get-tuple-element.298.k0.v0, bf16[512,2048]{1,0:T(8,128)(2,1)} %copy-done, ...), custom_call_target="tpu_custom_call" | custom-call | flops 2147483648 | bytes 10649600 | tf_op jit(solution)/shard_map/attend/pallas_call | solution.py:54
  85.0 12.4 %mixer_in.1 = (f32[512,1024]{1,0:T(8,128)}, bf16[512,1024]{1,0:T(8,128)(2,1)}, f32[512,1024]{1,0:T(8,128)}, f32[512,1024]{1,0:T(8,128)}, f32[32,1024]{1,0:T(8,128)}) custom-call(bf16[2,512,512]{2,1,0:T(8,128)(2,1)} %get-tuple-element.300.o0.o1.o.refs_10_, bf16[2,512,512]{2,1,0:T(8,128)(2,1)} %get-tuple-element.300.o0.o1.o.refs_10_, ...), custom_call_target="tpu_custom_call" | custom-call | flops 3221225472 | bytes 22163456 | tf_op jit(solution)/shard_map/mixer_in/pallas_call | solution.py:54
  98.9 2.2 collective-permute-start.9
  101.1 2.0 collective-permute-done.9.edge
  106.7 13.9 %mixer_out.1 = (f32[512,1024]{1,0:T(8,128)}, bf16[512,512]{1,0:T(8,128)(2,1)}, bf16[512,512]{1,0:T(8,128)(2,1)}, f32[512,1024]{1,0:T(8,128)}) custom-call(f32[512,1024]{1,0:T(8,128)} %get-tuple-element.303.u, f32[32,1024]{1,0:T(8,128)} %copy-done.19, f32[32,1024]{1,0:T(8,128)} %pad_maximum_fusion.9.kernel, f32[1,1024]{1,0:T(1,128)} %get-tuple-element.693.gain, ...), custom_call_target="tpu_custom_call" | custom-call | flops 1073741824 | bytes 11804672 | tf_op jit(solution)/shard_map/mixer_out/pallas_call | solution.py:54
  121.2 20.8 %feed_forward.1 = (bf16[512,1024]{1,0:T(8,128)(2,1)}, bf16[512,2048]{1,0:T(8,128)(2,1)}, bf16[512,2048]{1,0:T(8,128)(2,1)}, bf16[512,2048]{1,0:T(8,128)(2,1)}, b...) custom-call(f32[512,1024]{1,0:T(8,128)} %get-tuple-element.309.x, f32[1,1024]{1,0:T(1,128)} %bitcast.108, ...), custom_call_target="tpu_custom_call" | custom-call | flops 8589934592 | bytes 30437376 | tf_op jit(solution)/shard_map/feed_forward/pallas_call | solution.py:54
  142.1 5.6 %final_norm.1 = (bf16[512,1024]{1,0:T(8,128)(2,1)}, f32[512,1024]{1,0:T(8,128)}, bf16[512,1024]{1,0:T(8,128)(2,1)}, f32[16,1024]{1,0:T(8,128)}) custom-call(s32[1]{0:T(128)S(6)} %copy.75.flag, f32[512,1024]{1,0:T(8,128)} %get-tuple-element.315.x, bf16[512,1024]{1,0:T(8,128)(2,1)} %cotangent.1, f32[1,1024]{1,0:T(1,128)} %bitcast.78, f32[1,1024]{1,0:T(1,128)} %bitcast.79), custom_call_target="tpu_custom_call" | custom-call | bytes 7413760 | tf_op jit(solution)/shard_map/final_norm/pallas_call | solution.py:54
  147.6 22.1 %feed_back.1 = (bf16[512,2048]{1,0:T(8,128)(2,1)}, bf16[512,2048]{1,0:T(8,128)(2,1)}, f32[8,2048]{1,0:T(8,128)}, f32[8,2048]{1,0:T(8,128)}, f32[512,1024]{1,0:T(...) custom-call(f32[512,1024]{1,0:T(8,128)} %get-tuple-element.317.g, bf16[512,1024]{1,0:T(8,128)(2,1)} %get-tuple-element.318.d.refs_0_, ...), custom_call_target="tpu_custom_call" | custom-call | flops 8589934592 | bytes 33787904 | tf_op jit(solution)/shard_map/feed_back/pallas_call | solution.py:54
  171.1 8.8 %mixer_mid.1 = (f32[512,1024]{1,0:T(8,128)}, f32[16,1024]{1,0:T(8,128)}, f32[32,1024]{1,0:T(8,128)}) custom-call(bf16[512,1024]{1,0:T(8,128)(2,1)} %get-tuple-element.321.d.refs_0_, bf16[512,1024]{1,0:T(8,128)(2,1)} %out0.4, bf16[512,1024]{1,0:T(8,128)(2,1)} %copy-done.5, f32[512,1024]{1,0:T(8,128)} %get-tuple-element.322.z, ...), custom_call_target="tpu_custom_call" | custom-call | flops 1073741824 | bytes 7544832 | tf_op jit(solution)/shard_map/mixer_mid/pallas_call | solution.py:54
  181.8 17.3 %weight_gradient.4 = (bf16[512,1536]{1,0:T(8,128)(2,1)}, bf16[512,1536]{1,0:T(8,128)(2,1)}, bf16[512,1536]{1,0:T(8,128)(2,1)}, bf16[512,1536]{1,0:T(8,128)(2,1)}...) custom-call(s32[1]{0:T(128)} %bitcast.21.me, bf16[512,1024]{1,0:T(8,128)(2,1)} %get-tuple-element.318.d.refs_0_, ...), custom_call_target="tpu_custom_call" | custom-call | flops 8589934592 | bytes 20971520 | tf_op jit(solution)/shard_map/weight_gradient/pallas_call | solution.py:54
  199.2 3.0 collective-permute-start.27
  203.7 24.6 %mixer_back.1 = (bf16[2,512,512]{2,1,0:T(8,128)(2,1)}, bf16[2,512,512]{2,1,0:T(8,128)(2,1)}, f32[32,1024]{1,0:T(8,128)}, f32[512,1024]{1,0:T(8,128)}, bf16[512,1...) custom-call(f32[512,1024]{1,0:T(8,128)} %get-tuple-element.341.bz, ...), custom_call_target="tpu_custom_call" | custom-call | flops 3221225472 | bytes 27889664 | tf_op jit(solution)/shard_map/mixer_back/pallas_call | solution.py:54
  228.8 1.6 collective-permute-start.29
  230.4 34.3 %attend_back.2 = (bf16[512,512]{1,0:T(8,128)(2,1)}, f32[512,512]{1,0:T(8,128)}, f32[512,512]{1,0:T(8,128)}, bf16[2,512,512]{2,1,0:T(8,128)(2,1)}, f32[128,128]{1,0:T(8,128)}) custom-call(s32[1]{0:T(128)} %bitcast.core, bf16[512,1024]{1,0:T(8,128)(2,1)} %query.1.q, bf16[512,512]{1,0:T(8,128)(2,1)} %get-tuple-element.346.do, ...), custom_call_target="tpu_custom_call" | custom-call | flops 2684354560 | bytes 14909440 | tf_op jit(solution)/shard_map/attend_back/pallas_call | solution.py:54
  266.9 12.4 %weight_gradient.5 = (bf16[512,1024]{1,0:T(8,128)(2,1)}, bf16[512,1024]{1,0:T(8,128)(2,1)}, bf16[512,1024]{1,0:T(8,128)(2,1)}, bf16[512,1024]{1,0:T(8,128)(2,1)}) custom-call(s32[1]{0:T(128)} %bitcast.21.me, bf16[512,1024]{1,0:T(8,128)(2,1)} %get-tuple-element.321.d.refs_0_, bf16[512,1024]{1,0:T(8,128)(2,1)} %copy-done.32, ...), custom_call_target="tpu_custom_call" | custom-call | flops 4294967296 | bytes 15204352 | tf_op jit(solution)/shard_map/weight_gradient/pallas_call | solution.py:54
  279.3 2.6 slice_add_fusion
  286.6 34.1 %attend_back.3 = (bf16[512,512]{1,0:T(8,128)(2,1)}, f32[512,512]{1,0:T(8,128)}, f32[512,512]{1,0:T(8,128)}, bf16[2,512,512]{2,1,0:T(8,128)(2,1)}, f32[128,128]{1,0:T(8,128)}) custom-call(s32[1]{0:T(128)} %bitcast.core, bf16[512,1024]{1,0:T(8,128)(2,1)} %query.1.q, bf16[512,512]{1,0:T(8,128)(2,1)} %get-tuple-element.379.do, ...), custom_call_target="tpu_custom_call" | custom-call | flops 2684354560 | bytes 14909440 | tf_op jit(solution)/shard_map/attend_back/pallas_call | solution.py:54
  320.8 1.9 slice_add_fusion.20
  325.1 1.6 collective-permute-start.35
  327.8 14.2 %project_back.1 = (bf16[2,512,512]{2,1,0:T(8,128)(2,1)}, bf16[2,512,512]{2,1,0:T(8,128)(2,1)}, f32[512,1024]{1,0:T(8,128)}, bf16[512,1024]{1,0:T(8,128)(2,1)}, f32[32,1024]{1,0:T(8,128)}) custom-call(bf16[512,512]{1,0:T(8,128)(2,1)} %get-tuple-element.377.kq0.refs_6_, f32[512,512]{1,0:T(8,128)} %get-tuple-element.395.dk0, ...), custom_call_target="tpu_custom_call" | custom-call | flops 3221225472 | bytes 23203840 | tf_op jit(solution)/shard_map/project_back/pallas_call | solution.py:54
  347.2 2.6 collective-permute-start.43
  353.6 19.4 %weight_gradient.6 = (bf16[512,1280]{1,0:T(8,128)(2,1)}, bf16[512,1280]{1,0:T(8,128)(2,1)}, bf16[512,1280]{1,0:T(8,128)(2,1)}, bf16[512,1280]{1,0:T(8,128)(2,1)}...) custom-call(s32[1]{0:T(128)} %bitcast.21.me, bf16[512,1024]{1,0:T(8,128)(2,1)} %get-tuple-element.445.refs_0_.d, ...), custom_call_target="tpu_custom_call" | custom-call | flops 7516192768 | bytes 18874368 | tf_op jit(solution)/shard_map/weight_gradient/pallas_call | solution.py:54
  377.2 2.0 collective-permute-start.48
  379.2 12.3 %feed_key.1 = (bf16[512,2048]{1,0:T(8,128)(2,1)}, bf16[512,2048]{1,0:T(8,128)(2,1)}, f32[8,2048]{1,0:T(8,128)}, f32[8,2048]{1,0:T(8,128)}) custom-call(bf16[512,1024]{1,0:T(8,128)(2,1)} %get-tuple-element.445.refs_0_.d, bf16[2048,1024]{1,0:T(8,128)(2,1)} %down0.3, bf16[2048,1024]{1,0:T(8,128)(2,1)} %collective-permute-done.2.refs_5_.down1, ...), custom_call_target="tpu_custom_call" | custom-call | flops 4294967296 | bytes 17956864 | tf_op jit(solution)/shard_map/feed_key/pallas_call | solution.py:54
  392.8 15.6 %feed_end.1 = (f32[512,1024]{1,0:T(8,128)}, f32[24,1024]{1,0:T(8,128)}) custom-call(f32[512,1024]{1,0:T(8,128)} %get-tuple-element.414.g, bf16[512,1024]{1,0:T(8,128)(2,1)} %get-tuple-element.445.refs_0_.d, bf16[512,1024]{1,0:T(8,128)(2,1)} %x.5, f32[1,1024]{1,0:T(1,128)} %bitcast.83, bf16[1024,2048]{1,0:T(8,128)(2,1)} %up0.3, bf16[1024,2048]{1,0:T(8,128)(2,1)} %copy-done.2, ...), custom_call_target="tpu_custom_call" | custom-call | flops 4294967296 | bytes 18976768 | tf_op jit(solution)/shard_map/feed_end/pallas_call | solution.py:54
  408.4 2.3 collective-permute-done.48
  416.1 1.7 collective-permute-start.55
  419.4 10.9 %weight_gradient.7 = (bf16[512,768]{1,0:T(8,128)(2,1)}, bf16[512,768]{1,0:T(8,128)(2,1)}, bf16[512,768]{1,0:T(8,128)(2,1)}, bf16[512,768]{1,0:T(8,128)(2,1)}, bf...) custom-call(s32[1]{0:T(128)} %bitcast.21.me, bf16[512,1024]{1,0:T(8,128)(2,1)} %get-tuple-element.476.refs_0_, ...), custom_call_target="tpu_custom_call" | custom-call | flops 4294967296 | bytes 10485760 | tf_op jit(solution)/shard_map/weight_gradient/pallas_call | solution.py:54
  430.7 2.2 pack.1
  440.2 1.6 collective-permute-start.58
  441.8 10.3 %collective-permute-done.61 = bf16[512,512]{1,0:T(8,128)(2,1)S(1)} collective-permute-done((bf16[512,512]{1,0:T(8,128)(2,1)}, bf16[512,512]{1,0:T(8,128)(2,1)S(1)}, u32[]{:S(2)}, u32[]{:S(2)}) %collective-permute-start.61) | collective-permute-done | bytes 524320 | tf_op jit(solution)/shard_map/ppermute | solution.py:1259
  452.8 2.3 collective-permute-done.60
  455.2 1.7 collective-permute-start.54
  457.1 3.0 collective-permute-done.58
  460.2 2.5 collective-permute-done.56
  464.1 1.7 collective-permute-start.65
  469.1 2.8 collective-permute-done.66
  471.9 7.6 %collective-permute-done.65 = bf16[256,768]{1,0:T(8,128)(2,1)S(1)} collective-permute-done((bf16[256,768]{1,0:T(8,128)(2,1)S(1)}, bf16[256,768]{1,0:T(8,128)(2,1)S(1)}, u32[]{:S(2)}, u32[]{:S(2)}) %collective-permute-start.65) | collective-permute-done | bytes 393248 | tf_op jit(solution)/shard_map/ppermute | solution.py:1259
  479.6 8.6 %collective-permute-done.63 = bf16[64,3584]{1,0:T(8,128)(2,1)S(1)} collective-permute-done((bf16[64,3584]{1,0:T(8,128)(2,1)S(1)}, bf16[64,3584]{1,0:T(8,128)(2,1)S(1)}, u32[]{:S(2)}, u32[]{:S(2)}) %collective-permute-start.63) | collective-permute-done | bytes 458784 | tf_op jit(solution)/shard_map/ppermute | solution.py:1259
  491.9 2.8 collective-permute-done.70
  494.8 2.6 collective-permute-start.72
  499.6 6.2 %collective-permute-done.72 = bf16[64,2048]{1,0:T(8,128)(2,1)S(1)} collective-permute-done((bf16[64,2048]{1,0:T(8,128)(2,1)S(1)}, bf16[64,2048]{1,0:T(8,128)(2,1)S(1)}, u32[]{:S(2)}, u32[]{:S(2)}) %collective-permute-start.72) | collective-permute-done | bytes 262176 | tf_op jit(solution)/shard_map/ppermute | solution.py:1259
  (281 shorter events, 74.6 us)
Async XLA Ops:
  0.7 17.6 %collective-permute-start = (bf16[1024,2048]{1,0:T(8,128)(2,1)}, bf16[1024,2048]{1,0:T(8,128)(2,1)S(1)}, u32[]{:S(2)}, u32[]{:S(2)}) collective-permute-start(bf16[1024,2048]{1,0:T(8,128)(2,1)} %up0.3), channel_id=1, source_target_pairs={{0,1},{1,0},{2,3},{3,2},{4,5},{5,4},{6,7},{7,6},{8,9},{9,8},{10,11... | collective-permute-start | bytes 12582920 | tf_op jit(solution)/shard_map/ppermute | solution.py:1255
  1.2 17.0 %collective-permute-start.2 = (bf16[2048,1024]{1,0:T(8,128)(2,1)}, bf16[2048,1024]{1,0:T(8,128)(2,1)}, u32[]{:S(2)}, u32[]{:S(2)}) collective-permute-start(bf16[2048,1024]{1,0:T(8,128)(2,1)} %down0.3), channel_id=1, source_target_pairs={{0,1},{1,0},{2,3},{3,2},{4,5},{5,4},{6,7},{7,6},{8,9},{9,8},{10,11... | collective-permute-start | bytes 12582920 | tf_op jit(solution)/shard_map/ppermute | solution.py:1255
  3.4 28.9 %collective-permute-start.3 = (bf16[1024,512]{1,0:T(8,128)(2,1)}, bf16[1024,512]{1,0:T(8,128)(2,1)}, u32[]{:S(2)}, u32[]{:S(2)}) collective-permute-start(bf16[1024,512]{1,0:T(8,128)(2,1)} %kw0.3), channel_id=1, source_target_pairs={{0,1},{1,0},{2,3},{3,2},{4,5},{5,4},{6,7},{7,6},{8,9},{9,8},{10,11... | collective-permute-start | bytes 3145736 | tf_op jit(solution)/shard_map/ppermute | solution.py:1255
  3.5 28.9 %collective-permute-start.4 = (bf16[1024,512]{1,0:T(8,128)(2,1)}, bf16[1024,512]{1,0:T(8,128)(2,1)}, u32[]{:S(2)}, u32[]{:S(2)}) collective-permute-start(bf16[1024,512]{1,0:T(8,128)(2,1)} %vw0.3), channel_id=1, source_target_pairs={{0,1},{1,0},{2,3},{3,2},{4,5},{5,4},{6,7},{7,6},{8,9},{9,8},{10,11... | collective-permute-start | bytes 3145736 | tf_op jit(solution)/shard_map/ppermute | solution.py:1255
  16.9 23.9 %collective-permute-start.5 = (bf16[1024,512]{1,0:T(8,128)(2,1)S(1)}, bf16[1024,512]{1,0:T(8,128)(2,1)}, u32[]{:S(2)}, u32[]{:S(2)}) collective-permute-start(bf16[1024,512]{1,0:T(8,128)(2,1)S(1)} %copy-done.4), channel_id=1, source_target_pairs={{0,1},{1,0},{2,3},{3,2},{4,5},{5,4},{6,7},{7,6},{8,9},{9,8},{10,11... | collective-permute-start | bytes 3145736 | tf_op jit(solution)/shard_map/ppermute | solution.py:1255
  41.3 42.6 %collective-permute-start.8 = (bf16[2,1024,512]{2,1,0:T(8,128)(2,1)}, bf16[2,1024,512]{2,1,0:T(8,128)(2,1)}, u32[]{:S(2)}, u32[]{:S(2)}) collective-permute-start(bf16[2,1024,512]{2,1,0:T(8,128)(2,1)} %gate0.3), channel_id=1, source_target_pairs={{0,1},{1,0},{2,3},{3,2},{4,5},{5,4},{6,7},{7,6},{8,9},{9,8},{10,11... | collective-permute-start | bytes 6291464 | tf_op jit(solution)/shard_map/ppermute | solution.py:1255
  41.3 42.5 %collective-permute-start.7 = (bf16[512,1024]{1,0:T(8,128)(2,1)}, bf16[512,1024]{1,0:T(8,128)(2,1)}, u32[]{:S(2)}, u32[]{:S(2)}) collective-permute-start(bf16[512,1024]{1,0:T(8,128)(2,1)} %out0.5), channel_id=1, source_target_pairs={{0,1},{1,0},{2,3},{3,2},{4,5},{5,4},{6,7},{7,6},{8,9},{9,8},{10,11... | collective-permute-start | bytes 3145736 | tf_op jit(solution)/shard_map/ppermute | solution.py:1255
  83.8 37.4 %collective-permute-start.14 = (bf16[1024,2048]{1,0:T(8,128)(2,1)}, bf16[1024,2048]{1,0:T(8,128)(2,1)}, u32[]{:S(2)}, u32[]{:S(2)}) collective-permute-start(bf16[1024,2048]{1,0:T(8,128)(2,1)} %up0.2), channel_id=1, source_target_pairs={{0,1},{1,0},{2,3},{3,2},{4,5},{5,4},{6,7},{7,6},{8,9},{9,8},{10,11... | collective-permute-start | bytes 12582920 | tf_op jit(solution)/shard_map/ppermute | solution.py:1255
  84.0 37.3 %collective-permute-start.15 = (bf16[2048,1024]{1,0:T(8,128)(2,1)}, bf16[2048,1024]{1,0:T(8,128)(2,1)}, u32[]{:S(2)}, u32[]{:S(2)}) collective-permute-start(bf16[2048,1024]{1,0:T(8,128)(2,1)} %down0.2), channel_id=1, source_target_pairs={{0,1},{1,0},{2,3},{3,2},{4,5},{5,4},{6,7},{7,6},{8,9},{9,8},{10,11... | collective-permute-start | bytes 12582920 | tf_op jit(solution)/shard_map/ppermute | solution.py:1255
  84.5 36.5 %collective-permute-start.12 = (bf16[512,2048]{1,0:T(8,128)(2,1)}, bf16[512,2048]{1,0:T(8,128)(2,1)}, u32[]{:S(2)}, u32[]{:S(2)}) collective-permute-start(bf16[512,2048]{1,0:T(8,128)(2,1)} %get-tuple-element.308), channel_id=1, source_target_pairs={{0,1},{1,0},{2,3},{3,2},{4,5},{5,4},{6,7},{7,6},{8,9},{9,8},{10,11... | collective-permute-start | bytes 6291464 | tf_op jit(solution)/shard_map/ppermute | solution.py:1255
  84.9 20.1 %collective-permute-start.10 = (bf16[512,1024]{1,0:T(8,128)(2,1)S(1)}, bf16[512,1024]{1,0:T(8,128)(2,1)S(1)}, u32[]{:S(2)}, u32[]{:S(2)}) collective-permute-start(bf16[512,1024]{1,0:T(8,128)(2,1)S(1)} %copy-done.3), channel_id=1, source_target_pairs={{0,1},{1,0},{2,3},{3,2},{4,5},{5,4},{6,7},{7,6},{8,9},{9,8},{10,11... | collective-permute-start | bytes 3145736 | tf_op jit(solution)/shard_map/ppermute | solution.py:1255
  103.2 17.5 %collective-permute-start.13 = (bf16[512,1024]{1,0:T(8,128)(2,1)S(1)}, bf16[512,1024]{1,0:T(8,128)(2,1)}, u32[]{:S(2)}, u32[]{:S(2)}) collective-permute-start(bf16[512,1024]{1,0:T(8,128)(2,1)S(1)} %copy-done.11), channel_id=1, source_target_pairs={{0,1},{1,0},{2,3},{3,2},{4,5},{5,4},{6,7},{7,6},{8,9},{9,8},{10,11... | collective-permute-start | bytes 3145736 | tf_op jit(solution)/shard_map/ppermute | solution.py:1255
  105.0 37.0 %collective-permute-start.17 = (bf16[512,1024]{1,0:T(8,128)(2,1)}, bf16[512,1024]{1,0:T(8,128)(2,1)}, u32[]{:S(2)}, u32[]{:S(2)}) collective-permute-start(bf16[512,1024]{1,0:T(8,128)(2,1)} %get-tuple-element.313.refs_2_), channel_id=1, source_target_pairs={{0,1},{1,0},{2,3},{3,2},{4,5},{5,4},{6,7},{7,6},{8,9},{9,8},{10,11... | collective-permute-start | bytes 3145736 | tf_op jit(solution)/shard_map/ppermute | solution.py:1255
  120.6 21.4 %collective-permute-start.16 = (bf16[1,512,512]{2,1,0:T(8,128)(2,1)S(1)}, bf16[1,512,512]{2,1,0:T(8,128)(2,1)S(1)}, u32[]{:S(2)}, u32[]{:S(2)}) collective-permute-start(bf16[1,512,512]{2,1,0:T(8,128)(2,1)S(1)} %slice.597), channel_id=1, source_target_pairs={{0,1},{1,0},{2,3},{3,2},{4,5},{5,4},{6,7},{7,6},{8,9},{9,8},{10,11... | collective-permute-start | bytes 1572872 | tf_op jit(solution)/shard_map/ppermute | solution.py:1255
  121.0 21.1 %collective-permute-start.18 = (bf16[512,512]{1,0:T(8,128)(2,1)}, bf16[512,512]{1,0:T(8,128)(2,1)S(1)}, u32[]{:S(2)}, u32[]{:S(2)}) collective-permute-start(bf16[512,512]{1,0:T(8,128)(2,1)} %get-tuple-element.314), channel_id=1, source_target_pairs={{0,1},{1,0},{2,3},{3,2},{4,5},{5,4},{6,7},{7,6},{8,9},{9,8},{10,11... | collective-permute-start | bytes 1572872 | tf_op jit(solution)/shard_map/ppermute | solution.py:1255
  179.9 19.2 %collective-permute-start.24 = (f32[32,1024]{1,0:T(8,128)}, f32[32,1024]{1,0:T(8,128)S(1)}, u32[]{:S(2)}, u32[]{:S(2)}) collective-permute-start(f32[32,1024]{1,0:T(8,128)} %get-tuple-element.328), channel_id=1, source_target_pairs={{1,0},{3,2},{5,4},{7,6},{9,8},{11,10},{13,12},{15,14},{17,16},{19,... | collective-permute-start | bytes 393224 | tf_op jit(solution)/shard_map/ppermute | solution.py:1498
  199.2 65.6 %collective-permute-start.27 = (bf16[512,1536]{1,0:T(8,128)(2,1)}, bf16[512,1536]{1,0:T(8,128)(2,1)S(1)}, u32[]{:S(2)}, u32[]{:S(2)}) collective-permute-start(bf16[512,1536]{1,0:T(8,128)(2,1)} %get-tuple-element.351), channel_id=1, source_target_pairs={{0,2},{2,0},{4,6},{6,4},{8,10},{10,8},{12,14},{14,12},{16,18},{18,... | collective-permute-start | bytes 4718600 | tf_op jit(solution)/shard_map/ppermute | solution.py:1259
  202.1 62.7 %collective-permute-start.28 = (bf16[512,1536]{1,0:T(8,128)(2,1)}, bf16[512,1536]{1,0:T(8,128)(2,1)S(1)}, u32[]{:S(2)}, u32[]{:S(2)}) collective-permute-start(bf16[512,1536]{1,0:T(8,128)(2,1)} %get-tuple-element.353), channel_id=1, source_target_pairs={{0,4},{2,6},{4,0},{6,2},{8,12},{10,14},{12,8},{14,10},{16,20},{18,... | collective-permute-start | bytes 4718600 | tf_op jit(solution)/shard_map/ppermute | solution.py:1259
  228.2 36.5 %collective-permute-start.25 = (bf16[2,512,512]{2,1,0:T(8,128)(2,1)}, bf16[2,512,512]{2,1,0:T(8,128)(2,1)}, u32[]{:S(2)}, u32[]{:S(2)}) collective-permute-start(bf16[2,512,512]{2,1,0:T(8,128)(2,1)} %get-tuple-element.349), channel_id=1, source_target_pairs={{0,1},{1,0},{2,3},{3,2},{4,5},{5,4},{6,7},{7,6},{8,9},{9,8},{10,11... | collective-permute-start | bytes 3145736 | tf_op jit(solution)/shard_map/ppermute | solution.py:1255
  228.5 36.3 %collective-permute-start.26 = (bf16[512,1024]{1,0:T(8,128)(2,1)}, bf16[512,1024]{1,0:T(8,128)(2,1)}, u32[]{:S(2)}, u32[]{:S(2)}) collective-permute-start(bf16[512,1024]{1,0:T(8,128)(2,1)} %get-tuple-element.350.refs_4_), channel_id=1, source_target_pairs={{0,1},{1,0},{2,3},{3,2},{4,5},{5,4},{6,7},{7,6},{8,9},{9,8},{10,11... | collective-permute-start | bytes 3145736 | tf_op jit(solution)/shard_map/ppermute | solution.py:1255
  228.8 36.0 %collective-permute-start.29 = (bf16[512,1024]{1,0:T(8,128)(2,1)}, bf16[512,1024]{1,0:T(8,128)(2,1)S(1)}, u32[]{:S(2)}, u32[]{:S(2)}) collective-permute-start(bf16[512,1024]{1,0:T(8,128)(2,1)} %get-tuple-element.355), channel_id=1, source_target_pairs={{0,8},{2,10},{4,12},{6,14},{8,0},{10,2},{12,4},{14,6},{16,24},{18,... | collective-permute-start | bytes 3145736 | tf_op jit(solution)/shard_map/ppermute | solution.py:1259
  264.7 17.3 %collective-permute-start.30 = (bf16[2,512,512]{2,1,0:T(8,128)(2,1)}, bf16[2,512,512]{2,1,0:T(8,128)(2,1)}, u32[]{:S(2)}, u32[]{:S(2)}) collective-permute-start(bf16[2,512,512]{2,1,0:T(8,128)(2,1)} %get-tuple-element.358), channel_id=1, source_target_pairs={{0,1},{1,0},{2,3},{3,2},{4,5},{5,4},{6,7},{7,6},{8,9},{9,8},{10,11... | collective-permute-start | bytes 3145736 | tf_op jit(solution)/shard_map/ppermute | solution.py:1255
  282.0 38.7 %collective-permute-start.31 = (bf16[256,1536]{1,0:T(8,128)(2,1)S(1)}, bf16[256,1536]{1,0:T(8,128)(2,1)}, u32[]{:S(2)}, u32[]{:S(2)}) collective-permute-start(bf16[256,1536]{1,0:T(8,128)(2,1)S(1)} %get-tuple-element.382), channel_id=1, source_target_pairs={{0,4},{2,6},{4,0},{6,2},{8,12},{10,14},{12,8},{14,10},{16,20},{18,... | collective-permute-start | bytes 2359304 | tf_op jit(solution)/shard_map/ppermute | solution.py:1259
  282.6 38.1 %collective-permute-start.32 = (bf16[256,1536]{1,0:T(8,128)(2,1)}, bf16[256,1536]{1,0:T(8,128)(2,1)}, u32[]{:S(2)}, u32[]{:S(2)}) collective-permute-start(bf16[256,1536]{1,0:T(8,128)(2,1)} %get-tuple-element.384), channel_id=1, source_target_pairs={{0,8},{2,10},{4,12},{6,14},{8,0},{10,2},{12,4},{14,6},{16,24},{18,... | collective-permute-start | bytes 2359304 | tf_op jit(solution)/shard_map/ppermute | solution.py:1259
  283.1 37.7 %collective-permute-start.33 = (bf16[256,1024]{1,0:T(8,128)(2,1)}, bf16[256,1024]{1,0:T(8,128)(2,1)}, u32[]{:S(2)}, u32[]{:S(2)}) collective-permute-start(bf16[256,1024]{1,0:T(8,128)(2,1)} %get-tuple-element.386), channel_id=1, source_target_pairs={{0,2},{2,0},{4,6},{6,4},{8,10},{10,8},{12,14},{14,12},{16,18},{18,... | collective-permute-start | bytes 1572872 | tf_op jit(solution)/shard_map/ppermute | solution.py:1259
  283.6 58.4 %collective-permute-start.38 = (bf16[512,1024]{1,0:T(8,128)(2,1)}, bf16[512,1024]{1,0:T(8,128)(2,1)S(1)}, u32[]{:S(2)}, u32[]{:S(2)}) collective-permute-start(bf16[512,1024]{1,0:T(8,128)(2,1)} %get-tuple-element.410), channel_id=1, source_target_pairs={{0,2},{2,0},{4,6},{6,4},{8,10},{10,8},{12,14},{14,12},{16,18},{18,... | collective-permute-start | bytes 3145736 | tf_op jit(solution)/shard_map/ppermute | solution.py:1259
  285.1 57.0 %collective-permute-start.39 = (bf16[512,1024]{1,0:T(8,128)(2,1)}, bf16[512,1024]{1,0:T(8,128)(2,1)S(1)}, u32[]{:S(2)}, u32[]{:S(2)}) collective-permute-start(bf16[512,1024]{1,0:T(8,128)(2,1)} %get-tuple-element.412), channel_id=1, source_target_pairs={{0,4},{2,6},{4,0},{6,2},{8,12},{10,14},{12,8},{14,10},{16,20},{18,... | collective-permute-start | bytes 3145736 | tf_op jit(solution)/shard_map/ppermute | solution.py:1259
  325.1 17.6 %collective-permute-start.35 = (bf16[128,1536]{1,0:T(8,128)(2,1)S(1)}, bf16[128,1536]{1,0:T(8,128)(2,1)S(1)}, u32[]{:S(2)}, u32[]{:S(2)}) collective-permute-start(bf16[128,1536]{1,0:T(8,128)(2,1)S(1)} %get-tuple-element.404), channel_id=1, source_target_pairs={{0,8},{2,10},{4,12},{6,14},{8,0},{10,2},{12,4},{14,6},{16,24},{18,... | collective-permute-start | bytes 1179656 | tf_op jit(solution)/shard_map/ppermute | solution.py:1259
  326.7 16.0 %collective-permute-start.36 = (bf16[128,1536]{1,0:T(8,128)(2,1)}, bf16[128,1536]{1,0:T(8,128)(2,1)S(1)}, u32[]{:S(2)}, u32[]{:S(2)}) collective-permute-start(bf16[128,1536]{1,0:T(8,128)(2,1)} %get-tuple-element.406), channel_id=1, source_target_pairs={{0,2},{2,0},{4,6},{6,4},{8,10},{10,8},{12,14},{14,12},{16,18},{18,... | collective-permute-start | bytes 1179656 | tf_op jit(solution)/shard_map/ppermute | solution.py:1259
  347.2 26.0 %collective-permute-start.43 = (bf16[64,4096]{1,0:T(8,128)(2,1)S(1)}, bf16[64,4096]{1,0:T(8,128)(2,1)S(1)}, u32[]{:S(2)}, u32[]{:S(2)}) collective-permute-start(bf16[64,4096]{1,0:T(8,128)(2,1)S(1)} %pad_maximum_fusion), channel_id=1, source_target_pairs={{0,16},{2,18},{4,20},{6,22},{8,24},{10,26},{12,28},{14,30},{16,0},... | collective-permute-start | bytes 1572872 | tf_op jit(solution)/shard_map/ppermute | solution.py:1259
  349.8 23.4 %collective-permute-start.44 = (bf16[256,1024]{1,0:T(8,128)(2,1)S(1)}, bf16[256,1024]{1,0:T(8,128)(2,1)S(1)}, u32[]{:S(2)}, u32[]{:S(2)}) collective-permute-start(bf16[256,1024]{1,0:T(8,128)(2,1)S(1)} %get-tuple-element.441), channel_id=1, source_target_pairs={{0,4},{2,6},{4,0},{6,2},{8,12},{10,14},{12,8},{14,10},{16,20},{18,... | collective-permute-start | bytes 1572872 | tf_op jit(solution)/shard_map/ppermute | solution.py:1259
  351.3 21.9 %collective-permute-start.45 = (bf16[256,1024]{1,0:T(8,128)(2,1)S(1)}, bf16[256,1024]{1,0:T(8,128)(2,1)S(1)}, u32[]{:S(2)}, u32[]{:S(2)}) collective-permute-start(bf16[256,1024]{1,0:T(8,128)(2,1)S(1)} %get-tuple-element.443), channel_id=1, source_target_pairs={{0,2},{2,0},{4,6},{6,4},{8,10},{10,8},{12,14},{14,12},{16,18},{18,... | collective-permute-start | bytes 1572872 | tf_op jit(solution)/shard_map/ppermute | solution.py:1259
  374.2 34.2 %collective-permute-start.49 = (bf16[128,2048]{1,0:T(8,128)(2,1)}, bf16[128,2048]{1,0:T(8,128)(2,1)S(1)}, u32[]{:S(2)}, u32[]{:S(2)}) collective-permute-start(bf16[128,2048]{1,0:T(8,128)(2,1)} %pad_maximum_fusion.2), channel_id=1, source_target_pairs={{0,8},{2,10},{4,12},{6,14},{8,0},{10,2},{12,4},{14,6},{16,24},{18,... | collective-permute-start | bytes 1572872 | tf_op jit(solution)/shard_map/ppermute | solution.py:1259
  374.5 36.2 %collective-permute-start.46 = (bf16[512,1280]{1,0:T(8,128)(2,1)}, bf16[512,1280]{1,0:T(8,128)(2,1)S(1)}, u32[]{:S(2)}, u32[]{:S(2)}) collective-permute-start(bf16[512,1280]{1,0:T(8,128)(2,1)} %get-tuple-element.457), channel_id=1, source_target_pairs={{0,2},{2,0},{4,6},{6,4},{8,10},{10,8},{12,14},{14,12},{16,18},{18,... | collective-permute-start | bytes 3932168 | tf_op jit(solution)/shard_map/ppermute | solution.py:1259
  375.7 35.1 %collective-permute-start.47 = (bf16[512,1280]{1,0:T(8,128)(2,1)}, bf16[512,1280]{1,0:T(8,128)(2,1)S(1)}, u32[]{:S(2)}, u32[]{:S(2)}) collective-permute-start(bf16[512,1280]{1,0:T(8,128)(2,1)} %get-tuple-element.459), channel_id=1, source_target_pairs={{0,4},{2,6},{4,0},{6,2},{8,12},{10,14},{12,8},{14,10},{16,20},{18,... | collective-permute-start | bytes 3932168 | tf_op jit(solution)/shard_map/ppermute | solution.py:1259
  377.2 33.5 %collective-permute-start.48 = (bf16[512,1024]{1,0:T(8,128)(2,1)}, bf16[512,1024]{1,0:T(8,128)(2,1)S(1)}, u32[]{:S(2)}, u32[]{:S(2)}) collective-permute-start(bf16[512,1024]{1,0:T(8,128)(2,1)} %get-tuple-element.461), channel_id=1, source_target_pairs={{0,8},{2,10},{4,12},{6,14},{8,0},{10,2},{12,4},{14,6},{16,24},{18,... | collective-permute-start | bytes 3145736 | tf_op jit(solution)/shard_map/ppermute | solution.py:1259
  391.5 22.4 %collective-permute-start.50 = (bf16[512,2048]{1,0:T(8,128)(2,1)}, bf16[512,2048]{1,0:T(8,128)(2,1)}, u32[]{:S(2)}, u32[]{:S(2)}) collective-permute-start(bf16[512,2048]{1,0:T(8,128)(2,1)} %get-tuple-element.449.k1), channel_id=1, source_target_pairs={{0,1},{1,0},{2,3},{3,2},{4,5},{5,4},{6,7},{7,6},{8,9},{9,8},{10,11... | collective-permute-start | bytes 6291464 | tf_op jit(solution)/shard_map/ppermute | solution.py:1255
  413.9 16.4 %collective-permute-start.51 = (bf16[64,2048]{1,0:T(8,128)(2,1)}, bf16[64,2048]{1,0:T(8,128)(2,1)S(1)}, u32[]{:S(2)}, u32[]{:S(2)}) collective-permute-start(bf16[64,2048]{1,0:T(8,128)(2,1)} %get-tuple-element.485), channel_id=1, source_target_pairs={{0,16},{2,18},{4,20},{6,22},{8,24},{10,26},{12,28},{14,30},{16,0},... | collective-permute-start | bytes 786440 | tf_op jit(solution)/shard_map/ppermute | solution.py:1259
  414.6 21.4 %collective-permute-start.57 = (bf16[256,1024]{1,0:T(8,128)(2,1)}, bf16[256,1024]{1,0:T(8,128)(2,1)}, u32[]{:S(2)}, u32[]{:S(2)}) collective-permute-start(bf16[256,1024]{1,0:T(8,128)(2,1)} %get-tuple-element.501), channel_id=1, source_target_pairs={{0,2},{2,0},{4,6},{6,4},{8,10},{10,8},{12,14},{14,12},{16,18},{18,... | collective-permute-start | bytes 1572872 | tf_op jit(solution)/shard_map/ppermute | solution.py:1259
  416.1 23.1 %collective-permute-start.55 = (bf16[256,1280]{1,0:T(8,128)(2,1)S(1)}, bf16[256,1280]{1,0:T(8,128)(2,1)S(1)}, u32[]{:S(2)}, u32[]{:S(2)}) collective-permute-start(bf16[256,1280]{1,0:T(8,128)(2,1)S(1)} %get-tuple-element.499), channel_id=1, source_target_pairs={{0,8},{2,10},{4,12},{6,14},{8,0},{10,2},{12,4},{14,6},{16,24},{18,... | collective-permute-start | bytes 1966088 | tf_op jit(solution)/shard_map/ppermute | solution.py:1259
  417.9 22.3 %collective-permute-start.53 = (bf16[256,1280]{1,0:T(8,128)(2,1)S(1)}, bf16[256,1280]{1,0:T(8,128)(2,1)S(1)}, u32[]{:S(2)}, u32[]{:S(2)}) collective-permute-start(bf16[256,1280]{1,0:T(8,128)(2,1)S(1)} %get-tuple-element.497), channel_id=1, source_target_pairs={{0,4},{2,6},{4,0},{6,2},{8,12},{10,14},{12,8},{14,10},{16,20},{18,... | collective-permute-start | bytes 1966088 | tf_op jit(solution)/shard_map/ppermute | solution.py:1259
  430.4 21.7 %collective-permute-start.61 = (bf16[512,512]{1,0:T(8,128)(2,1)}, bf16[512,512]{1,0:T(8,128)(2,1)S(1)}, u32[]{:S(2)}, u32[]{:S(2)}) collective-permute-start(bf16[512,512]{1,0:T(8,128)(2,1)} %get-tuple-element.507), channel_id=1, source_target_pairs={{0,8},{2,10},{4,12},{6,14},{8,0},{10,2},{12,4},{14,6},{16,24},{18,... | collective-permute-start | bytes 1572872 | tf_op jit(solution)/shard_map/ppermute | solution.py:1259
  434.6 20.6 %collective-permute-start.60 = (bf16[512,768]{1,0:T(8,128)(2,1)}, bf16[512,768]{1,0:T(8,128)(2,1)S(1)}, u32[]{:S(2)}, u32[]{:S(2)}) collective-permute-start(bf16[512,768]{1,0:T(8,128)(2,1)} %get-tuple-element.505), channel_id=1, source_target_pairs={{0,4},{2,6},{4,0},{6,2},{8,12},{10,14},{12,8},{14,10},{16,20},{18,... | collective-permute-start | bytes 2359304 | tf_op jit(solution)/shard_map/ppermute | solution.py:1259
  436.0 21.0 %collective-permute-start.59 = (bf16[512,768]{1,0:T(8,128)(2,1)S(1)}, bf16[512,768]{1,0:T(8,128)(2,1)S(1)}, u32[]{:S(2)}, u32[]{:S(2)}) collective-permute-start(bf16[512,768]{1,0:T(8,128)(2,1)S(1)} %copy-done.35), channel_id=1, source_target_pairs={{0,2},{2,0},{4,6},{6,4},{8,10},{10,8},{12,14},{14,12},{16,18},{18,... | collective-permute-start | bytes 2359304 | tf_op jit(solution)/shard_map/ppermute | solution.py:1259
  439.2 28.2 %collective-permute-start.62 = (f32[48,1024]{1,0:T(8,128)S(1)}, f32[48,1024]{1,0:T(8,128)S(1)}, u32[]{:S(2)}, u32[]{:S(2)}) collective-permute-start(f32[48,1024]{1,0:T(8,128)S(1)} %add.257), channel_id=1, source_target_pairs={{0,16},{2,18},{4,20},{6,22},{8,24},{10,26},{12,28},{14,30},{16,0},... | collective-permute-start | bytes 589832 | tf_op jit(solution)/shard_map/ppermute | solution.py:1259
  440.2 20.0 %collective-permute-start.58 = (bf16[128,1024]{1,0:T(8,128)(2,1)S(1)}, bf16[128,1024]{1,0:T(8,128)(2,1)S(1)}, u32[]{:S(2)}, u32[]{:S(2)}) collective-permute-start(bf16[128,1024]{1,0:T(8,128)(2,1)S(1)} %get-tuple-element.617), channel_id=1, source_target_pairs={{0,4},{2,6},{4,0},{6,2},{8,12},{10,14},{12,8},{14,10},{16,20},{18,... | collective-permute-start | bytes 786440 | tf_op jit(solution)/shard_map/ppermute | solution.py:1259
  466.6 21.6 %collective-permute-start.63 = (bf16[64,3584]{1,0:T(8,128)(2,1)S(1)}, bf16[64,3584]{1,0:T(8,128)(2,1)S(1)}, u32[]{:S(2)}, u32[]{:S(2)}) collective-permute-start(bf16[64,3584]{1,0:T(8,128)(2,1)S(1)} %pad_maximum_fusion.4), channel_id=1, source_target_pairs={{0,16},{2,18},{4,20},{6,22},{8,24},{10,26},{12,28},{14,30},{16,0},... | collective-permute-start | bytes 1376264 | tf_op jit(solution)/shard_map/ppermute | solution.py:1259
  467.5 22.8 %collective-permute-start.67 = (f32[48,1024]{1,0:T(8,128)S(1)}, f32[48,1024]{1,0:T(8,128)S(1)}, u32[]{:S(2)}, u32[]{:S(2)}) collective-permute-start(f32[48,1024]{1,0:T(8,128)S(1)} %add.270), channel_id=1, source_target_pairs={{0,2},{2,0},{4,6},{6,4},{8,10},{10,8},{12,14},{14,12},{16,18},{18,... | collective-permute-start | bytes 589832 | tf_op jit(solution)/shard_map/ppermute | solution.py:1259
  (65 other events, 664.3 us)
